TPU v7x, 512 devices: a whole 4x8x8 slice. The times are simulated.
512 devices in a mesh: slab: 64 (over x, y, z_lo), grp: 8 (over z_hi, core).
Axes of the slice: x: 4, y: 8, z: 8 (z_hi: 4, z_lo: 2; z = z_hi * 2 + z_lo), core: 2. Of those that a mesh axis runs over, the one named last changes fastest.
Arguments:
- echo_data: bfloat16 [64, 1024, 2048], P('slab', 'grp'), may hold values from -6 to 6
- acquirer: int32 [3], replicated, may hold values from 0 to 63, as said below
- panels: bfloat16 [64, 3, 64, 128, 128], P('slab', None, 'grp'), may hold values from -0.00390625 to 0.00390625
- block_count: int32 [64, 3], P('slab'), may hold values from 16 to 64, as said below
- block_rows: int32 [64, 3, 64], P('slab'), may hold values from 0 to 7
- block_columns: int32 [64, 3, 64], P('slab'), may hold values from 0 to 15
- apodization: float32 [16, 1024], P(None, 'grp'), may hold values from 0.25 to 2.5
- window_index: int32 [65536], P('slab'), may hold values from 0 to 15
Outputs:
- image: float32 [65536], P(('slab', 'grp'))
Inputs may be any that keep to these rules, and one draw needn't show every extreme that they name: `acquirer`: 3 distinct slab indices, the last slab index always among them. `block_count`: slots below the count are live, the others unused; some slab and transmit has all 64 live in every draw.
All inputs are finite; a program needn't handle non-finite values.
Results may differ from a plain program's by a relative error of at most 0.0003.
Values may be sent and summed in bfloat16 or wider, within the bound.
No kernel may reach another device: no remote copies, remote signals or barrier semaphores. Data moves between devices by JAX's collectives and lax.ppermute only.
A program may use at most 128 MiB of HBM per device.

v0:
```python
import math

import jax
import jax.numpy as jnp
from jax import lax
from jax.sharding import PartitionSpec as P


def from_root(block, axis, holder):
    block = jnp.where(lax.axis_index(axis) == holder, block, jnp.zeros_like(block))
    return lax.psum(block, axis)


def table_rows(window_index, table):
    windows = table.shape[0]
    onehot = (window_index[:, None] == jnp.arange(windows, dtype=jnp.int32)[None, :]).astype(
        jnp.float32
    )
    return jnp.dot(
        onehot, table, precision=lax.Precision.HIGHEST, preferred_element_type=jnp.float32
    )


def block_terms(piece, columns, signal):
    block_size = piece.shape[-1]
    channels = signal.shape[0]
    grid = signal.reshape(channels, signal.shape[1] // block_size, block_size)
    picked = jnp.take(grid, columns, axis=1)
    return jnp.einsum("kvs,cks->kvc", piece, picked, preferred_element_type=jnp.float32)


def place_rows(terms, rows, live, row_blocks):
    onehot = (rows[:, None] == jnp.arange(row_blocks, dtype=jnp.int32)[None, :]).astype(
        jnp.float32
    ) * live[:, None]
    return jnp.einsum("kr,kvc->rvc", onehot, terms, precision=lax.Precision.HIGHEST)


def masked_slots(running, piece, rows, columns, live, signal):
    width = piece.shape[0]
    block_size = piece.shape[-1]
    channels = signal.shape[0]
    limit = max(1, (1 << 18) // (block_size * channels))
    group = math.gcd(width, limit)
    turns = width // group
    grouped = (
        piece.reshape(turns, group, block_size, block_size),
        rows.reshape(turns, group),
        columns.reshape(turns, group),
        live.reshape(turns, group),
    )

    def one_group(current, inputs):
        group_piece, group_rows, group_columns, group_live = inputs
        terms = block_terms(group_piece, group_columns, signal)
        return (current + place_rows(terms, group_rows, group_live, current.shape[0]), None)

    result, unused = lax.scan(one_group, running, grouped)
    return result


def add_slots(running, piece, rows_all, columns_all, count, signal):
    width = piece.shape[0]
    live = (jnp.arange(width, dtype=jnp.int32) < count).astype(jnp.float32)
    return masked_slots(running, piece, rows_all, columns_all, live, signal)


def per_device(
    echo_data, acquirer, panels, block_count, block_rows, block_columns, apodization, window_index
):
    signal_own = echo_data[0]
    block_size = panels.shape[-1]
    voxel_count = window_index.shape[0]
    row_blocks = voxel_count // block_size
    weights = table_rows(window_index, apodization)
    running = jnp.zeros((row_blocks, block_size, signal_own.shape[0]), jnp.float32)
    for transmit in range(acquirer.shape[0]):
        signal = from_root(signal_own, "slab", acquirer[transmit])
        rows_all = block_rows[0, transmit]
        columns_all = block_columns[0, transmit]
        count = block_count[0, transmit]

        def fold_panels(
            current,
            piece,
            start,
            signal=signal,
            rows_all=rows_all,
            columns_all=columns_all,
            count=count,
        ):
            return add_slots(current, piece, rows_all, columns_all, count, signal)

        running = fold_panels(
            running, lax.all_gather(panels[0, transmit], "grp", axis=0, tiled=True), jnp.int32(0)
        )
    partial_value = jnp.sum(running.reshape(voxel_count, running.shape[2]) * weights, axis=1)
    return lax.psum_scatter(partial_value, "grp", scatter_dimension=0, tiled=True)


def solution(mesh):
    return jax.shard_map(
        per_device,
        mesh=mesh,
        in_specs=(
            P("slab", "grp", None),
            P(),
            P("slab", None, "grp", None, None),
            P("slab", None),
            P("slab", None, None),
            P("slab", None, None),
            P(None, "grp"),
            P("slab"),
        ),
        out_specs=P(("slab", "grp")),
        check_vma=False,
    )
```

profile of v0, /device:TPU:1, one launch (start us, length us, event | category | flops | bytes accessed | tf_op | source)
XLA Modules:
  0.0 722.1 jit_solution(10459350146008842801)
XLA Ops:
  7.4 1.4 fusion.66
  10.6 1.3 copy.28
  12.0 1.2 select_bitcast_fusion
  13.5 0.9 slice_bitcast_fusion
  18.6 1.3 dynamic-slice
  20.4 580.0 %all-reduce.4.cloned.1.call-done = (bf16[128,2048]{0,1:T(8,128)(2,1)}, bf16[128,2048]{0,1:T(8,128)(2,1)}, bf16[128,2048]{0,1:T(8,128)(2,1)}) async-done(((bf16[128,2048]{0,1:T(8,128)(2,1)}, bf16[128,2048]{0,1:T(8,128)(2,1)}, bf16[128,2048]{0,1:T(8,128)(2,1)}), (bf16[128,2048]{0,1:T(8,128)(2,1)}, bf16[128,2048]{0,1:T(8,128)(2,1)}, bf16[128,2048]{0,1:T(8,128)(2,1)})) %all-reduce.4.cloned.1.call-update) | async-done | bytes 1572880 | tf_op jit(solution)/shard_map/psum | solution.py:11
  600.5 20.0 %while.33 = (s32[]{:T(128)}, f32[8,128,128]{2,0,1:T(8,128)S(1)}, s32[4,16]{1,0:T(4,128)S(1)}, f32[4,16]{1,0:T(4,128)S(1)}, bf16[4,16,128,128]{3,2,1,0:T(8,128)(2...) while((s32[]{:T(128)}, f32[8,128,128]{2,0,1:T(8,128)S(1)}, ...), condition=%wide.region_2.4_spmd.clone, body=%wide.region_1.3_spmd.clone.sunk | while | flops 92800352 | bytes 6296851 | solution.py:58
  600.5 1.4 copy.56
  601.9 0.7 gather_fusion.2
  602.5 1.6 fusion.107
  604.2 1.3 convolution_add_fusion.8
  605.5 1.3 copy.56
  606.8 0.7 gather_fusion.2
  607.5 1.6 fusion.107
  609.2 1.3 convolution_add_fusion.8
  610.5 1.3 copy.56
  612.5 1.6 fusion.107
  614.1 1.3 convolution_add_fusion.8
  615.5 1.3 copy.56
  617.5 1.6 fusion.107
  619.1 1.3 convolution_add_fusion.8
  620.5 15.9 %while.31 = (s32[]{:T(128)}, f32[8,128,128]{2,0,1:T(8,128)S(1)}, s32[4,16]{1,0:T(4,128)S(1)}, f32[4,16]{1,0:T(4,128)S(1)}, bf16[4,16,128,128]{3,2,1,0:T(8,128)(2...) while((s32[]{:T(128)}, f32[8,128,128]{2,0,1:T(8,128)S(1)}, s32[4,16]{1,0:T(4,128)S(1)}, ...), condition=%wide.region_5.7_spmd, body=%wide.region_4.6_spmd.sunk | while | flops 92669280 | bytes 6296833 | solution.py:58
  620.9 0.7 gather_fusion
  621.5 1.6 fusion.93
  623.2 1.3 convolution_add_fusion.6
  624.9 0.7 gather_fusion
  625.5 1.6 fusion.93
  627.2 1.3 convolution_add_fusion.6
  628.8 0.7 gather_fusion
  629.5 1.6 fusion.93
  631.1 1.3 convolution_add_fusion.6
  632.8 0.7 gather_fusion
  633.5 1.6 fusion.93
  635.1 1.3 convolution_add_fusion.6
  636.5 15.9 %while.32 = (s32[]{:T(128)}, f32[8,128,128]{2,0,1:T(8,128)S(1)}, s32[4,16]{1,0:T(4,128)S(1)}, f32[4,16]{1,0:T(4,128)S(1)}, bf16[4,16,128,128]{3,2,1,0:T(8,128)(2...) while((s32[]{:T(128)}, f32[8,128,128]{2,0,1:T(8,128)S(1)}, ...), condition=%wide.region_8.10_spmd, body=%wide.region_7.9_spmd.sunk | while | flops 92669280 | bytes 6296833 | solution.py:58
  636.9 0.7 gather_fusion.1
  637.5 1.6 fusion.100
  639.2 1.3 convolution_add_fusion.7
  640.9 0.7 gather_fusion.1
  641.5 1.6 fusion.100
  643.2 1.3 convolution_add_fusion.7
  644.9 0.7 gather_fusion.1
  645.5 1.6 fusion.100
  647.2 1.3 convolution_add_fusion.7
  648.8 0.7 gather_fusion.1
  649.5 1.6 fusion.100
  651.1 1.3 convolution_add_fusion.7
  653.4 60.5 %all-reduce = f32[1024]{0:T(1024)S(1)} all-reduce(f32[1024]{0:T(1024)S(1)} %fusion.57), channel_id=5, replica_groups=mesh['slab'=64,'grp'=8] {'grp'}, use_global_device_ids=true, to_apply=%region_10.12.clone | all-reduce | flops 1024 | bytes 8192
  (100 shorter events, 10.0 us)
Async XLA Ops:
  7.4 645.4 %copy-start = (f32[16,128]{1,0:T(8,128)S(1)}, f32[16,128]{1,0:T(8,128)}, u32[]{:S(2)}) copy-start(f32[16,128]{1,0:T(8,128)} %param.22) | copy-start | bytes 24580
  7.4 593.1 %all-reduce.4.cloned.1.call-start = ((), (), s32[]{:S(2)}) async-start(), calls=%async_computation.3 | async-start | bytes 3145728 | tf_op jit(solution)/shard_map/psum | solution.py:11
  12.0 1.6 copy-start.3
  13.2 2.4 copy-start.6
  13.2 2.4 copy-start.7
  13.2 2.6 copy-start.4
  13.2 587.2 %all-gather.7.cloned.1.call-start = ((), (), s32[]{:S(2)}) async-start(), calls=%async_computation | async-start | bytes 2359296 | tf_op jit(solution)/shard_map/all_gather | solution.py:95
  14.4 606.1 %all-gather.9.cloned.1.call-start = ((), (), s32[]{:S(2)}) async-start(), calls=%async_computation.1 | async-start | bytes 2359296 | tf_op jit(solution)/shard_map/all_gather | solution.py:95
  15.0 621.5 %all-gather.11.cloned.1.call-start = ((), (), s32[]{:S(2)}) async-start(), calls=%async_computation.2 | async-start | bytes 2359296 | tf_op jit(solution)/shard_map/all_gather | solution.py:95
  600.5 20.0 %copy-start.2 = (bf16[128,2048]{0,1:T(8,128)(2,1)S(1)}, bf16[128,2048]{0,1:T(8,128)(2,1)}, u32[]{:S(2)}) copy-start(bf16[128,2048]{0,1:T(8,128)(2,1)} %get-tuple-element.389) | copy-start | bytes 1572868
  620.5 16.0 %copy-start.1 = (bf16[128,2048]{0,1:T(8,128)(2,1)S(1)}, bf16[128,2048]{0,1:T(8,128)(2,1)}, u32[]{:S(2)}) copy-start(bf16[128,2048]{0,1:T(8,128)(2,1)} %get-tuple-element.413) | copy-start | bytes 1572868
  636.5 16.3 %copy-start.5 = (s32[1024]{0:T(1024)S(1)}, s32[1024]{0:T(1024)}, u32[]{:S(2)}) copy-start(s32[1024]{0:T(1024)} %param.23) | copy-start | bytes 12292
Sparse Core Ops, SparseCore 0:
  13.4 587.0 all-reduce.3
Sparse Core Ops, SparseCore 1:
  15.9 46.7 all-gather.6
  64.8 39.5 all-gather.8
  106.6 39.3 all-gather.10
where the time goes:
time: 723 us; the launch traced here: 722 us
  waiting for transfers between devices  581 us (80%)
  blocking collectives  60.5 us (8%)
  matrix products  35.8 us (5%)
  local copies, waits for them, and re-layouts  22.7 us (3%)
  between operations  17.7 us (2%)
    psum x1, waiting for transfers between devices, from_root(): return lax.psum(block, axis)  580 us
    unnamed x1, blocking collectives  60.5 us
    dot_general x12, matrix products, block_terms(): jnp.einsum('kvs,cks->kvc', piece, picked, preferred_element_type=jnp.floa...  19.3 us
    dot_general x12, matrix products, place_rows(): jnp.einsum('kr,kvc->rvc', onehot, terms, precision=lax.Precision.HIGHEST)  15.9 us
  transfers between devices with their start and end apart: 4, of which 1 were waited for; matrix products, arithmetic and copies ran while one was open for 6% of the time, Pallas kernels for 0%

commit v1 on v0

v1 whole, which is shorter than its diff:
```python
import jax
import jax.numpy as jnp
from jax import lax
from jax.experimental import pallas as pl
from jax.experimental.pallas import tpu as pltpu
from jax.sharding import PartitionSpec as P

LANES = 128
VMEM = pl.BlockSpec(memory_space=pltpu.VMEM)
SMEM = pl.BlockSpec(memory_space=pltpu.SMEM)
NT = (((1,), (1,)), ((), ()))
PARAMS = pltpu.CompilerParams(vmem_limit_bytes=8 * 1024 * 1024)


def window_sums(apodization, echo):
    windows, channels = apodization.shape
    samples = echo.shape[-1]
    blocks, quarters = samples // LANES, windows // 4

    def kernel(apod_ref, echo_ref, out_ref):
        apod = apod_ref[...]
        high = apod.astype(jnp.bfloat16)
        rest = apod - high.astype(jnp.float32)
        middle = rest.astype(jnp.bfloat16)
        low = (rest - middle.astype(jnp.float32)).astype(jnp.bfloat16)
        terms = jnp.concatenate([high, middle, low], axis=0)
        sums = jnp.dot(terms, echo_ref[0], preferred_element_type=jnp.float32)
        sums = sums[:windows] + (sums[windows : 2 * windows] + sums[2 * windows :])
        for block in range(blocks):
            for quarter in range(quarters):
                out_ref[block * quarters + quarter] = sums[
                    4 * quarter : 4 * quarter + 4, block * LANES : (block + 1) * LANES
                ]

    return pl.pallas_call(
        kernel,
        out_shape=jax.ShapeDtypeStruct((blocks * quarters, 4, LANES), jnp.float32),
        in_specs=[VMEM, VMEM],
        out_specs=VMEM,
        compiler_params=PARAMS,
    )(apodization, echo)


def pick_acquirers(acquirer, pieces, copies):
    transmits = acquirer.shape[0]

    def kernel(acquirer_ref, pieces_ref, out_ref):
        for transmit in range(transmits):
            picked = pieces_ref[acquirer_ref[transmit]]
            for copy in range(copies):
                out_ref[copy, transmit] = picked

    return pl.pallas_call(
        kernel,
        out_shape=jax.ShapeDtypeStruct((copies, transmits) + pieces.shape[1:], pieces.dtype),
        in_specs=[SMEM, VMEM],
        out_specs=VMEM,
        compiler_params=PARAMS,
    )(acquirer, pieces)


def sum_and_copy(parts, copies):
    def kernel(parts_ref, out_ref):
        total = jnp.sum(parts_ref[...], axis=0)
        for copy in range(copies):
            out_ref[copy] = total

    return pl.pallas_call(
        kernel,
        out_shape=jax.ShapeDtypeStruct((copies,) + parts.shape[1:], parts.dtype),
        in_specs=[VMEM],
        out_specs=VMEM,
        compiler_params=PARAMS,
    )(parts)


def slot_sums(counts, rows, columns, windows_of_voxels, table, panels):
    transmits, slots, block, _ = panels.shape[1:]
    quarters = 4
    row_blocks = windows_of_voxels.shape[0] // block
    windows = quarters * table.shape[2]
    windows_of_voxels = windows_of_voxels.reshape(row_blocks, 1, block)

    def kernel(counts_ref, rows_ref, columns_ref, index_ref, table_ref, panels_ref, out_ref, total):
        first = lax.axis_index("grp") * slots
        total[...] = jnp.zeros_like(total)
        for transmit in range(transmits):
            for slot in range(slots):
                k = first + slot
                column = columns_ref[0, transmit, k]
                row = jnp.where(k < counts_ref[0, transmit], rows_ref[0, transmit, k], row_blocks)
                weighted = jnp.concatenate(
                    [table_ref[column * quarters + quarter, transmit] for quarter in range(quarters)],
                    axis=0,
                )
                high = weighted.astype(jnp.bfloat16)
                low = (weighted - high.astype(jnp.float32)).astype(jnp.bfloat16)
                terms = lax.dot_general(
                    jnp.concatenate([high, low], axis=0),
                    panels_ref[0, transmit, slot],
                    NT,
                    preferred_element_type=jnp.float32,
                )
                total[row] += terms[:windows] + terms[windows:]
        number = lax.broadcasted_iota(jnp.int32, (windows, block), 0)
        for row in range(row_blocks):
            chosen = jnp.where(number == index_ref[row], total[row], 0.0)
            out_ref[row] = jnp.sum(chosen, axis=0, keepdims=True)

    return pl.pallas_call(
        kernel,
        out_shape=jax.ShapeDtypeStruct((row_blocks, 1, block), jnp.float32),
        in_specs=[SMEM, SMEM, SMEM, VMEM, VMEM, VMEM],
        out_specs=VMEM,
        compiler_params=PARAMS,
        scratch_shapes=[pltpu.VMEM((row_blocks + 1, windows, block), jnp.float32)],
    )(counts, rows, columns, windows_of_voxels, table, panels)


def exchange(pieces, axis):
    return lax.all_to_all(pieces, axis, split_axis=0, concat_axis=0, tiled=True)


def per_device(
    echo_data, acquirer, panels, block_count, block_rows, block_columns, apodization, window_index
):
    slabs, groups = lax.axis_size("slab"), lax.axis_size("grp")
    pieces = exchange(window_sums(apodization, echo_data), "slab")
    parts = exchange(pick_acquirers(acquirer, pieces, groups), "grp")
    table = exchange(sum_and_copy(parts, slabs), "slab")
    partial = slot_sums(block_count, block_rows, block_columns, window_index, table, panels)
    return jnp.sum(exchange(partial, "grp"), axis=(0, 1))


def solution(mesh):
    return jax.shard_map(
        per_device,
        mesh=mesh,
        in_specs=(
            P("slab", "grp", None),
            P(),
            P("slab", None, "grp", None, None),
            P("slab", None),
            P("slab", None, None),
            P("slab", None, None),
            P(None, "grp"),
            P("slab"),
        ),
        out_specs=P(("slab", "grp")),
        check_vma=False,
    )
```

time: 723 us -> 76.5 us (0.11)
  waiting for transfers between devices: 581 us -> 13.1 us
  matrix products: 35.8 us -> 0 us
  local copies, waits for them, and re-layouts: 22.7 us -> 1.77 us
  between operations: 17.7 us -> 0.1 us
  blocking collectives: 60.5 us -> 53.1 us
    psum x1 -> x0, waiting for transfers between devices: 580 us -> none  [from_root(): return lax.psum(block, axis)]
    unnamed x1 -> x0, blocking collectives: 60.5 us -> none
    all_to_all x0 -> x3, blocking collectives: none -> 53.1 us  [exchange(): return lax.all_to_all(pieces, axis, split_axis=0, concat_axis=0, tiled=True)]
    dot_general x25 -> x0, matrix products: 35.8 us -> none  [the longest x12 19.3 us: block_terms(): jnp.einsum('kvs,cks->kvc', piece, picked, preferred_element_type=jnp.floa...]
    all_to_all x0 -> x1, waiting for transfers between devices: none -> 13.1 us  [exchange(): return lax.all_to_all(pieces, axis, split_axis=0, concat_axis=0, tiled=True)]
    gather x12 -> x0, local copies, waits for them, and re-layouts: 7.81 us -> none  [block_terms(): picked = jnp.take(grid, columns, axis=1)]
    reshape x12 -> x0, local copies, waits for them, and re-layouts: 7.68 us -> none  [block_terms(): grid = signal.reshape(channels, signal.shape[1] // block_size, block_size)]
  transfers between devices with their start and end apart: 4 -> 1, of which waited for: 1 -> 1; matrix products, arithmetic and copies ran while one was open for 6% -> 0% of each run, Pallas kernels for 0% -> 0%
where the time goes in v1:
time: 76.5 us; the launch traced here: 76.1 us
  blocking collectives  53.1 us (69%)
  waiting for transfers between devices  13.1 us (17%)
  starting transfers between devices  4.76 us (6%)
  Pallas kernels  2.7 us (4%)
  local copies, waits for them, and re-layouts  1.77 us (2%)
    all_to_all x3, blocking collectives, exchange(): return lax.all_to_all(pieces, axis, split_axis=0, concat_axis=0, tiled=True)  53.1 us
    all_to_all x1, waiting for transfers between devices, exchange(): return lax.all_to_all(pieces, axis, split_axis=0, concat_axis=0, tiled=True)  13.1 us
    all_to_all x1, starting transfers between devices, exchange(): return lax.all_to_all(pieces, axis, split_axis=0, concat_axis=0, tiled=True)  4.76 us
    unnamed x18, local copies, waits for them, and re-layouts  1.77 us
  transfers between devices with their start and end apart: 1, of which 1 were waited for; matrix products, arithmetic and copies ran while one was open for 0% of the time, Pallas kernels for 0%

profile of v1, /device:TPU:1, one launch (start us, length us, event | category | flops | bytes accessed | tf_op | source)
XLA Modules:
  0.0 76.1 jit_solution(18227214398682058107)
XLA Ops:
  0.0 0.0 copy-start.1
  0.0 1.0 %copy-done.1 = bf16[1,128,2048]{2,1,0:T(8,128)(2,1)S(1)} copy-done((bf16[1,128,2048]{2,1,0:T(8,128)(2,1)S(1)}, bf16[1,128,2048]{2,1,0:T(8,128)(2,1)}, u32[]{:S(2)}) %copy-start.1) | copy-done | bytes 524312
  1.0 0.0 copy-start.2
  1.0 0.7 copy-done.2
  1.7 0.2 shard_map.82
  1.9 0.0 copy-start.4
  2.0 22.4 %all_to_all.20.pieces_ref = f32[64,4,128]{2,1,0:T(4,128)S(1)} all-to-all(f32[64,4,128]{2,1,0:T(4,128)S(1)} %shard_map.82), channel_id=1, replica_groups=mesh['slab'=64,'grp'=8] {'slab'}, dimensions={0} | all-to-all | bytes 262144 | tf_op jit(solution)/shard_map/all_to_all | solution.py:121
  24.3 0.0 copy-done.4
  24.3 0.0 copy-start
  24.3 0.6 shard_map.83
  24.9 18.6 %all_to_all.21.parts_ref = f32[8,3,4,128]{3,2,1,0:T(4,128)S(1)} all-to-all(f32[8,3,4,128]{3,2,1,0:T(4,128)S(1)} %shard_map.83), channel_id=1, replica_groups=mesh['slab'=64,'grp'=8] {'grp'}, dimensions={0} | all-to-all | bytes 98304 | tf_op jit(solution)/shard_map/all_to_all | solution.py:121
  43.5 0.8 %shard_map.84 = f32[64,3,4,128]{3,2,1,0:T(4,128)} custom-call(f32[8,3,4,128]{3,2,1,0:T(4,128)S(1)} %all_to_all.21.parts_ref), custom_call_target="tpu_custom_call" | custom-call | tf_op jit(solution)/shard_map/pallas_call | solution.py:68
  44.3 0.0 copy-start.6
  44.3 0.0 copy-start.7
  44.3 4.8 %all-to-all-start.2 = ((f32[64,3,4,128]{3,2,1,0:T(4,128)}), f32[64,3,4,128]{3,2,1,0:T(4,128)S(1)}, u32[]{:S(2)}, u32[]{:S(2)}) async-start(f32[64,3,4,128]{3,2,1,0:T(4,128)} %shard_map.84), calls=%async_computation.2 | async-start | bytes 786432 | tf_op jit(solution)/shard_map/all_to_all | solution.py:121
  49.1 0.0 copy-done.6
  49.1 0.0 copy-start.3
  49.1 0.0 copy-done.7
  49.2 0.0 copy-start.5
  49.2 13.1 %all-to-all-done.2.table_ref = f32[64,3,4,128]{3,2,1,0:T(4,128)S(1)} async-done(((f32[64,3,4,128]{3,2,1,0:T(4,128)}), f32[64,3,4,128]{3,2,1,0:T(4,128)S(1)}, u32[]{:S(2)}, u32[]{:S(2)}) %all-to-all-start.2) | async-done | bytes 393248 | tf_op jit(solution)/shard_map/all_to_all | solution.py:121
  62.3 0.0 copy-done
  62.3 0.0 copy-done.3
  62.3 0.0 copy-done.5
  62.3 1.1 %shard_map.85 = f32[8,1,128]{2,1,0:T(1,128)S(1)} custom-call(s32[1,3]{1,0:T(1,128)S(1)} %copy-done.5, s32[1,3,64]{2,1,0:T(4,128)S(1)} %copy.9.rows_ref, s32[1,3,64]{2,1,0:T(4,128)S(1)} %copy.10.columns_ref, s32[8,1,128]{2,1,0:T(1,128)S(1)} %bitcast.1, f32[64,3,4,128]{3,2,1,0:T(4,128)S(1)} %all-to-all-done.2.table_ref, bf16[1,3,8,128,128]{4,3,2,1,0:T(8,128)(2,1)S(1)} %copy-done), custom_call_target="tpu_custom_call" | custom-call | tf_op jit(solution)/shard_map/pallas_call | solution.py:110
  63.5 12.1 %all_to_all.22 = f32[8,1,128]{2,1,0:T(1,128)S(1)} all-to-all(f32[8,1,128]{2,1,0:T(1,128)S(1)} %shard_map.85), channel_id=1, replica_groups=mesh['slab'=64,'grp'=8] {'grp'}, dimensions={0} | all-to-all | bytes 8192 | tf_op jit(solution)/shard_map/all_to_all | solution.py:121
  75.6 0.5 reduce_sum.9
  (2 shorter events, 0.0 us)
Async XLA Ops:
  0.0 1.0 %copy-start.1 = (bf16[1,128,2048]{2,1,0:T(8,128)(2,1)S(1)}, bf16[1,128,2048]{2,1,0:T(8,128)(2,1)}, u32[]{:S(2)}) copy-start(bf16[1,128,2048]{2,1,0:T(8,128)(2,1)} %echo_ref.1) | copy-start | bytes 1572868
  1.0 0.7 copy-start.2
  1.9 22.4 %copy-start.4 = (s32[3]{0:T(128)S(1)}, s32[3]{0:T(128)}, u32[]{:S(2)}) copy-start(s32[3]{0:T(128)} %acquirer_ref.1) | copy-start | bytes 40
  24.3 38.0 %copy-start = (bf16[1,3,8,128,128]{4,3,2,1,0:T(8,128)(2,1)S(1)}, bf16[1,3,8,128,128]{4,3,2,1,0:T(8,128)(2,1)}, u32[]{:S(2)}) copy-start(bf16[1,3,8,128,128]{4,3,2,1,0:T(8,128)(2,1)} %panels_ref.1) | copy-start | bytes 2359300
  44.3 4.8 %copy-start.6 = (s32[1,3,64]{2,0,1:T(1,128)S(1)}, s32[1,3,64]{2,0,1:T(1,128)}, u32[]{:S(2)}) copy-start(s32[1,3,64]{2,0,1:T(1,128)} %param.13) | copy-start | bytes 2308
  44.3 4.8 %copy-start.7 = (s32[1,3,64]{2,0,1:T(1,128)S(1)}, s32[1,3,64]{2,0,1:T(1,128)}, u32[]{:S(2)}) copy-start(s32[1,3,64]{2,0,1:T(1,128)} %param.12) | copy-start | bytes 2308
  44.3 18.0 %all-to-all-start.2 = ((f32[64,3,4,128]{3,2,1,0:T(4,128)}), f32[64,3,4,128]{3,2,1,0:T(4,128)S(1)}, u32[]{:S(2)}, u32[]{:S(2)}) async-start(f32[64,3,4,128]{3,2,1,0:T(4,128)} %shard_map.84), calls=%async_computation.2 | async-start | bytes 786432 | tf_op jit(solution)/shard_map/all_to_all | solution.py:121
  49.1 13.2 %copy-start.3 = (s32[1024]{0:T(1024)S(1)}, s32[1024]{0:T(1024)}, u32[]{:S(2)}) copy-start(s32[1024]{0:T(1024)} %param.15) | copy-start | bytes 12292
  49.2 13.2 %copy-start.5 = (s32[1,3]{1,0:T(1,128)S(1)}, s32[1,3]{1,0:T(1,128)}, u32[]{:S(2)}) copy-start(s32[1,3]{1,0:T(1,128)} %counts_ref.1) | copy-start | bytes 40

commit v2 on v1

--- a/solution.py
+++ b/solution.py
@@ -87,8 +87,8 @@
         for transmit in range(transmits):
             for slot in range(slots):
                 k = first + slot
-                column = columns_ref[0, transmit, k]
-                row = jnp.where(k < counts_ref[0, transmit], rows_ref[0, transmit, k], row_blocks)
+                column = columns_ref[transmit, 0, k]
+                row = jnp.where(k < counts_ref[0, transmit], rows_ref[transmit, 0, k], row_blocks)
                 weighted = jnp.concatenate(
                     [table_ref[column * quarters + quarter, transmit] for quarter in range(quarters)],
                     axis=0,
@@ -128,7 +128,8 @@
     pieces = exchange(window_sums(apodization, echo_data), "slab")
     parts = exchange(pick_acquirers(acquirer, pieces, groups), "grp")
     table = exchange(sum_and_copy(parts, slabs), "slab")
-    partial = slot_sums(block_count, block_rows, block_columns, window_index, table, panels)
+    rows, columns = (jnp.transpose(x, (1, 0, 2)) for x in (block_rows, block_columns))
+    partial = slot_sums(block_count, rows, columns, window_index, table, panels)
     return jnp.sum(exchange(partial, "grp"), axis=(0, 1))
 
 

time: 76.5 us -> 75.9 us (level)
  blocking collectives: 53.1 us -> 70.6 us
  waiting for transfers between devices: 13.1 us -> 0 us
  starting transfers between devices: 4.76 us -> 0 us
  Pallas kernels: 2.7 us -> 1.93 us
    all_to_all x3 -> x4, blocking collectives: 53.1 us -> 70.6 us  [exchange(): return lax.all_to_all(pieces, axis, split_axis=0, concat_axis=0, tiled=True)]
    all_to_all x1 -> x0, waiting for transfers between devices: 13.1 us -> none  [exchange(): return lax.all_to_all(pieces, axis, split_axis=0, concat_axis=0, tiled=True)]
    all_to_all x1 -> x0, starting transfers between devices: 4.76 us -> none  [exchange(): return lax.all_to_all(pieces, axis, split_axis=0, concat_axis=0, tiled=True)]
    unnamed x18 -> x16, local copies, waits for them, and re-layouts: 1.77 us -> 2.44 us
  transfers between devices with their start and end apart: 1 -> 0, of which waited for: 1 -> 0; matrix products, arithmetic and copies ran while one was open for 0% -> 0% of each run, Pallas kernels for 0% -> 0%
where the time goes in v2:
time: 75.9 us; the launch traced here: 75.6 us
  blocking collectives  70.6 us (93%)
  local copies, waits for them, and re-layouts  2.44 us (3%)
  Pallas kernels  1.93 us (3%)
    all_to_all x4, blocking collectives, exchange(): return lax.all_to_all(pieces, axis, split_axis=0, concat_axis=0, tiled=True)  70.6 us
    unnamed x16, local copies, waits for them, and re-layouts  2.44 us

profile of v2, /device:TPU:1, one launch (start us, length us, event | category | flops | bytes accessed | tf_op | source)
XLA Modules:
  0.0 75.6 jit_solution(82678341623946242)
XLA Ops:
  0.0 0.0 copy-start.1
  0.0 1.0 %copy-done.1 = bf16[1,128,2048]{2,1,0:T(8,128)(2,1)S(1)} copy-done((bf16[1,128,2048]{2,1,0:T(8,128)(2,1)S(1)}, bf16[1,128,2048]{2,1,0:T(8,128)(2,1)}, u32[]{:S(2)}) %copy-start.1) | copy-done | bytes 524312
  1.0 0.0 copy-start.2
  1.0 0.7 copy-done.2
  1.7 0.2 shard_map.82
  1.9 0.0 copy-start.7
  2.0 22.4 %all_to_all.20.pieces_ref = f32[64,4,128]{2,1,0:T(4,128)S(1)} all-to-all(f32[64,4,128]{2,1,0:T(4,128)S(1)} %shard_map.82), channel_id=1, replica_groups=mesh['slab'=64,'grp'=8] {'slab'}, dimensions={0} | all-to-all | bytes 262144 | tf_op jit(solution)/shard_map/all_to_all | solution.py:121
  24.3 0.0 copy-done.7
  24.3 0.0 copy-start
  24.3 0.6 shard_map.83
  24.9 18.6 %all_to_all.21.parts_ref = f32[8,3,4,128]{3,2,1,0:T(4,128)S(1)} all-to-all(f32[8,3,4,128]{3,2,1,0:T(4,128)S(1)} %shard_map.83), channel_id=1, replica_groups=mesh['slab'=64,'grp'=8] {'grp'}, dimensions={0} | all-to-all | bytes 98304 | tf_op jit(solution)/shard_map/all_to_all | solution.py:121
  43.5 0.1 shard_map.84
  43.6 0.0 copy-start.5
  43.6 0.0 copy-start.6
  43.6 17.5 %all_to_all.22.table_ref = f32[64,3,4,128]{3,2,1,0:T(4,128)S(1)} all-to-all(f32[64,3,4,128]{3,2,1,0:T(4,128)S(1)} %shard_map.84), channel_id=1, replica_groups=mesh['slab'=64,'grp'=8] {'slab'}, dimensions={0} | all-to-all | bytes 786432 | tf_op jit(solution)/shard_map/all_to_all | solution.py:121
  61.1 0.0 copy-start.3
  61.1 0.0 copy-start.4
  61.1 0.0 copy-done
  61.1 0.0 copy-done.5
  61.1 0.0 copy-done.6
  61.1 0.7 copy-done.3
  61.8 0.0 copy-done.4
  61.8 1.1 %shard_map.85 = f32[8,1,128]{2,1,0:T(1,128)S(1)} custom-call(s32[1,3]{1,0:T(1,128)S(1)} %copy-done.6, s32[3,1,64]{2,1,0:T(1,128)S(1)} %bitcast.4, s32[3,1,64]{2,1,0:T(1,128)S(1)} %bitcast.5, s32[8,1,128]{2,1,0:T(1,128)S(1)} %bitcast.3, f32[64,3,4,128]{3,2,1,0:T(4,128)S(1)} %all_to_all.22.table_ref, bf16[1,3,8,128,128]{4,3,2,1,0:T(8,128)(2,1)S(1)} %copy-done), custom_call_target="tpu_custom_call" | custom-call | tf_op jit(solution)/shard_map/pallas_call | solution.py:110
  63.0 12.1 %all_to_all.23 = f32[8,1,128]{2,1,0:T(1,128)S(1)} all-to-all(f32[8,1,128]{2,1,0:T(1,128)S(1)} %shard_map.85), channel_id=1, replica_groups=mesh['slab'=64,'grp'=8] {'grp'}, dimensions={0} | all-to-all | bytes 8192 | tf_op jit(solution)/shard_map/all_to_all | solution.py:121
  75.0 0.5 reduce_sum.9
Async XLA Ops:
  0.0 1.0 %copy-start.1 = (bf16[1,128,2048]{2,1,0:T(8,128)(2,1)S(1)}, bf16[1,128,2048]{2,1,0:T(8,128)(2,1)}, u32[]{:S(2)}) copy-start(bf16[1,128,2048]{2,1,0:T(8,128)(2,1)} %echo_ref.1) | copy-start | bytes 1572868
  1.0 0.7 copy-start.2
  1.9 22.4 %copy-start.7 = (s32[3]{0:T(128)S(1)}, s32[3]{0:T(128)}, u32[]{:S(2)}) copy-start(s32[3]{0:T(128)} %acquirer_ref.1) | copy-start | bytes 40
  24.3 36.8 %copy-start = (bf16[1,3,8,128,128]{4,3,2,1,0:T(8,128)(2,1)S(1)}, bf16[1,3,8,128,128]{4,3,2,1,0:T(8,128)(2,1)}, u32[]{:S(2)}) copy-start(bf16[1,3,8,128,128]{4,3,2,1,0:T(8,128)(2,1)} %panels_ref.1) | copy-start | bytes 2359300
  43.6 17.5 %copy-start.5 = (s32[1,3,64]{2,0,1:T(1,128)S(1)}, s32[1,3,64]{2,0,1:T(1,128)}, u32[]{:S(2)}) copy-start(s32[1,3,64]{2,0,1:T(1,128)} %param.13) | copy-start | bytes 2308
  43.6 17.5 %copy-start.6 = (s32[1,3]{1,0:T(1,128)S(1)}, s32[1,3]{1,0:T(1,128)}, u32[]{:S(2)}) copy-start(s32[1,3]{1,0:T(1,128)} %counts_ref.1) | copy-start | bytes 40
  61.1 0.7 copy-start.3
  61.1 0.7 copy-start.4

commit v3 on v1

v3 whole, which is shorter than its diff:
```python
import jax
import jax.numpy as jnp
from jax import lax
from jax.experimental import pallas as pl
from jax.experimental.pallas import tpu as pltpu
from jax.sharding import PartitionSpec as P

LANES = 128
Y, Z = 8, 2
VMEM = pl.BlockSpec(memory_space=pltpu.VMEM)
SMEM = pl.BlockSpec(memory_space=pltpu.SMEM)
NT = (((1,), (1,)), ((), ()))
PARAMS = pltpu.CompilerParams(vmem_limit_bytes=8 * 1024 * 1024)


def swap_granules(arrays):
    arrays = list(arrays)
    count = len(arrays)
    width = LANES // count
    granule = lax.broadcasted_iota(jnp.int32, arrays[0].shape, 1) // width
    step = count // 2
    while step:
        upper = (granule & step) != 0
        for low in range(count):
            if low & step:
                continue
            a, b = arrays[low], arrays[low + step]
            arrays[low] = jnp.where(upper, pltpu.roll(b, step * width, 1), a)
            arrays[low + step] = jnp.where(upper, b, pltpu.roll(a, LANES - step * width, 1))
        step //= 2
    return arrays


def window_sums(apodization, echo, groups):
    windows, channels = apodization.shape
    samples = echo.shape[-1]
    halves = samples // LANES // groups

    def kernel(apod_ref, echo_ref, out_ref):
        apod = apod_ref[...]
        high = apod.astype(jnp.bfloat16)
        rest = apod - high.astype(jnp.float32)
        middle = rest.astype(jnp.bfloat16)
        low = (rest - middle.astype(jnp.float32)).astype(jnp.bfloat16)
        terms = jnp.concatenate([high, middle, low], axis=0)
        sums = jnp.dot(terms, echo_ref[0], preferred_element_type=jnp.float32)
        sums = sums[:windows] + (sums[windows : 2 * windows] + sums[2 * windows :])
        for half in range(halves):
            blocks = [
                sums[:, (half * groups + i) * LANES : (half * groups + i + 1) * LANES]
                for i in range(groups)
            ]
            for group, share in enumerate(swap_granules(blocks)):
                out_ref[group, half] = share

    return pl.pallas_call(
        kernel,
        out_shape=jax.ShapeDtypeStruct((groups, halves, windows, LANES), jnp.float32),
        in_specs=[VMEM, VMEM],
        out_specs=VMEM,
        compiler_params=PARAMS,
    )(apodization, echo)


def panel_shares(panels, groups):
    transmits, slots, block, _ = panels.shape[1:]

    def kernel(panels_ref, out_ref):
        for transmit in range(transmits):
            for start in range(0, block, 32):
                rows = pl.ds(start, 32)
                tiles = [panels_ref[0, transmit, slot, rows].astype(jnp.float32) for slot in range(slots)]
                for group, share in enumerate(swap_granules(tiles)):
                    out_ref[group, transmit, rows] = share.astype(jnp.bfloat16)

    return pl.pallas_call(
        kernel,
        out_shape=jax.ShapeDtypeStruct((groups, transmits, block, LANES), panels.dtype),
        in_specs=[VMEM],
        out_specs=VMEM,
        compiler_params=PARAMS,
    )(panels)


def sum_and_copy(parts, copies):
    def kernel(parts_ref, out_ref):
        total = jnp.sum(parts_ref[...], axis=0)
        for copy in range(copies):
            out_ref[copy] = total

    return pl.pallas_call(
        kernel,
        out_shape=jax.ShapeDtypeStruct((copies,) + parts.shape[1:], parts.dtype),
        in_specs=[VMEM],
        out_specs=VMEM,
        compiler_params=PARAMS,
    )(parts)


def pick_and_copy(acquirer, line, copies):
    transmits = acquirer.shape[0]

    def kernel(acquirer_ref, line_ref, out_ref):
        for transmit in range(transmits):
            picked = line_ref[lax.rem(lax.div(acquirer_ref[transmit], Z), Y)]
            for copy in range(copies):
                out_ref[copy, transmit] = picked

    return pl.pallas_call(
        kernel,
        out_shape=jax.ShapeDtypeStruct((copies, transmits) + line.shape[1:], line.dtype),
        in_specs=[SMEM, VMEM],
        out_specs=VMEM,
        compiler_params=PARAMS,
    )(acquirer, line)


def slot_sums(acquirer, counts, rows, columns, windows_of_voxels, table, shares):
    groups, transmits, block, _ = shares.shape
    windows = table.shape[3]
    slots = rows.shape[2] // groups
    width = LANES // slots
    row_blocks = windows_of_voxels.shape[0] // block
    windows_of_voxels = windows_of_voxels.reshape(row_blocks, 1, block)

    def kernel(acquirer_ref, counts_ref, rows_ref, columns_ref, index_ref, table_ref, shares_ref, out_ref):
        granule = lax.broadcasted_iota(jnp.int32, (windows, LANES), 1) // width
        total = jnp.zeros((row_blocks * 2 * windows, block), jnp.float32)
        for transmit in range(transmits):
            root = acquirer_ref[transmit]
            member = lax.div(root, Y * Z) * Z + lax.rem(root, Z)
            for group in range(groups):
                gathered = jnp.zeros((windows, LANES), jnp.float32)
                row_of = jnp.full((windows, LANES), row_blocks, jnp.int32)
                for i in range(slots):
                    k = group * slots + i
                    column = columns_ref[transmit, 0, k]
                    row = jnp.where(k < counts_ref[0, transmit], rows_ref[transmit, 0, k], row_blocks)
                    samples = table_ref[member, transmit, lax.div(column, slots)]
                    samples = pltpu.roll(samples, ((i - column) & (slots - 1)) * width, 1)
                    gathered = jnp.where(granule == i, samples, gathered)
                    row_of = jnp.where(granule == i, row, row_of)
                high = gathered.astype(jnp.bfloat16).astype(jnp.float32)
                low = gathered - high
                left = []
                for row in range(row_blocks):
                    left.append(jnp.where(row_of == row, high, 0.0).astype(jnp.bfloat16))
                    left.append(jnp.where(row_of == row, low, 0.0).astype(jnp.bfloat16))
                total += lax.dot_general(
                    jnp.concatenate(left, axis=0),
                    shares_ref[group, transmit],
                    NT,
                    preferred_element_type=jnp.float32,
                )
        number = lax.broadcasted_iota(jnp.int32, (windows, block), 0)
        for row in range(row_blocks):
            start = 2 * windows * row
            both = total[start : start + windows] + total[start + windows : start + 2 * windows]
            out_ref[row] = jnp.sum(jnp.where(number == index_ref[row], both, 0.0), axis=0, keepdims=True)

    return pl.pallas_call(
        kernel,
        out_shape=jax.ShapeDtypeStruct((row_blocks, 1, block), jnp.float32),
        in_specs=[SMEM, SMEM, SMEM, SMEM, VMEM, VMEM, VMEM],
        out_specs=VMEM,
        compiler_params=PARAMS,
    )(acquirer, counts, rows, columns, windows_of_voxels, table, shares)


def exchange(pieces, axis, lines=None):
    return lax.all_to_all(
        pieces, axis, split_axis=0, concat_axis=0, axis_index_groups=lines, tiled=True
    )


def per_device(
    echo_data, acquirer, panels, block_count, block_rows, block_columns, apodization, window_index
):
    slabs, groups = lax.axis_size("slab"), lax.axis_size("grp")
    x = slabs // (Y * Z)
    along_y = [[(i * Y + j) * Z + k for j in range(Y)] for i in range(x) for k in range(Z)]
    along_xz = [[(i * Y + j) * Z + k for i in range(x) for k in range(Z)] for j in range(Y)]
    shares = exchange(panel_shares(panels, groups), "grp")
    parts = exchange(window_sums(apodization, echo_data, groups), "grp")
    line = lax.all_gather(sum_and_copy(parts, 1)[0], "slab", axis_index_groups=along_y)
    table = lax.all_gather(pick_and_copy(acquirer, line, 1)[0], "slab", axis_index_groups=along_xz)
    rows, columns = (jnp.transpose(v, (1, 0, 2)) for v in (block_rows, block_columns))
    partial = slot_sums(acquirer, block_count, rows, columns, window_index, table, shares)
    return jnp.sum(exchange(partial, "grp"), axis=(0, 1))


def solution(mesh):
    return jax.shard_map(
        per_device,
        mesh=mesh,
        in_specs=(
            P("slab", "grp", None),
            P(),
            P("slab", None, "grp", None, None),
            P("slab", None),
            P("slab", None, None),
            P("slab", None, None),
            P(None, "grp"),
            P("slab"),
        ),
        out_specs=P(("slab", "grp")),
        check_vma=False,
    )
```

time: 76.5 us -> 102 us (1.33)
  blocking collectives: 53.1 us -> 69.7 us
  starting transfers between devices: 4.76 us -> 16.5 us
  waiting for transfers between devices: 13.1 us -> 5.97 us
  Pallas kernels: 2.7 us -> 6.19 us
    all_gather x0 -> x2, blocking collectives: none -> 44.8 us  [the longest x1 24.1 us: per_device(): lax.all_gather(pick_and_copy(acquirer, line, 1)[0], 'slab', axis_index_gr...]
    all_to_all x3 -> x1, blocking collectives: 53.1 us -> 24.9 us  [exchange(): lax.all_to_all(pieces, axis, split_axis=0, concat_axis=0, axis_index_grou...]
    all_to_all x1 -> x2, starting transfers between devices: 4.76 us -> 16.5 us  [exchange(): lax.all_to_all(pieces, axis, split_axis=0, concat_axis=0, axis_index_grou...]
    all_to_all x1 -> x2, waiting for transfers between devices: 13.1 us -> 5.97 us  [exchange(): lax.all_to_all(pieces, axis, split_axis=0, concat_axis=0, axis_index_grou...]
    pallas_call x2 -> x3, Pallas kernels: 0.75 us -> 4.41 us  [the longest x1 2.76 us: panel_shares(): pl.pallas_call(kernel, out_shape=jax.ShapeDtypeStruct((groups, transmits,...]
    unnamed x18 -> x16, local copies, waits for them, and re-layouts: 1.77 us -> 2.5 us
  transfers between devices with their start and end apart: 1 -> 2, of which waited for: 1 -> 1; matrix products, arithmetic and copies ran while one was open for 0% -> 0% of each run, Pallas kernels for 0% -> 3%
where the time goes in v3:
time: 102 us; the launch traced here: 101 us
  blocking collectives  69.7 us (68%)
  starting transfers between devices  16.5 us (16%)
  Pallas kernels  6.19 us (6%)
  waiting for transfers between devices  5.97 us (6%)
  local copies, waits for them, and re-layouts  2.5 us (2%)
    all_to_all x1, blocking collectives, exchange(): lax.all_to_all(pieces, axis, split_axis=0, concat_axis=0, axis_index_grou...  24.9 us
    all_gather x1, blocking collectives, per_device(): lax.all_gather(pick_and_copy(acquirer, line, 1)[0], 'slab', axis_index_gr...  24.1 us
    all_gather x1, blocking collectives, per_device(): lax.all_gather(sum_and_copy(parts, 1)[0], 'slab', axis_index_groups=along_y)  20.8 us
    all_to_all x2, starting transfers between devices, exchange(): lax.all_to_all(pieces, axis, split_axis=0, concat_axis=0, axis_index_grou...  16.5 us
    all_to_all x2, waiting for transfers between devices, exchange(): lax.all_to_all(pieces, axis, split_axis=0, concat_axis=0, axis_index_grou...  5.97 us
    pallas_call x1, Pallas kernels, panel_shares(): pl.pallas_call(kernel, out_shape=jax.ShapeDtypeStruct((groups, transmits,...  2.76 us
    unnamed x16, local copies, waits for them, and re-layouts  2.5 us
  transfers between devices with their start and end apart: 2, of which 1 were waited for; matrix products, arithmetic and copies ran while one was open for 0% of the time, Pallas kernels for 3%

profile of v3, /device:TPU:1, one launch (start us, length us, event | category | flops | bytes accessed | tf_op | source)
XLA Modules:
  0.0 101.5 jit_solution(8694295968277559202)
XLA Ops:
  0.0 0.0 copy-start
  0.0 0.0 copy-start.1
  0.0 1.1 %copy-done.1 = bf16[1,128,2048]{2,1,0:T(8,128)(2,1)S(1)} copy-done((bf16[1,128,2048]{2,1,0:T(8,128)(2,1)S(1)}, bf16[1,128,2048]{2,1,0:T(8,128)(2,1)}, u32[]{:S(2)}) %copy-start.1) | copy-done | bytes 524312
  1.1 0.0 copy-start.2
  1.1 0.7 copy-done.2
  1.8 1.1 %shard_map.82 = f32[8,2,16,128]{3,2,1,0:T(8,128)} custom-call(f32[16,128]{1,0:T(8,128)S(1)} %copy-done.2, bf16[1,128,2048]{2,1,0:T(8,128)(2,1)S(1)} %copy-done.1), custom_call_target="tpu_custom_call" | custom-call | tf_op jit(solution)/shard_map/pallas_call | solution.py:56
  2.9 11.8 %all-to-all-start = ((f32[8,2,16,128]{3,2,1,0:T(8,128)}), f32[8,2,16,128]{3,2,1,0:T(8,128)S(1)}, u32[]{:S(2)}, u32[]{:S(2)}) async-start(f32[8,2,16,128]{3,2,1,0:T(8,128)} %shard_map.82), calls=%async_computation | async-start | bytes 262144 | tf_op jit(solution)/shard_map/all_to_all | solution.py:171
  14.7 0.0 copy-done
  14.7 2.8 %shard_map.85 = bf16[8,3,128,128]{3,2,1,0:T(8,128)(2,1)} custom-call(bf16[1,3,8,128,128]{4,3,2,1,0:T(8,128)(2,1)S(1)} %copy-done), custom_call_target="tpu_custom_call" | custom-call | tf_op jit(solution)/shard_map/pallas_call | solution.py:76
  17.5 6.0 %all-to-all-done.parts_ref = f32[8,2,16,128]{3,2,1,0:T(8,128)S(1)} async-done(((f32[8,2,16,128]{3,2,1,0:T(8,128)}), f32[8,2,16,128]{3,2,1,0:T(8,128)S(1)}, u32[]{:S(2)}, u32[]{:S(2)}) %all-to-all-start) | async-done | bytes 131104 | tf_op jit(solution)/shard_map/all_to_all | solution.py:171
  23.5 4.7 %all-to-all-start.1 = ((bf16[8,3,128,128]{3,2,1,0:T(8,128)(2,1)}), bf16[8,3,128,128]{3,2,1,0:T(8,128)(2,1)S(1)}, u32[]{:S(2)}, u32[]{:S(2)}) async-start(bf16[8,3,128,128]{3,2,1,0:T(8,128)(2,1)} %shard_map.85), calls=%async_computation.1 | async-start | bytes 1572864 | tf_op jit(solution)/shard_map/all_to_all | solution.py:171
  28.1 0.0 copy-start.4
  28.1 20.8 %all_gather.6.line_ref = f32[8,2,16,128]{3,2,1,0:T(8,128)S(1)} all-gather(f32[1,2,16,128]{3,2,1,0:T(8,128)S(1)} %shard_map.83), channel_id=1, replica_groups={{0,16,32,48,64,80,96,112},{8,24,40,56,72,88,104,120},{128,144,160,176,1..., dimensions={0}, use_global_device_ids=true | all-gather | bytes 147456 | tf_op jit(solution)/shard_map/all_gather | solution.py:185
  48.9 0.0 copy-done.4
  48.9 0.6 shard_map.84
  49.5 0.0 copy-start.6
  49.5 0.0 copy-start.7
  49.5 24.1 %all_gather.7.table_ref = f32[8,3,2,16,128]{4,3,2,1,0:T(8,128)S(1)} all-gather(f32[1,3,2,16,128]{4,3,2,1,0:T(8,128)S(1)} %shard_map.84), channel_id=1, replica_groups={{0,8,128,136,256,264,384,392},{16,24,144,152,272,280,400,408},{32,40,16..., dimensions={0}, use_global_device_ids=true | all-gather | bytes 442368 | tf_op jit(solution)/shard_map/all_gather | solution.py:186
  73.6 0.0 copy-start.3
  73.6 0.0 all-to-all-done.1.shares_ref
  73.6 0.0 copy-start.5
  73.6 0.0 copy-done.6
  73.6 0.0 copy-done.7
  73.6 0.7 copy-done.3
  74.2 0.0 copy-done.5
  74.3 1.8 %shard_map.86 = f32[8,1,128]{2,1,0:T(1,128)S(1)} custom-call(s32[3]{0:T(128)S(1)} %copy-done.4, s32[1,3]{1,0:T(1,128)S(1)} %copy-done.7, s32[3,1,64]{2,1,0:T(1,128)S(1)} %bitcast.4, s32[3,1,64]{2,1,0:T(1,128)S(1)} %bitcast.5, s32[8,1,128]{2,1,0:T(1,128)S(1)} %bitcast.3, f32[8,3,2,16,128]{4,3,2,1,0:T(8,128)S(1)} %all_gather.7.table_ref, ...), custom_call_target="tpu_custom_call" | custom-call | tf_op jit(solution)/shard_map/pallas_call | solution.py:161
  76.0 24.9 %all_to_all.15 = f32[8,1,128]{2,1,0:T(1,128)S(1)} all-to-all(f32[8,1,128]{2,1,0:T(1,128)S(1)} %shard_map.86), channel_id=1, replica_groups=mesh['slab'=64,'grp'=8] {'grp'}, dimensions={0} | all-to-all | bytes 8192 | tf_op jit(solution)/shard_map/all_to_all | solution.py:171
  100.9 0.5 reduce_sum.9
  (1 shorter events, 0.0 us)
Async XLA Ops:
  0.0 14.7 %copy-start = (bf16[1,3,8,128,128]{4,3,2,1,0:T(8,128)(2,1)S(1)}, bf16[1,3,8,128,128]{4,3,2,1,0:T(8,128)(2,1)}, u32[]{:S(2)}) copy-start(bf16[1,3,8,128,128]{4,3,2,1,0:T(8,128)(2,1)} %panels_ref.1) | copy-start | bytes 2359300
  0.0 1.1 %copy-start.1 = (bf16[1,128,2048]{2,1,0:T(8,128)(2,1)S(1)}, bf16[1,128,2048]{2,1,0:T(8,128)(2,1)}, u32[]{:S(2)}) copy-start(bf16[1,128,2048]{2,1,0:T(8,128)(2,1)} %echo_ref.1) | copy-start | bytes 1572868
  1.1 0.7 copy-start.2
  2.9 20.5 %all-to-all-start = ((f32[8,2,16,128]{3,2,1,0:T(8,128)}), f32[8,2,16,128]{3,2,1,0:T(8,128)S(1)}, u32[]{:S(2)}, u32[]{:S(2)}) async-start(f32[8,2,16,128]{3,2,1,0:T(8,128)} %shard_map.82), calls=%async_computation | async-start | bytes 262144 | tf_op jit(solution)/shard_map/all_to_all | solution.py:171
  23.5 50.1 %all-to-all-start.1 = ((bf16[8,3,128,128]{3,2,1,0:T(8,128)(2,1)}), bf16[8,3,128,128]{3,2,1,0:T(8,128)(2,1)S(1)}, u32[]{:S(2)}, u32[]{:S(2)}) async-start(bf16[8,3,128,128]{3,2,1,0:T(8,128)(2,1)} %shard_map.85), calls=%async_computation.1 | async-start | bytes 1572864 | tf_op jit(solution)/shard_map/all_to_all | solution.py:171
  28.1 20.8 %copy-start.4 = (s32[3]{0:T(128)S(1)}, s32[3]{0:T(128)}, u32[]{:S(2)}) copy-start(s32[3]{0:T(128)} %acquirer_ref.3) | copy-start | bytes 40
  49.5 24.1 %copy-start.6 = (s32[1,3,64]{2,0,1:T(1,128)S(1)}, s32[1,3,64]{2,0,1:T(1,128)}, u32[]{:S(2)}) copy-start(s32[1,3,64]{2,0,1:T(1,128)} %param.13) | copy-start | bytes 2308
  49.5 24.1 %copy-start.7 = (s32[1,3]{1,0:T(1,128)S(1)}, s32[1,3]{1,0:T(1,128)}, u32[]{:S(2)}) copy-start(s32[1,3]{1,0:T(1,128)} %counts_ref.1) | copy-start | bytes 40
  73.6 0.7 copy-start.3
  73.6 0.7 copy-start.5

commit v4 on v1

v4 whole, which is shorter than its diff:
```python
import jax
import jax.numpy as jnp
from jax import lax
from jax.experimental import pallas as pl
from jax.experimental.pallas import tpu as pltpu
from jax.sharding import PartitionSpec as P

LANES, SUBLANES = 128, 8
Z = 2
VMEM = pl.BlockSpec(memory_space=pltpu.VMEM)
SMEM = pl.BlockSpec(memory_space=pltpu.SMEM)
NT = (((1,), (1,)), ((), ()))
PARAMS = pltpu.CompilerParams(vmem_limit_bytes=8 * 1024 * 1024)


def window_sums(apodization, echo):
    windows, channels = apodization.shape
    samples = echo.shape[-1]
    blocks, halves = samples // LANES, windows // SUBLANES

    def kernel(apod_ref, echo_ref, out_ref):
        apod = apod_ref[...]
        high = apod.astype(jnp.bfloat16)
        rest = apod - high.astype(jnp.float32)
        middle = rest.astype(jnp.bfloat16)
        low = (rest - middle.astype(jnp.float32)).astype(jnp.bfloat16)
        terms = jnp.concatenate([high, middle, low], axis=0)
        sums = jnp.dot(terms, echo_ref[0], preferred_element_type=jnp.float32)
        sums = sums[:windows] + (sums[windows : 2 * windows] + sums[2 * windows :])
        for block in range(blocks):
            for half in range(halves):
                out_ref[block * halves + half] = sums[
                    half * SUBLANES : (half + 1) * SUBLANES, block * LANES : (block + 1) * LANES
                ]

    return pl.pallas_call(
        kernel,
        out_shape=jax.ShapeDtypeStruct((blocks * halves, SUBLANES, LANES), jnp.float32),
        in_specs=[VMEM, VMEM],
        out_specs=VMEM,
        compiler_params=PARAMS,
    )(apodization, echo)


def pick_acquirers(acquirer, pieces, copies, rows, slots):
    transmits = acquirer.shape[0]

    def kernel(acquirer_ref, pieces_ref, rows_ref, out_ref, rows_out):
        for transmit in range(transmits):
            picked = pieces_ref[lax.div(acquirer_ref[transmit], Z)]
            for copy in range(copies):
                out_ref[copy, transmit] = picked
        first = lax.axis_index("grp") * slots
        for transmit in range(transmits):
            for slot in range(slots):
                rows_out[transmit * slots + slot] = rows_ref[transmit, 0, first + slot]

    return pl.pallas_call(
        kernel,
        out_shape=(
            jax.ShapeDtypeStruct((copies, transmits) + pieces.shape[1:], pieces.dtype),
            jax.ShapeDtypeStruct((transmits * slots,), jnp.int32),
        ),
        in_specs=[SMEM, VMEM, SMEM],
        out_specs=(VMEM, SMEM),
        compiler_params=PARAMS,
    )(acquirer, pieces, rows)


def sum_and_copy(acquirer, parts, groups, copies, counts, own_rows, columns, slots, row_blocks):
    transmits = acquirer.shape[0]

    def kernel(acquirer_ref, parts_ref, counts_ref, rows_ref, columns_ref, out_ref, slots_out):
        for transmit in range(transmits):
            start = lax.rem(acquirer_ref[transmit], Z) * groups
            total = parts_ref[start, transmit]
            for group in range(1, groups):
                total += parts_ref[start + group, transmit]
            for copy in range(copies):
                out_ref[copy, transmit] = total
        first = lax.axis_index("grp") * slots
        for transmit in range(transmits):
            for slot in range(slots):
                place, k = transmit * slots + slot, first + slot
                live = k < counts_ref[0, transmit]
                slots_out[0, place] = jnp.where(live, rows_ref[place], row_blocks)
                slots_out[1, place] = columns_ref[transmit, 0, k]

    return pl.pallas_call(
        kernel,
        out_shape=(
            jax.ShapeDtypeStruct((copies,) + parts.shape[1:], parts.dtype),
            jax.ShapeDtypeStruct((2, transmits * slots), jnp.int32),
        ),
        in_specs=[SMEM, VMEM, SMEM, SMEM, SMEM],
        out_specs=(VMEM, SMEM),
        compiler_params=PARAMS,
    )(acquirer, parts, counts, own_rows, columns)


def slot_sums(slot_table, windows_of_voxels, table, panels, halves):
    transmits, slots, block, _ = panels.shape[1:]
    row_blocks = windows_of_voxels.shape[0]
    windows = halves * SUBLANES

    def kernel(slots_ref, index_ref, table_ref, panels_ref, out_ref, total):
        total[...] = jnp.zeros_like(total)
        for transmit in range(transmits):
            for slot in range(slots):
                row = slots_ref[0, transmit * slots + slot]
                column = slots_ref[1, transmit * slots + slot]
                weighted = jnp.concatenate(
                    [table_ref[column * halves + half, transmit] for half in range(halves)], axis=0
                )
                high = weighted.astype(jnp.bfloat16)
                low = (weighted - high.astype(jnp.float32)).astype(jnp.bfloat16)
                terms = lax.dot_general(
                    jnp.concatenate([high, low], axis=0),
                    panels_ref[0, transmit, slot],
                    NT,
                    preferred_element_type=jnp.float32,
                )
                total[row] += terms[:windows] + terms[windows:]
        number = lax.broadcasted_iota(jnp.int32, (windows, block), 0)
        for row in range(row_blocks):
            chosen = jnp.where(number == index_ref[row], total[row], 0.0)
            out_ref[row] = jnp.sum(chosen, axis=0, keepdims=True)

    return pl.pallas_call(
        kernel,
        out_shape=jax.ShapeDtypeStruct((row_blocks, 1, block), jnp.float32),
        in_specs=[SMEM, VMEM, VMEM, VMEM],
        out_specs=VMEM,
        scratch_shapes=[pltpu.VMEM((row_blocks + 1, windows, block), jnp.float32)],
        compiler_params=PARAMS,
    )(slot_table, windows_of_voxels, table, panels)


def exchange(pieces, axis, lines=None):
    return lax.all_to_all(
        pieces, axis, split_axis=0, concat_axis=0, axis_index_groups=lines, tiled=True
    )


def per_device(
    echo_data, acquirer, panels, block_count, block_rows, block_columns, apodization, window_index
):
    slabs, groups = lax.axis_size("slab"), lax.axis_size("grp")
    slots, block = panels.shape[2], panels.shape[3]
    planes = [list(range(z, slabs, Z)) for z in range(Z)]
    lines = [
        [(chip * Z + z) * groups + group for z in range(Z) for group in range(groups)]
        for chip in range(slabs // Z)
    ]
    row_blocks = window_index.shape[0] // block
    rows, columns = (jnp.transpose(v, (1, 0, 2)) for v in (block_rows, block_columns))
    voxels = window_index.reshape(row_blocks, 1, block)
    pieces = exchange(window_sums(apodization, echo_data), "slab", planes)
    picked, own_rows = pick_acquirers(acquirer, pieces, Z * groups, rows, slots)
    parts = exchange(picked, ("slab", "grp"), lines)
    sums, slot_table = sum_and_copy(
        acquirer, parts, groups, slabs // Z, block_count, own_rows, columns, slots, row_blocks
    )
    table = exchange(sums, "slab", planes)
    partial = slot_sums(slot_table, voxels, table, panels, apodization.shape[0] // SUBLANES)
    return jnp.sum(exchange(partial, "grp"), axis=(0, 1))


def solution(mesh):
    return jax.shard_map(
        per_device,
        mesh=mesh,
        in_specs=(
            P("slab", "grp", None),
            P(),
            P("slab", None, "grp", None, None),
            P("slab", None),
            P("slab", None, None),
            P("slab", None, None),
            P(None, "grp"),
            P("slab"),
        ),
        out_specs=P(("slab", "grp")),
        check_vma=False,
    )
```

time: 76.5 us -> 76.6 us (level)
  blocking collectives: 53.1 us -> 70.2 us
  waiting for transfers between devices: 13.1 us -> 0 us
  starting transfers between devices: 4.76 us -> 0 us
  Pallas kernels: 2.7 us -> 3.74 us
    all_to_all x3 -> x4, blocking collectives: 53.1 us -> 70.2 us  [exchange(): lax.all_to_all(pieces, axis, split_axis=0, concat_axis=0, axis_index_grou...]
    all_to_all x1 -> x0, waiting for transfers between devices: 13.1 us -> none  [exchange(): return lax.all_to_all(pieces, axis, split_axis=0, concat_axis=0, tiled=True)]
    all_to_all x1 -> x0, starting transfers between devices: 4.76 us -> none  [exchange(): return lax.all_to_all(pieces, axis, split_axis=0, concat_axis=0, tiled=True)]
    pallas_call x3, Pallas kernels: 1.55 us -> 2.65 us  [the longest x1 1.25 us: sum_and_copy(): pl.pallas_call(kernel, out_shape=(jax.ShapeDtypeStruct((copies,) + parts....]
    unnamed x18 -> x16, local copies, waits for them, and re-layouts: 1.77 us -> 1.77 us
  transfers between devices with their start and end apart: 1 -> 0, of which waited for: 1 -> 0; matrix products, arithmetic and copies ran while one was open for 0% -> 0% of each run, Pallas kernels for 0% -> 0%
where the time goes in v4:
time: 76.6 us; the launch traced here: 76.3 us
  blocking collectives  70.2 us (92%)
  Pallas kernels  3.74 us (5%)
  local copies, waits for them, and re-layouts  1.77 us (2%)
    all_to_all x4, blocking collectives, exchange(): lax.all_to_all(pieces, axis, split_axis=0, concat_axis=0, axis_index_grou...  70.2 us
    unnamed x16, local copies, waits for them, and re-layouts  1.77 us

profile of v4, /device:TPU:1, one launch (start us, length us, event | category | flops | bytes accessed | tf_op | source)
XLA Modules:
  0.0 76.3 jit_solution(12683274543067149884)
XLA Ops:
  0.0 0.0 copy-start.1
  0.0 1.0 %copy-done.1 = bf16[1,128,2048]{2,1,0:T(8,128)(2,1)S(1)} copy-done((bf16[1,128,2048]{2,1,0:T(8,128)(2,1)S(1)}, bf16[1,128,2048]{2,1,0:T(8,128)(2,1)}, u32[]{:S(2)}) %copy-start.1) | copy-done | bytes 524312
  1.0 0.0 copy-start.2
  1.0 0.7 copy-done.2
  1.7 0.2 shard_map.82
  1.9 0.0 copy-start.4
  1.9 0.0 copy-start.5
  1.9 0.0 copy-start.6
  2.0 0.0 copy-start.7
  2.0 19.6 %all_to_all.20.pieces_ref = f32[32,8,128]{2,1,0:T(8,128)S(1)} all-to-all(f32[32,8,128]{2,1,0:T(8,128)S(1)} %shard_map.82), channel_id=1, replica_groups={{0,16,32,48,64,80,96,112,128,144,160,176,192,208,224,240,256,272,288,30..., dimensions={0} | all-to-all | bytes 262144 | tf_op jit(solution)/shard_map/all_to_all | solution.py:140
  21.6 0.0 copy-start
  21.6 0.0 copy-done.4
  21.6 0.0 copy-done.5
  21.6 1.2 %shard_map.83 = (f32[16,3,8,128]{3,2,1,0:T(8,128)S(1)}, s32[24]{0:T(128)S(1)}) custom-call(s32[3]{0:T(128)S(1)} %copy-done.4, f32[32,8,128]{2,1,0:T(8,128)S(1)} %all_to_all.20.pieces_ref, s32[3,1,64]{2,1,0:T(1,128)S(1)} %bitcast.4), custom_call_target="tpu_custom_call" | custom-call | tf_op jit(solution)/shard_map/pallas_call | solution.py:58
  22.8 22.7 %all_to_all.21.parts_ref = f32[16,3,8,128]{3,2,1,0:T(8,128)S(1)} all-to-all(f32[16,3,8,128]{3,2,1,0:T(8,128)S(1)} %get-tuple-element.9), channel_id=1, replica_groups={{0,1,2,3,4,5,6,7,8,9,10,11,12,13,14,15},{16,17,18,19,20,21,22,23,24,25,..., dimensions={0} | all-to-all | bytes 393216 | tf_op jit(solution)/shard_map/all_to_all | solution.py:140
  45.5 0.0 copy-done.6
  45.5 0.0 copy-done.7
  45.5 1.3 %shard_map.84 = (f32[32,3,8,128]{3,2,1,0:T(8,128)S(1)}, s32[2,24]{1,0:T(2,128)S(1)}) custom-call(s32[3]{0:T(128)S(1)} %copy-done.4, f32[16,3,8,128]{3,2,1,0:T(8,128)S(1)} %all_to_all.21.parts_ref, s32[1,3]{1,0:T(1,128)S(1)} %copy-done.7, s32[24]{0:T(128)S(1)} %get-tuple-element.10.rows_ref, s32[3,1,64]{2,1,0:T(1,128)S(1)} %bitcast.5), custom_call_target="tpu_custom_call" | custom-call | tf_op jit(solution)/shard_map/pallas_call | solution.py:89
  46.8 0.0 copy-start.3
  46.8 17.3 %all_to_all.22.table_ref = f32[32,3,8,128]{3,2,1,0:T(8,128)S(1)} all-to-all(f32[32,3,8,128]{3,2,1,0:T(8,128)S(1)} %get-tuple-element.12), channel_id=1, replica_groups={{0,16,32,48,64,80,96,112,128,144,160,176,192,208,224,240,256,272,288,30..., dimensions={0} | all-to-all | bytes 786432 | tf_op jit(solution)/shard_map/all_to_all | solution.py:140
  64.1 0.0 copy-done
  64.1 0.0 copy-done.3
  64.1 1.1 %shard_map.85 = f32[8,1,128]{2,1,0:T(1,128)S(1)} custom-call(s32[2,24]{1,0:T(2,128)S(1)} %get-tuple-element.11.slots_ref, s32[8,1,128]{2,1,0:T(1,128)S(1)} %bitcast.3, f32[32,3,8,128]{3,2,1,0:T(8,128)S(1)} %all_to_all.22.table_ref, bf16[1,3,8,128,128]{4,3,2,1,0:T(8,128)(2,1)S(1)} %copy-done), custom_call_target="tpu_custom_call" | custom-call | tf_op jit(solution)/shard_map/pallas_call | solution.py:129
  65.2 10.5 %all_to_all.23 = f32[8,1,128]{2,1,0:T(1,128)S(1)} all-to-all(f32[8,1,128]{2,1,0:T(1,128)S(1)} %shard_map.85), channel_id=1, replica_groups=mesh['slab'=64,'grp'=8] {'grp'}, dimensions={0} | all-to-all | bytes 8192 | tf_op jit(solution)/shard_map/all_to_all | solution.py:140
  75.8 0.5 reduce_sum.9
Async XLA Ops:
  0.0 1.0 %copy-start.1 = (bf16[1,128,2048]{2,1,0:T(8,128)(2,1)S(1)}, bf16[1,128,2048]{2,1,0:T(8,128)(2,1)}, u32[]{:S(2)}) copy-start(bf16[1,128,2048]{2,1,0:T(8,128)(2,1)} %echo_ref.1) | copy-start | bytes 1572868
  1.0 0.7 copy-start.2
  1.9 19.6 %copy-start.4 = (s32[3]{0:T(128)S(1)}, s32[3]{0:T(128)}, u32[]{:S(2)}) copy-start(s32[3]{0:T(128)} %acquirer_ref.3) | copy-start | bytes 40
  1.9 19.6 %copy-start.5 = (s32[1,3,64]{2,0,1:T(1,128)S(1)}, s32[1,3,64]{2,0,1:T(1,128)}, u32[]{:S(2)}) copy-start(s32[1,3,64]{2,0,1:T(1,128)} %param.12) | copy-start | bytes 2308
  1.9 43.6 %copy-start.6 = (s32[1,3,64]{2,0,1:T(1,128)S(1)}, s32[1,3,64]{2,0,1:T(1,128)}, u32[]{:S(2)}) copy-start(s32[1,3,64]{2,0,1:T(1,128)} %param.13) | copy-start | bytes 2308
  2.0 43.5 %copy-start.7 = (s32[1,3]{1,0:T(1,128)S(1)}, s32[1,3]{1,0:T(1,128)}, u32[]{:S(2)}) copy-start(s32[1,3]{1,0:T(1,128)} %counts_ref.1) | copy-start | bytes 40
  21.6 42.5 %copy-start = (bf16[1,3,8,128,128]{4,3,2,1,0:T(8,128)(2,1)S(1)}, bf16[1,3,8,128,128]{4,3,2,1,0:T(8,128)(2,1)}, u32[]{:S(2)}) copy-start(bf16[1,3,8,128,128]{4,3,2,1,0:T(8,128)(2,1)} %panels_ref.1) | copy-start | bytes 2359300
  46.8 17.3 %copy-start.3 = (s32[1024]{0:T(1024)S(1)}, s32[1024]{0:T(1024)}, u32[]{:S(2)}) copy-start(s32[1024]{0:T(1024)} %param.15) | copy-start | bytes 12292

commit v5 on v2

--- a/solution.py
+++ b/solution.py
@@ -41,10 +41,17 @@
     )(apodization, echo)
 
 
-def pick_acquirers(acquirer, pieces, copies):
+def hand_on(refs, count):
+    for i in range(count):
+        refs[count + 1 + i][...] = refs[i][...]
+    return refs[count]
+
+
+def pick_acquirers(acquirer, pieces, copies, handed):
     transmits = acquirer.shape[0]
 
-    def kernel(acquirer_ref, pieces_ref, out_ref):
+    def kernel(acquirer_ref, pieces_ref, *refs):
+        out_ref = hand_on(refs, len(handed))
         for transmit in range(transmits):
             picked = pieces_ref[acquirer_ref[transmit]]
             for copy in range(copies):
@@ -52,34 +59,40 @@
 
     return pl.pallas_call(
         kernel,
-        out_shape=jax.ShapeDtypeStruct((copies, transmits) + pieces.shape[1:], pieces.dtype),
-        in_specs=[SMEM, VMEM],
-        out_specs=VMEM,
+        out_shape=(
+            jax.ShapeDtypeStruct((copies, transmits) + pieces.shape[1:], pieces.dtype),
+            *(jax.ShapeDtypeStruct(table.shape, table.dtype) for table in handed),
+        ),
+        in_specs=[SMEM, VMEM] + [VMEM] * len(handed),
+        out_specs=(VMEM,) * (1 + len(handed)),
         compiler_params=PARAMS,
-    )(acquirer, pieces)
+    )(acquirer, pieces, *handed)
 
 
-def sum_and_copy(parts, copies):
-    def kernel(parts_ref, out_ref):
+def sum_and_copy(parts, copies, handed):
+    def kernel(parts_ref, *refs):
+        out_ref = hand_on(refs, len(handed))
         total = jnp.sum(parts_ref[...], axis=0)
         for copy in range(copies):
             out_ref[copy] = total
 
     return pl.pallas_call(
         kernel,
-        out_shape=jax.ShapeDtypeStruct((copies,) + parts.shape[1:], parts.dtype),
-        in_specs=[VMEM],
-        out_specs=VMEM,
+        out_shape=(
+            jax.ShapeDtypeStruct((copies,) + parts.shape[1:], parts.dtype),
+            *(jax.ShapeDtypeStruct(table.shape, table.dtype) for table in handed),
+        ),
+        in_specs=[VMEM] * (1 + len(handed)),
+        out_specs=(VMEM,) * (1 + len(handed)),
         compiler_params=PARAMS,
-    )(parts)
+    )(parts, *handed)
 
 
 def slot_sums(counts, rows, columns, windows_of_voxels, table, panels):
     transmits, slots, block, _ = panels.shape[1:]
     quarters = 4
-    row_blocks = windows_of_voxels.shape[0] // block
+    row_blocks = windows_of_voxels.shape[0]
     windows = quarters * table.shape[2]
-    windows_of_voxels = windows_of_voxels.reshape(row_blocks, 1, block)
 
     def kernel(counts_ref, rows_ref, columns_ref, index_ref, table_ref, panels_ref, out_ref, total):
         first = lax.axis_index("grp") * slots
@@ -125,11 +138,13 @@
     echo_data, acquirer, panels, block_count, block_rows, block_columns, apodization, window_index
 ):
     slabs, groups = lax.axis_size("slab"), lax.axis_size("grp")
+    rows, columns = (jnp.transpose(x, (1, 0, 2)) for x in (block_rows, block_columns))
     pieces = exchange(window_sums(apodization, echo_data), "slab")
-    parts = exchange(pick_acquirers(acquirer, pieces, groups), "grp")
-    table = exchange(sum_and_copy(parts, slabs), "slab")
-    rows, columns = (jnp.transpose(x, (1, 0, 2)) for x in (block_rows, block_columns))
-    partial = slot_sums(block_count, rows, columns, window_index, table, panels)
+    voxels = window_index.reshape(-1, 1, panels.shape[-1])
+    picked, rows, voxels = pick_acquirers(acquirer, pieces, groups, (rows, voxels))
+    sums, columns, counts = sum_and_copy(exchange(picked, "grp"), slabs, (columns, block_count))
+    table = exchange(sums, "slab")
+    partial = slot_sums(counts, rows, columns, voxels, table, panels)
     return jnp.sum(exchange(partial, "grp"), axis=(0, 1))
 
 

time: 75.9 us -> 75.2 us (level)
  no operation moved by 1% of the time
where the time goes in v5:
time: 75.2 us; the launch traced here: 74.9 us
  blocking collectives  70.6 us (94%)
  Pallas kernels  1.94 us (3%)
  local copies, waits for them, and re-layouts  1.76 us (2%)
    all_to_all x4, blocking collectives, exchange(): return lax.all_to_all(pieces, axis, split_axis=0, concat_axis=0, tiled=True)  70.6 us
    unnamed x16, local copies, waits for them, and re-layouts  1.76 us

profile of v5, /device:TPU:1, one launch (start us, length us, event | category | flops | bytes accessed | tf_op | source)
XLA Modules:
  0.0 74.9 jit_solution(15928067630173561486)
XLA Ops:
  0.0 0.0 copy-start.1
  0.0 1.0 %copy-done.1 = bf16[1,128,2048]{2,1,0:T(8,128)(2,1)S(1)} copy-done((bf16[1,128,2048]{2,1,0:T(8,128)(2,1)S(1)}, bf16[1,128,2048]{2,1,0:T(8,128)(2,1)}, u32[]{:S(2)}) %copy-start.1) | copy-done | bytes 524312
  1.0 0.0 copy-start.2
  1.0 0.7 copy-done.2
  1.7 0.0 copy-start.3
  1.7 0.0 copy-start.4
  1.7 0.0 copy-start.6
  1.7 0.0 copy-start.5
  1.8 0.0 copy-start.7
  1.8 0.2 shard_map.82
  2.0 0.0 copy-start
  2.0 22.4 %all_to_all.20.pieces_ref = f32[64,4,128]{2,1,0:T(4,128)S(1)} all-to-all(f32[64,4,128]{2,1,0:T(4,128)S(1)} %shard_map.82), channel_id=1, replica_groups=mesh['slab'=64,'grp'=8] {'slab'}, dimensions={0} | all-to-all | bytes 262144 | tf_op jit(solution)/shard_map/all_to_all | solution.py:134
  24.4 0.0 copy-done.3
  24.4 0.0 copy-done.4
  24.4 0.0 copy-done.6
  24.4 0.6 shard_map.83
  24.9 18.6 %all_to_all.21.parts_ref = f32[8,3,4,128]{3,2,1,0:T(4,128)S(1)} all-to-all(f32[8,3,4,128]{3,2,1,0:T(4,128)S(1)} %get-tuple-element.11), channel_id=1, replica_groups=mesh['slab'=64,'grp'=8] {'grp'}, dimensions={0} | all-to-all | bytes 98304 | tf_op jit(solution)/shard_map/all_to_all | solution.py:134
  43.6 0.0 copy-done.5
  43.6 0.0 copy-done.7
  43.6 0.1 shard_map.84
  43.6 17.5 %all_to_all.22.table_ref = f32[64,3,4,128]{3,2,1,0:T(4,128)S(1)} all-to-all(f32[64,3,4,128]{3,2,1,0:T(4,128)S(1)} %get-tuple-element.16), channel_id=1, replica_groups=mesh['slab'=64,'grp'=8] {'slab'}, dimensions={0} | all-to-all | bytes 786432 | tf_op jit(solution)/shard_map/all_to_all | solution.py:134
  61.1 0.0 copy-done
  61.1 1.1 %shard_map.85 = f32[8,1,128]{2,1,0:T(1,128)S(1)} custom-call(s32[1,3]{1,0:T(1,128)S(1)} %get-tuple-element.12.counts_ref, s32[3,1,64]{2,1,0:T(1,128)S(1)} %get-tuple-element.13.rows_ref, s32[3,1,64]{2,1,0:T(1,128)S(1)} %get-tuple-element.14.columns_ref, s32[8,1,128]{2,1,0:T(1,128)S(1)} %get-tuple-element.15.index_ref, ...), custom_call_target="tpu_custom_call" | custom-call | tf_op jit(solution)/shard_map/pallas_call | solution.py:123
  62.3 12.1 %all_to_all.23 = f32[8,1,128]{2,1,0:T(1,128)S(1)} all-to-all(f32[8,1,128]{2,1,0:T(1,128)S(1)} %shard_map.85), channel_id=1, replica_groups=mesh['slab'=64,'grp'=8] {'grp'}, dimensions={0} | all-to-all | bytes 8192 | tf_op jit(solution)/shard_map/all_to_all | solution.py:134
  74.4 0.5 reduce_sum.9
Async XLA Ops:
  0.0 1.0 %copy-start.1 = (bf16[1,128,2048]{2,1,0:T(8,128)(2,1)S(1)}, bf16[1,128,2048]{2,1,0:T(8,128)(2,1)}, u32[]{:S(2)}) copy-start(bf16[1,128,2048]{2,1,0:T(8,128)(2,1)} %echo_ref.1) | copy-start | bytes 1572868
  1.0 0.7 copy-start.2
  1.7 22.6 %copy-start.3 = (s32[1024]{0:T(1024)S(1)}, s32[1024]{0:T(1024)}, u32[]{:S(2)}) copy-start(s32[1024]{0:T(1024)} %param.15) | copy-start | bytes 12292
  1.7 22.6 %copy-start.4 = (s32[1,3,64]{2,0,1:T(1,128)S(1)}, s32[1,3,64]{2,0,1:T(1,128)}, u32[]{:S(2)}) copy-start(s32[1,3,64]{2,0,1:T(1,128)} %param.12) | copy-start | bytes 2308
  1.7 22.6 %copy-start.6 = (s32[3]{0:T(128)S(1)}, s32[3]{0:T(128)}, u32[]{:S(2)}) copy-start(s32[3]{0:T(128)} %acquirer_ref.1) | copy-start | bytes 40
  1.7 41.8 %copy-start.5 = (s32[1,3,64]{2,0,1:T(1,128)S(1)}, s32[1,3,64]{2,0,1:T(1,128)}, u32[]{:S(2)}) copy-start(s32[1,3,64]{2,0,1:T(1,128)} %param.13) | copy-start | bytes 2308
  1.8 41.8 %copy-start.7 = (s32[1,3]{1,0:T(1,128)S(1)}, s32[1,3]{1,0:T(1,128)}, u32[]{:S(2)}) copy-start(s32[1,3]{1,0:T(1,128)} %refs_1_.1) | copy-start | bytes 40
  2.0 59.2 %copy-start = (bf16[1,3,8,128,128]{4,3,2,1,0:T(8,128)(2,1)S(1)}, bf16[1,3,8,128,128]{4,3,2,1,0:T(8,128)(2,1)}, u32[]{:S(2)}) copy-start(bf16[1,3,8,128,128]{4,3,2,1,0:T(8,128)(2,1)} %panels_ref.1) | copy-start | bytes 2359300

commit v6 on v5

v6 whole, which is shorter than its diff:
```python
import jax
import jax.numpy as jnp
from jax import lax
from jax.experimental import pallas as pl
from jax.experimental.pallas import tpu as pltpu
from jax.sharding import PartitionSpec as P

LANES = 128
Z = 2
VMEM = pl.BlockSpec(memory_space=pltpu.VMEM)
SMEM = pl.BlockSpec(memory_space=pltpu.SMEM)
NT = (((1,), (1,)), ((), ()))
PARAMS = pltpu.CompilerParams(vmem_limit_bytes=8 * 1024 * 1024)


def window_sums(apodization, echo):
    windows, channels = apodization.shape
    samples = echo.shape[-1]
    pairs, quarters = samples // (2 * LANES), windows // 4

    def kernel(apod_ref, echo_ref, out_ref):
        apod = apod_ref[...]
        high = apod.astype(jnp.bfloat16)
        rest = apod - high.astype(jnp.float32)
        middle = rest.astype(jnp.bfloat16)
        low = (rest - middle.astype(jnp.float32)).astype(jnp.bfloat16)
        terms = jnp.concatenate([high, middle, low], axis=0)
        sums = jnp.dot(terms, echo_ref[0], preferred_element_type=jnp.float32)
        sums = sums[:windows] + (sums[windows : 2 * windows] + sums[2 * windows :])
        left = lax.broadcasted_iota(jnp.int32, (windows, LANES), 1) < LANES // 2
        for pair in range(pairs):
            first, second = (
                sums[:, (2 * pair + i) * LANES : (2 * pair + i + 1) * LANES] for i in range(2)
            )
            halves = (
                jnp.where(left, first, pltpu.roll(second, LANES // 2, 1)),
                jnp.where(left, pltpu.roll(first, LANES // 2, 1), second),
            )
            for quarter in range(quarters):
                for half in range(2):
                    out_ref[pair * quarters + quarter, half] = halves[half][4 * quarter : 4 * quarter + 4]

    return pl.pallas_call(
        kernel,
        out_shape=jax.ShapeDtypeStruct((pairs * quarters, 2, 4, LANES), jnp.float32),
        in_specs=[VMEM, VMEM],
        out_specs=VMEM,
        compiler_params=PARAMS,
    )(apodization, echo)


def hand_on(refs, count):
    for i in range(count):
        refs[count + 1 + i][...] = refs[i][...]
    return refs[count]


def pick_acquirers(acquirer, pieces, copies, handed):
    transmits = acquirer.shape[0]

    def kernel(acquirer_ref, pieces_ref, *refs):
        out_ref = hand_on(refs, len(handed))
        for transmit in range(transmits):
            for half in range(2):
                picked = pieces_ref[lax.div(acquirer_ref[transmit], Z), half]
                for copy in range(half, copies, 2):
                    out_ref[copy, transmit] = picked

    return pl.pallas_call(
        kernel,
        out_shape=(
            jax.ShapeDtypeStruct((copies, transmits) + pieces.shape[2:], pieces.dtype),
            *(jax.ShapeDtypeStruct(table.shape, table.dtype) for table in handed),
        ),
        in_specs=[SMEM, VMEM] + [VMEM] * len(handed),
        out_specs=(VMEM,) * (1 + len(handed)),
        compiler_params=PARAMS,
    )(acquirer, pieces, *handed)


def sum_and_copy(acquirer, parts, groups, copies, handed):
    transmits = acquirer.shape[0]

    def kernel(acquirer_ref, parts_ref, *refs):
        out_ref = hand_on(refs, len(handed))
        for transmit in range(transmits):
            start = lax.rem(acquirer_ref[transmit], Z) * groups
            total = parts_ref[start, transmit]
            for group in range(1, groups):
                total += parts_ref[start + group, transmit]
            for copy in range(copies):
                out_ref[copy, transmit] = total

    return pl.pallas_call(
        kernel,
        out_shape=(
            jax.ShapeDtypeStruct((copies,) + parts.shape[1:], parts.dtype),
            *(jax.ShapeDtypeStruct(table.shape, table.dtype) for table in handed),
        ),
        in_specs=[SMEM] + [VMEM] * (1 + len(handed)),
        out_specs=(VMEM,) * (1 + len(handed)),
        compiler_params=PARAMS,
    )(acquirer, parts, *handed)


def slot_sums(counts, rows, columns, windows_of_voxels, table, panels, others):
    transmits, slots, block, _ = panels.shape[1:]
    quarters = 4
    row_blocks = windows_of_voxels.shape[0]
    windows = quarters * table.shape[2]
    pairs = table.shape[0] // quarters

    def kernel(
        counts_ref, rows_ref, columns_ref, index_ref, table_ref, panels_ref, others_ref, out_ref, weights, total
    ):
        group = lax.axis_index("grp")
        core = group & 1
        mine = (lax.broadcasted_iota(jnp.int32, (windows, LANES), 1) // (LANES // 2)) == core
        for transmit in range(transmits):
            for pair in range(pairs):
                both = jnp.concatenate(
                    [table_ref[pair * quarters + quarter, transmit] for quarter in range(quarters)], axis=0
                )
                for i, aligned in enumerate((both, pltpu.roll(both, LANES // 2, 1))):
                    aligned = jnp.where(mine, aligned, 0.0)
                    high = aligned.astype(jnp.bfloat16)
                    low = (aligned - high.astype(jnp.float32)).astype(jnp.bfloat16)
                    weights[(transmit * pairs + pair) * 2 + i] = jnp.concatenate([high, low], axis=0)
        total[...] = jnp.zeros_like(total)
        for first, source_ref in ((group * slots, panels_ref), ((group ^ 1) * slots, others_ref)):
            for transmit in range(transmits):
                for slot in range(slots):
                    k = first + slot
                    column = columns_ref[transmit, 0, k]
                    row = jnp.where(k < counts_ref[0, transmit], rows_ref[transmit, 0, k], row_blocks)
                    terms = lax.dot_general(
                        weights[transmit * pairs * 2 + (column ^ core)],
                        source_ref[0, transmit, slot],
                        NT,
                        preferred_element_type=jnp.float32,
                    )
                    total[row] += terms[:windows] + terms[windows:]
        number = lax.broadcasted_iota(jnp.int32, (windows, block), 0)
        for row in range(row_blocks):
            chosen = jnp.where(number == index_ref[row], total[row], 0.0)
            out_ref[row] = jnp.sum(chosen, axis=0, keepdims=True)

    return pl.pallas_call(
        kernel,
        out_shape=jax.ShapeDtypeStruct((row_blocks, 1, block), jnp.float32),
        in_specs=[SMEM, SMEM, SMEM, VMEM, VMEM, VMEM, VMEM],
        out_specs=VMEM,
        scratch_shapes=[
            pltpu.VMEM((transmits * pairs * 2, 2 * windows, LANES), jnp.bfloat16),
            pltpu.VMEM((row_blocks + 1, windows, block), jnp.float32),
        ],
        compiler_params=PARAMS,
    )(counts, rows, columns, windows_of_voxels, table, panels, others)


def exchange(pieces, axis, lines=None):
    return lax.all_to_all(
        pieces, axis, split_axis=0, concat_axis=0, axis_index_groups=lines, tiled=True
    )


def per_device(
    echo_data, acquirer, panels, block_count, block_rows, block_columns, apodization, window_index
):
    slabs, groups = lax.axis_size("slab"), lax.axis_size("grp")
    planes = [list(range(z, slabs, Z)) for z in range(Z)]
    lines = [
        [(chip * Z + z) * groups + group for z in range(Z) for group in range(groups)]
        for chip in range(slabs // Z)
    ]
    rows, columns = (jnp.transpose(x, (1, 0, 2)) for x in (block_rows, block_columns))
    voxels = window_index.reshape(-1, 1, panels.shape[-1])
    sums, given = lax.optimization_barrier((window_sums(apodization, echo_data), panels))
    others = lax.ppermute(given, "grp", [(i, i ^ 1) for i in range(groups)])
    pieces = exchange(sums, "slab", planes)
    picked, rows = pick_acquirers(acquirer, pieces, Z * groups, (rows,))
    parts = exchange(picked, ("slab", "grp"), lines)
    sums, columns, counts = sum_and_copy(acquirer, parts, groups, slabs // Z, (columns, block_count))
    table = exchange(sums, "slab", planes)
    partial = slot_sums(counts, rows, columns, voxels, table, panels, others)
    return jnp.sum(exchange(partial, "grp"), axis=(0, 1))


def solution(mesh):
    return jax.shard_map(
        per_device,
        mesh=mesh,
        in_specs=(
            P("slab", "grp", None),
            P(),
            P("slab", None, "grp", None, None),
            P("slab", None),
            P("slab", None, None),
            P("slab", None, None),
            P(None, "grp"),
            P("slab"),
        ),
        out_specs=P(("slab", "grp")),
        check_vma=False,
    )
```

time: 75.2 us -> 73.5 us (0.977)
  blocking collectives: 70.6 us -> 32 us
  starting transfers between devices: 0 us -> 17.4 us
  waiting for transfers between devices: 0 us -> 16.2 us
  Pallas kernels: 1.94 us -> 4.38 us
  local copies, waits for them, and re-layouts: 1.76 us -> 2.52 us
    all_to_all x4 -> x2, blocking collectives: 70.6 us -> 32 us  [exchange(): lax.all_to_all(pieces, axis, split_axis=0, concat_axis=0, axis_index_grou...]
    all_to_all x0 -> x2, waiting for transfers between devices: none -> 16.2 us  [exchange(): lax.all_to_all(pieces, axis, split_axis=0, concat_axis=0, axis_index_grou...]
    all_to_all x0 -> x2, starting transfers between devices: none -> 14.5 us  [exchange(): lax.all_to_all(pieces, axis, split_axis=0, concat_axis=0, axis_index_grou...]
    ppermute x0 -> x1, starting transfers between devices: none -> 2.86 us  [per_device(): others = lax.ppermute(given, 'grp', [(i, i ^ 1) for i in range(groups)])]
    pallas_call x1, Pallas kernels: 0.06 us -> 1.26 us  [sum_and_copy(): pl.pallas_call(kernel, out_shape=(jax.ShapeDtypeStruct((copies,) + parts....]
    unnamed x16, local copies, waits for them, and re-layouts: 1.76 us -> 2.52 us
  transfers between devices with their start and end apart: 0 -> 3, of which waited for: 0 -> 2; matrix products, arithmetic and copies ran while one was open for 0% -> 0% of each run, Pallas kernels for 0% -> 2%
where the time goes in v6:
time: 73.5 us; the launch traced here: 73.1 us
  blocking collectives  32 us (44%)
  starting transfers between devices  17.4 us (24%)
  waiting for transfers between devices  16.2 us (22%)
  Pallas kernels  4.38 us (6%)
  local copies, waits for them, and re-layouts  2.52 us (3%)
    all_to_all x2, blocking collectives, exchange(): lax.all_to_all(pieces, axis, split_axis=0, concat_axis=0, axis_index_grou...  32 us
    all_to_all x2, waiting for transfers between devices, exchange(): lax.all_to_all(pieces, axis, split_axis=0, concat_axis=0, axis_index_grou...  16.2 us
    all_to_all x2, starting transfers between devices, exchange(): lax.all_to_all(pieces, axis, split_axis=0, concat_axis=0, axis_index_grou...  14.5 us
    ppermute x1, starting transfers between devices, per_device(): others = lax.ppermute(given, 'grp', [(i, i ^ 1) for i in range(groups)])  2.86 us
    unnamed x16, local copies, waits for them, and re-layouts  2.52 us
    pallas_call x1, Pallas kernels, slot_sums(): pl.pallas_call(kernel, out_shape=jax.ShapeDtypeStruct((row_blocks, 1, blo...  1.63 us
  transfers between devices with their start and end apart: 3, of which 2 were waited for; matrix products, arithmetic and copies ran while one was open for 0% of the time, Pallas kernels for 2%

profile of v6, /device:TPU:1, one launch (start us, length us, event | category | flops | bytes accessed | tf_op | source)
XLA Modules:
  0.0 73.1 jit_solution(2240178682502885569)
XLA Ops:
  0.0 0.0 copy-start
  0.0 0.0 copy-start.1
  0.0 1.1 %copy-done.1 = bf16[1,128,2048]{2,1,0:T(8,128)(2,1)S(1)} copy-done((bf16[1,128,2048]{2,1,0:T(8,128)(2,1)S(1)}, bf16[1,128,2048]{2,1,0:T(8,128)(2,1)}, u32[]{:S(2)}) %copy-start.1) | copy-done | bytes 524312
  1.1 0.0 copy-start.2
  1.1 0.7 copy-done.2
  1.8 0.9 %shard_map.82 = f32[32,2,4,128]{3,2,1,0:T(4,128)} custom-call(f32[16,128]{1,0:T(8,128)S(1)} %copy-done.2, bf16[1,128,2048]{2,1,0:T(8,128)(2,1)S(1)} %copy-done.1), custom_call_target="tpu_custom_call" | custom-call | tf_op jit(solution)/shard_map/pallas_call | solution.py:43
  2.8 0.0 copy-start.5
  2.8 10.6 %all-to-all-start = ((f32[32,2,4,128]{3,2,1,0:T(4,128)}), f32[32,2,4,128]{3,2,1,0:T(4,128)S(1)}, u32[]{:S(2)}, u32[]{:S(2)}) async-start(f32[32,2,4,128]{3,2,1,0:T(4,128)} %shard_map.82), calls=%async_computation | async-start | bytes 262144 | tf_op jit(solution)/shard_map/all_to_all | solution.py:162
  13.4 0.0 copy-done
  13.4 0.0 copy-start.4
  13.4 2.9 %collective-permute-start = (bf16[1,3,8,128,128]{4,3,2,1,0:T(8,128)(2,1)S(1)}, bf16[1,3,8,128,128]{4,3,2,1,0:T(8,128)(2,1)S(1)}, u32[]{:S(2)}, u32[]{:S(2)}) collective-permute-start(bf16[1,3,8,128,128]{4,3,2,1,0:T(8,128)(2,1)S(1)} %copy-done), channel_id=1, source_target_pairs={{0,1},{1,0},{2,3},{3,2},{4,5},{5,4},{6,7},{7,6},{8,9},{9,8},{10,11... | collective-permute-start | bytes 2359304 | tf_op jit(solution)/shard_map/ppermute | solution.py:179
  16.3 6.3 %all-to-all-done.pieces_ref = f32[32,2,4,128]{3,2,1,0:T(4,128)S(1)} async-done(((f32[32,2,4,128]{3,2,1,0:T(4,128)}), f32[32,2,4,128]{3,2,1,0:T(4,128)S(1)}, u32[]{:S(2)}, u32[]{:S(2)}) %all-to-all-start) | async-done | bytes 131104 | tf_op jit(solution)/shard_map/all_to_all | solution.py:162
  22.5 0.0 copy-done.5
  22.6 0.0 copy-done.4
  22.6 0.6 shard_map.83
  23.1 0.0 copy-start.7
  23.1 20.7 %all_to_all.20.parts_ref = f32[16,3,4,128]{3,2,1,0:T(4,128)S(1)} all-to-all(f32[16,3,4,128]{3,2,1,0:T(4,128)S(1)} %get-tuple-element.13), channel_id=1, replica_groups={{0,1,2,3,4,5,6,7,8,9,10,11,12,13,14,15},{16,17,18,19,20,21,22,23,24,25,..., dimensions={0} | all-to-all | bytes 196608 | tf_op jit(solution)/shard_map/all_to_all | solution.py:162
  43.8 0.0 copy-start.6
  43.8 0.0 copy-done.7
  43.8 0.7 copy-done.6
  44.5 1.3 %shard_map.84 = (f32[32,3,4,128]{3,2,1,0:T(4,128)}, s32[3,1,64]{2,1,0:T(1,128)S(1)}, s32[1,3]{1,0:T(1,128)S(1)}) custom-call(s32[3]{0:T(128)S(1)} %copy-done.4, f32[16,3,4,128]{3,2,1,0:T(4,128)S(1)} %all_to_all.20.parts_ref, s32[3,1,64]{2,1,0:T(1,128)S(1)} %bitcast.5, s32[1,3]{1,0:T(1,128)S(1)} %copy-done.7), custom_call_target="tpu_custom_call" | custom-call | tf_op jit(solution)/shard_map/pallas_call | solution.py:94
  45.8 3.9 %all-to-all-start.2 = ((f32[32,3,4,128]{3,2,1,0:T(4,128)}), f32[32,3,4,128]{3,2,1,0:T(4,128)S(1)}, u32[]{:S(2)}, u32[]{:S(2)}) async-start(f32[32,3,4,128]{3,2,1,0:T(4,128)} %get-tuple-element.17), calls=%async_computation.2 | async-start | bytes 393216 | tf_op jit(solution)/shard_map/all_to_all | solution.py:162
  49.6 0.0 copy-start.3
  49.6 0.0 collective-permute-done.others_ref
  49.6 9.9 %all-to-all-done.2.table_ref = f32[32,3,4,128]{3,2,1,0:T(4,128)S(1)} async-done(((f32[32,3,4,128]{3,2,1,0:T(4,128)}), f32[32,3,4,128]{3,2,1,0:T(4,128)S(1)}, u32[]{:S(2)}, u32[]{:S(2)}) %all-to-all-start.2) | async-done | bytes 196640 | tf_op jit(solution)/shard_map/all_to_all | solution.py:162
  59.6 0.0 copy-done.3
  59.6 1.6 %shard_map.85 = f32[8,1,128]{2,1,0:T(1,128)S(1)} custom-call(s32[1,3]{1,0:T(1,128)S(1)} %get-tuple-element.14.counts_ref, s32[3,1,64]{2,1,0:T(1,128)S(1)} %get-tuple-element.15.rows_ref, s32[3,1,64]{2,1,0:T(1,128)S(1)} %get-tuple-element.16.columns_ref, s32[8,1,128]{2,1,0:T(1,128)S(1)} %bitcast.3, f32[32,3,4,128]{3,2,1,0:T(4,128)S(1)} %all-to-all-done.2.table_ref, ...), custom_call_target="tpu_custom_call" | custom-call | tf_op jit(solution)/shard_map/pallas_call | solution.py:148
  61.2 11.3 %all_to_all.21 = f32[8,1,128]{2,1,0:T(1,128)S(1)} all-to-all(f32[8,1,128]{2,1,0:T(1,128)S(1)} %shard_map.85), channel_id=1, replica_groups=mesh['slab'=64,'grp'=8] {'grp'}, dimensions={0} | all-to-all | bytes 8192 | tf_op jit(solution)/shard_map/all_to_all | solution.py:162
  72.6 0.5 reduce_sum.9
Async XLA Ops:
  0.0 13.4 %copy-start = (bf16[1,3,8,128,128]{4,3,2,1,0:T(8,128)(2,1)S(1)}, bf16[1,3,8,128,128]{4,3,2,1,0:T(8,128)(2,1)}, u32[]{:S(2)}) copy-start(bf16[1,3,8,128,128]{4,3,2,1,0:T(8,128)(2,1)} %panels_ref.1) | copy-start | bytes 2359300
  0.0 1.1 %copy-start.1 = (bf16[1,128,2048]{2,1,0:T(8,128)(2,1)S(1)}, bf16[1,128,2048]{2,1,0:T(8,128)(2,1)}, u32[]{:S(2)}) copy-start(bf16[1,128,2048]{2,1,0:T(8,128)(2,1)} %echo_ref.1) | copy-start | bytes 1572868
  1.1 0.7 copy-start.2
  2.8 19.8 %copy-start.5 = (s32[1,3,64]{2,0,1:T(1,128)S(1)}, s32[1,3,64]{2,0,1:T(1,128)}, u32[]{:S(2)}) copy-start(s32[1,3,64]{2,0,1:T(1,128)} %param.12) | copy-start | bytes 2308
  2.8 19.8 %all-to-all-start = ((f32[32,2,4,128]{3,2,1,0:T(4,128)}), f32[32,2,4,128]{3,2,1,0:T(4,128)S(1)}, u32[]{:S(2)}, u32[]{:S(2)}) async-start(f32[32,2,4,128]{3,2,1,0:T(4,128)} %shard_map.82), calls=%async_computation | async-start | bytes 262144 | tf_op jit(solution)/shard_map/all_to_all | solution.py:162
  13.4 9.1 %copy-start.4 = (s32[3]{0:T(128)S(1)}, s32[3]{0:T(128)}, u32[]{:S(2)}) copy-start(s32[3]{0:T(128)} %acquirer_ref.3) | copy-start | bytes 40
  13.4 36.2 %collective-permute-start = (bf16[1,3,8,128,128]{4,3,2,1,0:T(8,128)(2,1)S(1)}, bf16[1,3,8,128,128]{4,3,2,1,0:T(8,128)(2,1)S(1)}, u32[]{:S(2)}, u32[]{:S(2)}) collective-permute-start(bf16[1,3,8,128,128]{4,3,2,1,0:T(8,128)(2,1)S(1)} %copy-done), channel_id=1, source_target_pairs={{0,1},{1,0},{2,3},{3,2},{4,5},{5,4},{6,7},{7,6},{8,9},{9,8},{10,11... | collective-permute-start | bytes 2359304 | tf_op jit(solution)/shard_map/ppermute | solution.py:179
  23.1 20.7 %copy-start.7 = (s32[1,3]{1,0:T(1,128)S(1)}, s32[1,3]{1,0:T(1,128)}, u32[]{:S(2)}) copy-start(s32[1,3]{1,0:T(1,128)} %refs_1_.1) | copy-start | bytes 40
  43.8 0.7 copy-start.6
  45.8 13.8 %all-to-all-start.2 = ((f32[32,3,4,128]{3,2,1,0:T(4,128)}), f32[32,3,4,128]{3,2,1,0:T(4,128)S(1)}, u32[]{:S(2)}, u32[]{:S(2)}) async-start(f32[32,3,4,128]{3,2,1,0:T(4,128)} %get-tuple-element.17), calls=%async_computation.2 | async-start | bytes 393216 | tf_op jit(solution)/shard_map/all_to_all | solution.py:162
  49.6 10.0 %copy-start.3 = (s32[1024]{0:T(1024)S(1)}, s32[1024]{0:T(1024)}, u32[]{:S(2)}) copy-start(s32[1024]{0:T(1024)} %param.15) | copy-start | bytes 12292

commit v7 on v6

--- a/solution.py
+++ b/solution.py
@@ -6,6 +6,7 @@
 from jax.sharding import PartitionSpec as P
 
 LANES = 128
+COLUMN_BITS = 4
 Z = 2
 VMEM = pl.BlockSpec(memory_space=pltpu.VMEM)
 SMEM = pl.BlockSpec(memory_space=pltpu.SMEM)
@@ -49,17 +50,10 @@
     )(apodization, echo)
 
 
-def hand_on(refs, count):
-    for i in range(count):
-        refs[count + 1 + i][...] = refs[i][...]
-    return refs[count]
-
-
-def pick_acquirers(acquirer, pieces, copies, handed):
+def pick_acquirers(acquirer, pieces, copies):
     transmits = acquirer.shape[0]
 
-    def kernel(acquirer_ref, pieces_ref, *refs):
-        out_ref = hand_on(refs, len(handed))
+    def kernel(acquirer_ref, pieces_ref, out_ref):
         for transmit in range(transmits):
             for half in range(2):
                 picked = pieces_ref[lax.div(acquirer_ref[transmit], Z), half]
@@ -68,21 +62,17 @@
 
     return pl.pallas_call(
         kernel,
-        out_shape=(
-            jax.ShapeDtypeStruct((copies, transmits) + pieces.shape[2:], pieces.dtype),
-            *(jax.ShapeDtypeStruct(table.shape, table.dtype) for table in handed),
-        ),
-        in_specs=[SMEM, VMEM] + [VMEM] * len(handed),
-        out_specs=(VMEM,) * (1 + len(handed)),
+        out_shape=jax.ShapeDtypeStruct((copies, transmits) + pieces.shape[2:], pieces.dtype),
+        in_specs=[SMEM, VMEM],
+        out_specs=VMEM,
         compiler_params=PARAMS,
-    )(acquirer, pieces, *handed)
+    )(acquirer, pieces)
 
 
-def sum_and_copy(acquirer, parts, groups, copies, handed):
+def sum_and_copy(acquirer, parts, groups, copies):
     transmits = acquirer.shape[0]
 
-    def kernel(acquirer_ref, parts_ref, *refs):
-        out_ref = hand_on(refs, len(handed))
+    def kernel(acquirer_ref, parts_ref, out_ref):
         for transmit in range(transmits):
             start = lax.rem(acquirer_ref[transmit], Z) * groups
             total = parts_ref[start, transmit]
@@ -93,17 +83,14 @@
 
     return pl.pallas_call(
         kernel,
-        out_shape=(
-            jax.ShapeDtypeStruct((copies,) + parts.shape[1:], parts.dtype),
-            *(jax.ShapeDtypeStruct(table.shape, table.dtype) for table in handed),
-        ),
-        in_specs=[SMEM] + [VMEM] * (1 + len(handed)),
-        out_specs=(VMEM,) * (1 + len(handed)),
+        out_shape=jax.ShapeDtypeStruct((copies,) + parts.shape[1:], parts.dtype),
+        in_specs=[SMEM, VMEM],
+        out_specs=VMEM,
         compiler_params=PARAMS,
-    )(acquirer, parts, *handed)
+    )(acquirer, parts)
 
 
-def slot_sums(counts, rows, columns, windows_of_voxels, table, panels, others):
+def slot_sums(slot_table, windows_of_voxels, table, panels, others):
     transmits, slots, block, _ = panels.shape[1:]
     quarters = 4
     row_blocks = windows_of_voxels.shape[0]
@@ -111,7 +98,7 @@
     pairs = table.shape[0] // quarters
 
     def kernel(
-        counts_ref, rows_ref, columns_ref, index_ref, table_ref, panels_ref, others_ref, out_ref, weights, total
+        slots_ref, index_ref, table_ref, panels_ref, others_ref, out_ref, weights, total
     ):
         group = lax.axis_index("grp")
         core = group & 1
@@ -130,9 +117,8 @@
         for first, source_ref in ((group * slots, panels_ref), ((group ^ 1) * slots, others_ref)):
             for transmit in range(transmits):
                 for slot in range(slots):
-                    k = first + slot
-                    column = columns_ref[transmit, 0, k]
-                    row = jnp.where(k < counts_ref[0, transmit], rows_ref[transmit, 0, k], row_blocks)
+                    packed = slots_ref[transmit, 0, first + slot]
+                    row, column = packed >> COLUMN_BITS, packed & ((1 << COLUMN_BITS) - 1)
                     terms = lax.dot_general(
                         weights[transmit * pairs * 2 + (column ^ core)],
                         source_ref[0, transmit, slot],
@@ -148,14 +134,14 @@
     return pl.pallas_call(
         kernel,
         out_shape=jax.ShapeDtypeStruct((row_blocks, 1, block), jnp.float32),
-        in_specs=[SMEM, SMEM, SMEM, VMEM, VMEM, VMEM, VMEM],
+        in_specs=[SMEM, VMEM, VMEM, VMEM, VMEM],
         out_specs=VMEM,
         scratch_shapes=[
             pltpu.VMEM((transmits * pairs * 2, 2 * windows, LANES), jnp.bfloat16),
             pltpu.VMEM((row_blocks + 1, windows, block), jnp.float32),
         ],
         compiler_params=PARAMS,
-    )(counts, rows, columns, windows_of_voxels, table, panels, others)
+    )(slot_table, windows_of_voxels, table, panels, others)
 
 
 def exchange(pieces, axis, lines=None):
@@ -173,16 +159,17 @@
         [(chip * Z + z) * groups + group for z in range(Z) for group in range(groups)]
         for chip in range(slabs // Z)
     ]
-    rows, columns = (jnp.transpose(x, (1, 0, 2)) for x in (block_rows, block_columns))
     voxels = window_index.reshape(-1, 1, panels.shape[-1])
+    live = jnp.arange(block_rows.shape[2], dtype=jnp.int32) < block_count[:, :, None]
+    slot_table = (jnp.where(live, block_rows, voxels.shape[0]) << COLUMN_BITS) | block_columns
+    slot_table = jnp.transpose(slot_table, (1, 0, 2))
     sums, given = lax.optimization_barrier((window_sums(apodization, echo_data), panels))
     others = lax.ppermute(given, "grp", [(i, i ^ 1) for i in range(groups)])
     pieces = exchange(sums, "slab", planes)
-    picked, rows = pick_acquirers(acquirer, pieces, Z * groups, (rows,))
+    picked = pick_acquirers(acquirer, pieces, Z * groups)
     parts = exchange(picked, ("slab", "grp"), lines)
-    sums, columns, counts = sum_and_copy(acquirer, parts, groups, slabs // Z, (columns, block_count))
-    table = exchange(sums, "slab", planes)
-    partial = slot_sums(counts, rows, columns, voxels, table, panels, others)
+    table = exchange(sum_and_copy(acquirer, parts, groups, slabs // Z), "slab", planes)
+    partial = slot_sums(slot_table, voxels, table, panels, others)
     return jnp.sum(exchange(partial, "grp"), axis=(0, 1))
 
 

time: 73.5 us -> 72.9 us (level)
  transfers between devices with their start and end apart: 3 -> 3, of which waited for: 2 -> 2; matrix products, arithmetic and copies ran while one was open for 0% -> 0% of each run, Pallas kernels for 2% -> 3%
where the time goes in v7:
time: 72.9 us; the launch traced here: 72.6 us
  blocking collectives  32 us (44%)
  starting transfers between devices  17.5 us (24%)
  waiting for transfers between devices  16.1 us (22%)
  Pallas kernels  4.37 us (6%)
  local copies, waits for them, and re-layouts  1.84 us (3%)
    all_to_all x2, blocking collectives, exchange(): lax.all_to_all(pieces, axis, split_axis=0, concat_axis=0, axis_index_grou...  32 us
    all_to_all x2, waiting for transfers between devices, exchange(): lax.all_to_all(pieces, axis, split_axis=0, concat_axis=0, axis_index_grou...  16.1 us
    all_to_all x2, starting transfers between devices, exchange(): lax.all_to_all(pieces, axis, split_axis=0, concat_axis=0, axis_index_grou...  14.6 us
    ppermute x1, starting transfers between devices, per_device(): others = lax.ppermute(given, 'grp', [(i, i ^ 1) for i in range(groups)])  2.86 us
    unnamed x16, local copies, waits for them, and re-layouts  1.84 us
    pallas_call x1, Pallas kernels, slot_sums(): pl.pallas_call(kernel, out_shape=jax.ShapeDtypeStruct((row_blocks, 1, blo...  1.62 us
  transfers between devices with their start and end apart: 3, of which 2 were waited for; matrix products, arithmetic and copies ran while one was open for 0% of the time, Pallas kernels for 3%

profile of v7, /device:TPU:1, one launch (start us, length us, event | category | flops | bytes accessed | tf_op | source)
XLA Modules:
  0.0 72.6 jit_solution(3232509669513579668)
XLA Ops:
  0.0 0.0 copy-start
  0.0 0.0 copy-start.1
  0.0 1.1 %copy-done.1 = bf16[1,128,2048]{2,1,0:T(8,128)(2,1)S(1)} copy-done((bf16[1,128,2048]{2,1,0:T(8,128)(2,1)S(1)}, bf16[1,128,2048]{2,1,0:T(8,128)(2,1)}, u32[]{:S(2)}) %copy-start.1) | copy-done | bytes 524312
  1.1 0.0 copy-start.2
  1.1 0.7 copy-done.2
  1.8 0.9 %shard_map.85 = f32[32,2,4,128]{3,2,1,0:T(4,128)} custom-call(f32[16,128]{1,0:T(8,128)S(1)} %copy-done.2, bf16[1,128,2048]{2,1,0:T(8,128)(2,1)S(1)} %copy-done.1), custom_call_target="tpu_custom_call" | custom-call | tf_op jit(solution)/shard_map/pallas_call | solution.py:44
  2.7 0.0 copy-start.4
  2.7 10.6 %all-to-all-start = ((f32[32,2,4,128]{3,2,1,0:T(4,128)}), f32[32,2,4,128]{3,2,1,0:T(4,128)S(1)}, u32[]{:S(2)}, u32[]{:S(2)}) async-start(f32[32,2,4,128]{3,2,1,0:T(4,128)} %shard_map.85), calls=%async_computation | async-start | bytes 262144 | tf_op jit(solution)/shard_map/all_to_all | solution.py:148
  13.4 0.0 copy-done
  13.4 2.9 %collective-permute-start = (bf16[1,3,8,128,128]{4,3,2,1,0:T(8,128)(2,1)S(1)}, bf16[1,3,8,128,128]{4,3,2,1,0:T(8,128)(2,1)S(1)}, u32[]{:S(2)}, u32[]{:S(2)}) collective-permute-start(bf16[1,3,8,128,128]{4,3,2,1,0:T(8,128)(2,1)S(1)} %copy-done), channel_id=1, source_target_pairs={{0,1},{1,0},{2,3},{3,2},{4,5},{5,4},{6,7},{7,6},{8,9},{9,8},{10,11... | collective-permute-start | bytes 2359304 | tf_op jit(solution)/shard_map/ppermute | solution.py:167
  16.3 6.3 %all-to-all-done.pieces_ref = f32[32,2,4,128]{3,2,1,0:T(4,128)S(1)} async-done(((f32[32,2,4,128]{3,2,1,0:T(4,128)}), f32[32,2,4,128]{3,2,1,0:T(4,128)S(1)}, u32[]{:S(2)}, u32[]{:S(2)}) %all-to-all-start) | async-done | bytes 131104 | tf_op jit(solution)/shard_map/all_to_all | solution.py:148
  22.5 0.0 copy-done.4
  22.5 0.6 shard_map.86
  23.1 20.7 %all_to_all.20.parts_ref = f32[16,3,4,128]{3,2,1,0:T(4,128)S(1)} all-to-all(f32[16,3,4,128]{3,2,1,0:T(4,128)S(1)} %shard_map.86), channel_id=1, replica_groups={{0,1,2,3,4,5,6,7,8,9,10,11,12,13,14,15},{16,17,18,19,20,21,22,23,24,25,..., dimensions={0} | all-to-all | bytes 196608 | tf_op jit(solution)/shard_map/all_to_all | solution.py:148
  43.8 1.3 %shard_map.87 = f32[32,3,4,128]{3,2,1,0:T(4,128)} custom-call(s32[3]{0:T(128)S(1)} %copy-done.4, f32[16,3,4,128]{3,2,1,0:T(4,128)S(1)} %all_to_all.20.parts_ref), custom_call_target="tpu_custom_call" | custom-call | tf_op jit(solution)/shard_map/pallas_call | solution.py:84
  45.0 0.0 copy-start.5
  45.0 0.0 copy-start.6
  45.1 0.0 copy-start.7
  45.1 4.0 %all-to-all-start.2 = ((f32[32,3,4,128]{3,2,1,0:T(4,128)}), f32[32,3,4,128]{3,2,1,0:T(4,128)S(1)}, u32[]{:S(2)}, u32[]{:S(2)}) async-start(f32[32,3,4,128]{3,2,1,0:T(4,128)} %shard_map.87), calls=%async_computation.2 | async-start | bytes 393216 | tf_op jit(solution)/shard_map/all_to_all | solution.py:148
  49.1 0.0 copy-start.3
  49.1 0.0 copy-done.5
  49.1 0.0 copy-done.6
  49.1 0.0 copy-done.7
  49.1 0.1 fusion.2.slots_ref
  49.2 0.0 collective-permute-done.others_ref
  49.2 9.8 %all-to-all-done.2.table_ref = f32[32,3,4,128]{3,2,1,0:T(4,128)S(1)} async-done(((f32[32,3,4,128]{3,2,1,0:T(4,128)}), f32[32,3,4,128]{3,2,1,0:T(4,128)S(1)}, u32[]{:S(2)}, u32[]{:S(2)}) %all-to-all-start.2) | async-done | bytes 196640 | tf_op jit(solution)/shard_map/all_to_all | solution.py:148
  59.0 0.0 copy-done.3
  59.0 1.6 %shard_map.88 = f32[8,1,128]{2,1,0:T(1,128)S(1)} custom-call(s32[3,1,64]{2,1,0:T(1,128)S(1)} %fusion.2.slots_ref, s32[8,1,128]{2,1,0:T(1,128)S(1)} %bitcast.4, f32[32,3,4,128]{3,2,1,0:T(4,128)S(1)} %all-to-all-done.2.table_ref, bf16[1,3,8,128,128]{4,3,2,1,0:T(8,128)(2,1)S(1)} %copy-done, bf16[1,3,8,128,128]{4,3,2,1,0:T(8,128)(2,1)S(1)} %collective-permute-done.others_ref), custom_call_target="tpu_custom_call" | custom-call | tf_op jit(solution)/shard_map/pallas_call | solution.py:134
  60.6 11.4 %all_to_all.21 = f32[8,1,128]{2,1,0:T(1,128)S(1)} all-to-all(f32[8,1,128]{2,1,0:T(1,128)S(1)} %shard_map.88), channel_id=1, replica_groups=mesh['slab'=64,'grp'=8] {'grp'}, dimensions={0} | all-to-all | bytes 8192 | tf_op jit(solution)/shard_map/all_to_all | solution.py:148
  72.0 0.5 reduce_sum.9
Async XLA Ops:
  0.0 13.4 %copy-start = (bf16[1,3,8,128,128]{4,3,2,1,0:T(8,128)(2,1)S(1)}, bf16[1,3,8,128,128]{4,3,2,1,0:T(8,128)(2,1)}, u32[]{:S(2)}) copy-start(bf16[1,3,8,128,128]{4,3,2,1,0:T(8,128)(2,1)} %panels_ref.1) | copy-start | bytes 2359300
  0.0 1.1 %copy-start.1 = (bf16[1,128,2048]{2,1,0:T(8,128)(2,1)S(1)}, bf16[1,128,2048]{2,1,0:T(8,128)(2,1)}, u32[]{:S(2)}) copy-start(bf16[1,128,2048]{2,1,0:T(8,128)(2,1)} %echo_ref.1) | copy-start | bytes 1572868
  1.1 0.7 copy-start.2
  2.7 19.8 %copy-start.4 = (s32[3]{0:T(128)S(1)}, s32[3]{0:T(128)}, u32[]{:S(2)}) copy-start(s32[3]{0:T(128)} %acquirer_ref.3) | copy-start | bytes 40
  2.7 19.8 %all-to-all-start = ((f32[32,2,4,128]{3,2,1,0:T(4,128)}), f32[32,2,4,128]{3,2,1,0:T(4,128)S(1)}, u32[]{:S(2)}, u32[]{:S(2)}) async-start(f32[32,2,4,128]{3,2,1,0:T(4,128)} %shard_map.85), calls=%async_computation | async-start | bytes 262144 | tf_op jit(solution)/shard_map/all_to_all | solution.py:148
  13.4 35.8 %collective-permute-start = (bf16[1,3,8,128,128]{4,3,2,1,0:T(8,128)(2,1)S(1)}, bf16[1,3,8,128,128]{4,3,2,1,0:T(8,128)(2,1)S(1)}, u32[]{:S(2)}, u32[]{:S(2)}) collective-permute-start(bf16[1,3,8,128,128]{4,3,2,1,0:T(8,128)(2,1)S(1)} %copy-done), channel_id=1, source_target_pairs={{0,1},{1,0},{2,3},{3,2},{4,5},{5,4},{6,7},{7,6},{8,9},{9,8},{10,11... | collective-permute-start | bytes 2359304 | tf_op jit(solution)/shard_map/ppermute | solution.py:167
  45.0 4.0 %copy-start.5 = (s32[1,3,64]{2,0,1:T(1,128)S(1)}, s32[1,3,64]{2,0,1:T(1,128)}, u32[]{:S(2)}) copy-start(s32[1,3,64]{2,0,1:T(1,128)} %param.13) | copy-start | bytes 2308
  45.0 4.0 %copy-start.6 = (s32[1,3,64]{2,0,1:T(1,128)S(1)}, s32[1,3,64]{2,0,1:T(1,128)}, u32[]{:S(2)}) copy-start(s32[1,3,64]{2,0,1:T(1,128)} %param.12) | copy-start | bytes 2308
  45.1 4.0 %copy-start.7 = (s32[1,3]{1,0:T(1,128)S(1)}, s32[1,3]{1,0:T(1,128)}, u32[]{:S(2)}) copy-start(s32[1,3]{1,0:T(1,128)} %param.11) | copy-start | bytes 40
  45.1 14.0 %all-to-all-start.2 = ((f32[32,3,4,128]{3,2,1,0:T(4,128)}), f32[32,3,4,128]{3,2,1,0:T(4,128)S(1)}, u32[]{:S(2)}, u32[]{:S(2)}) async-start(f32[32,3,4,128]{3,2,1,0:T(4,128)} %shard_map.87), calls=%async_computation.2 | async-start | bytes 393216 | tf_op jit(solution)/shard_map/all_to_all | solution.py:148
  49.1 10.0 %copy-start.3 = (s32[1024]{0:T(1024)S(1)}, s32[1024]{0:T(1024)}, u32[]{:S(2)}) copy-start(s32[1024]{0:T(1024)} %param.15) | copy-start | bytes 12292

commit v8 on v7

--- a/solution.py
+++ b/solution.py
@@ -12,6 +12,19 @@
 SMEM = pl.BlockSpec(memory_space=pltpu.SMEM)
 NT = (((1,), (1,)), ((), ()))
 PARAMS = pltpu.CompilerParams(vmem_limit_bytes=8 * 1024 * 1024)
+
+
+def empty_sums(row_blocks, windows, block):
+    def kernel(out_ref):
+        out_ref[...] = jnp.zeros_like(out_ref)
+
+    return pl.pallas_call(
+        kernel,
+        out_shape=jax.ShapeDtypeStruct((row_blocks + 1, windows, block), jnp.float32),
+        out_specs=VMEM,
+        compiler_params=PARAMS,
+        cost_estimate=pl.CostEstimate(flops=200000000, bytes_accessed=0, transcendentals=0),
+    )()
 
 
 def window_sums(apodization, echo):
@@ -50,10 +63,14 @@
     )(apodization, echo)
 
 
-def pick_acquirers(acquirer, pieces, copies):
+def pick_acquirers(acquirer, pieces, copies, counts, rows, columns, row_blocks):
     transmits = acquirer.shape[0]
 
-    def kernel(acquirer_ref, pieces_ref, out_ref):
+    def kernel(acquirer_ref, pieces_ref, counts_ref, rows_ref, columns_ref, out_ref, slots_ref):
+        place = lax.broadcasted_iota(jnp.int32, rows.shape[1:], 1)
+        for transmit in range(transmits):
+            row = jnp.where(place < counts_ref[0, transmit], rows_ref[transmit], row_blocks)
+            slots_ref[transmit] = (row << COLUMN_BITS) | columns_ref[transmit]
         for transmit in range(transmits):
             for half in range(2):
                 picked = pieces_ref[lax.div(acquirer_ref[transmit], Z), half]
@@ -62,11 +79,14 @@
 
     return pl.pallas_call(
         kernel,
-        out_shape=jax.ShapeDtypeStruct((copies, transmits) + pieces.shape[2:], pieces.dtype),
-        in_specs=[SMEM, VMEM],
-        out_specs=VMEM,
-        compiler_params=PARAMS,
-    )(acquirer, pieces)
+        out_shape=(
+            jax.ShapeDtypeStruct((copies, transmits) + pieces.shape[2:], pieces.dtype),
+            jax.ShapeDtypeStruct(rows.shape, jnp.int32),
+        ),
+        in_specs=[SMEM, VMEM, SMEM, VMEM, VMEM],
+        out_specs=(VMEM, VMEM),
+        compiler_params=PARAMS,
+    )(acquirer, pieces, counts, rows, columns)
 
 
 def sum_and_copy(acquirer, parts, groups, copies):
@@ -90,7 +110,7 @@
     )(acquirer, parts)
 
 
-def slot_sums(slot_table, windows_of_voxels, table, panels, others):
+def slot_sums(slot_table, windows_of_voxels, empty, table, panels, others):
     transmits, slots, block, _ = panels.shape[1:]
     quarters = 4
     row_blocks = windows_of_voxels.shape[0]
@@ -98,7 +118,7 @@
     pairs = table.shape[0] // quarters
 
     def kernel(
-        slots_ref, index_ref, table_ref, panels_ref, others_ref, out_ref, weights, total
+        slots_ref, index_ref, empty_ref, table_ref, panels_ref, others_ref, out_ref, weights, total
     ):
         group = lax.axis_index("grp")
         core = group & 1
@@ -113,7 +133,7 @@
                     high = aligned.astype(jnp.bfloat16)
                     low = (aligned - high.astype(jnp.float32)).astype(jnp.bfloat16)
                     weights[(transmit * pairs + pair) * 2 + i] = jnp.concatenate([high, low], axis=0)
-        total[...] = jnp.zeros_like(total)
+        total[...] = empty_ref[...]
         for first, source_ref in ((group * slots, panels_ref), ((group ^ 1) * slots, others_ref)):
             for transmit in range(transmits):
                 for slot in range(slots):
@@ -134,14 +154,14 @@
     return pl.pallas_call(
         kernel,
         out_shape=jax.ShapeDtypeStruct((row_blocks, 1, block), jnp.float32),
-        in_specs=[SMEM, VMEM, VMEM, VMEM, VMEM],
+        in_specs=[SMEM, VMEM, VMEM, VMEM, VMEM, VMEM],
         out_specs=VMEM,
         scratch_shapes=[
             pltpu.VMEM((transmits * pairs * 2, 2 * windows, LANES), jnp.bfloat16),
-            pltpu.VMEM((row_blocks + 1, windows, block), jnp.float32),
+            pltpu.VMEM(empty.shape, empty.dtype),
         ],
         compiler_params=PARAMS,
-    )(slot_table, windows_of_voxels, table, panels, others)
+    )(slot_table, windows_of_voxels, empty, table, panels, others)
 
 
 def exchange(pieces, axis, lines=None):
@@ -160,16 +180,20 @@
         for chip in range(slabs // Z)
     ]
     voxels = window_index.reshape(-1, 1, panels.shape[-1])
-    live = jnp.arange(block_rows.shape[2], dtype=jnp.int32) < block_count[:, :, None]
-    slot_table = (jnp.where(live, block_rows, voxels.shape[0]) << COLUMN_BITS) | block_columns
-    slot_table = jnp.transpose(slot_table, (1, 0, 2))
-    sums, given = lax.optimization_barrier((window_sums(apodization, echo_data), panels))
+    rows, columns = (jnp.transpose(v, (1, 0, 2)) for v in (block_rows, block_columns))
+    empty = empty_sums(voxels.shape[0], apodization.shape[0], voxels.shape[2])
+    empty, given, apodization, echo_data = lax.optimization_barrier(
+        (empty, panels, apodization, echo_data)
+    )
     others = lax.ppermute(given, "grp", [(i, i ^ 1) for i in range(groups)])
-    pieces = exchange(sums, "slab", planes)
-    picked = pick_acquirers(acquirer, pieces, Z * groups)
+    pieces = exchange(window_sums(apodization, echo_data), "slab", planes)
+    picked, slot_table = pick_acquirers(
+        acquirer, pieces, Z * groups, block_count, rows, columns, voxels.shape[0]
+    )
+    picked, others = lax.optimization_barrier((picked, others))
     parts = exchange(picked, ("slab", "grp"), lines)
     table = exchange(sum_and_copy(acquirer, parts, groups, slabs // Z), "slab", planes)
-    partial = slot_sums(slot_table, voxels, table, panels, others)
+    partial = slot_sums(slot_table, voxels, empty, table, panels, others)
     return jnp.sum(exchange(partial, "grp"), axis=(0, 1))
 
 

time: 72.9 us -> 71.9 us (0.986)
  blocking collectives: 32 us -> 58.9 us
  waiting for transfers between devices: 16.1 us -> 0.01 us
  starting transfers between devices: 17.5 us -> 8.92 us
  local copies, waits for them, and re-layouts: 1.84 us -> 0.05 us
  Pallas kernels: 4.37 us -> 3.06 us
    all_to_all x2 -> x4, blocking collectives: 32 us -> 58.9 us  [exchange(): lax.all_to_all(pieces, axis, split_axis=0, concat_axis=0, axis_index_grou...]
    all_to_all x2 -> x0, waiting for transfers between devices: 16.1 us -> none  [exchange(): lax.all_to_all(pieces, axis, split_axis=0, concat_axis=0, axis_index_grou...]
    all_to_all x2 -> x0, starting transfers between devices: 14.6 us -> none  [exchange(): lax.all_to_all(pieces, axis, split_axis=0, concat_axis=0, axis_index_grou...]
    ppermute x1, starting transfers between devices: 2.86 us -> 8.92 us  [per_device(): others = lax.ppermute(given, 'grp', [(i, i ^ 1) for i in range(groups)])]
    unnamed x16, local copies, waits for them, and re-layouts: 1.84 us -> 0.05 us
  transfers between devices with their start and end apart: 3 -> 1, of which waited for: 2 -> 0; matrix products, arithmetic and copies ran while one was open for 0% -> 0% of each run, Pallas kernels for 3% -> 1%
where the time goes in v8:
time: 71.9 us; the launch traced here: 71.6 us
  blocking collectives  58.9 us (82%)
  starting transfers between devices  8.92 us (12%)
  Pallas kernels  3.06 us (4%)
    all_to_all x4, blocking collectives, exchange(): lax.all_to_all(pieces, axis, split_axis=0, concat_axis=0, axis_index_grou...  58.9 us
    ppermute x1, starting transfers between devices, per_device(): others = lax.ppermute(given, 'grp', [(i, i ^ 1) for i in range(groups)])  8.92 us
    pallas_call x1, Pallas kernels, slot_sums(): pl.pallas_call(kernel, out_shape=jax.ShapeDtypeStruct((row_blocks, 1, blo...  1.62 us
  transfers between devices with their start and end apart: 1, of which 0 were waited for; matrix products, arithmetic and copies ran while one was open for 0% of the time, Pallas kernels for 1%

profile of v8, /device:TPU:1, one launch (start us, length us, event | category | flops | bytes accessed | tf_op | source)
XLA Modules:
  0.0 71.6 jit_solution(3081217628348863552)
XLA Ops:
  0.0 0.0 copy-start.2
  0.0 0.0 copy-start.1
  0.0 8.9 %collective-permute-start = (bf16[1,3,8,128,128]{4,3,2,1,0:T(8,128)(2,1)}, bf16[1,3,8,128,128]{4,3,2,1,0:T(8,128)(2,1)S(1)}, u32[]{:S(2)}, u32[]{:S(2)}) collective-permute-start(bf16[1,3,8,128,128]{4,3,2,1,0:T(8,128)(2,1)} %panels_ref.1), channel_id=1, source_target_pairs={{0,1},{1,0},{2,3},{3,2},{4,5},{5,4},{6,7},{7,6},{8,9},{9,8},{10,11... | collective-permute-start | bytes 2359304 | tf_op jit(solution)/shard_map/ppermute | solution.py:188
  8.9 0.0 copy-done.2
  9.0 0.0 copy-done.1
  9.0 0.0 copy-start.4
  9.0 0.0 copy-start.5
  9.0 0.0 copy-start.6
  9.0 0.0 copy-start.7
  9.0 0.3 shard_map.83
  9.3 0.0 copy-start
  9.3 13.4 %all_to_all.20.pieces_ref = f32[32,2,4,128]{3,2,1,0:T(4,128)S(1)} all-to-all(f32[32,2,4,128]{3,2,1,0:T(4,128)S(1)} %shard_map.83), channel_id=1, replica_groups={{0,16,32,48,64,80,96,112,128,144,160,176,192,208,224,240,256,272,288,30..., dimensions={0} | all-to-all | bytes 262144 | tf_op jit(solution)/shard_map/all_to_all | solution.py:168
  22.7 0.0 copy-done.4
  22.7 0.0 copy-done.5
  22.7 0.0 copy-done.6
  22.7 0.0 copy-done.7
  22.7 0.6 shard_map.84
  23.3 0.0 collective-permute-done.others_ref
  23.3 20.7 %all_to_all.21.parts_ref = f32[16,3,4,128]{3,2,1,0:T(4,128)S(1)} all-to-all(f32[16,3,4,128]{3,2,1,0:T(4,128)S(1)} %get-tuple-element.19), channel_id=1, replica_groups={{0,1,2,3,4,5,6,7,8,9,10,11,12,13,14,15},{16,17,18,19,20,21,22,23,24,25,..., dimensions={0} | all-to-all | bytes 196608 | tf_op jit(solution)/shard_map/all_to_all | solution.py:168
  44.0 0.6 shard_map.85
  44.6 0.0 copy-start.3
  44.6 13.1 %all_to_all.22.table_ref = f32[32,3,4,128]{3,2,1,0:T(4,128)S(1)} all-to-all(f32[32,3,4,128]{3,2,1,0:T(4,128)S(1)} %shard_map.85), channel_id=1, replica_groups={{0,16,32,48,64,80,96,112,128,144,160,176,192,208,224,240,256,272,288,30..., dimensions={0} | all-to-all | bytes 393216 | tf_op jit(solution)/shard_map/all_to_all | solution.py:168
  57.7 0.0 copy-done
  57.7 0.0 copy-done.3
  57.7 1.6 %shard_map.86 = f32[8,1,128]{2,1,0:T(1,128)S(1)} custom-call(s32[3,1,64]{2,1,0:T(1,128)S(1)} %get-tuple-element.15.slots_ref, s32[8,1,128]{2,1,0:T(1,128)S(1)} %bitcast.3, f32[9,16,128]{2,1,0:T(8,128)S(1)} %shard_map.82.empty_ref, f32[32,3,4,128]{3,2,1,0:T(4,128)S(1)} %all_to_all.22.table_ref, bf16[1,3,8,128,128]{4,3,2,1,0:T(8,128)(2,1)S(1)} %copy-done, ...), custom_call_target="tpu_custom_call" | custom-call | tf_op jit(solution)/shard_map/pallas_call | solution.py:154
  59.3 11.8 %all_to_all.23 = f32[8,1,128]{2,1,0:T(1,128)S(1)} all-to-all(f32[8,1,128]{2,1,0:T(1,128)S(1)} %shard_map.86), channel_id=1, replica_groups=mesh['slab'=64,'grp'=8] {'grp'}, dimensions={0} | all-to-all | bytes 8192 | tf_op jit(solution)/shard_map/all_to_all | solution.py:168
  71.1 0.5 reduce_sum.9
  (1 shorter events, 0.0 us)
Async XLA Ops:
  0.0 8.9 %copy-start.2 = (f32[16,128]{1,0:T(8,128)S(1)}, f32[16,128]{1,0:T(8,128)}, u32[]{:S(2)}) copy-start(f32[16,128]{1,0:T(8,128)} %apod_ref) | copy-start | bytes 24580
  0.0 9.0 %copy-start.1 = (bf16[1,128,2048]{2,1,0:T(8,128)(2,1)S(1)}, bf16[1,128,2048]{2,1,0:T(8,128)(2,1)}, u32[]{:S(2)}) copy-start(bf16[1,128,2048]{2,1,0:T(8,128)(2,1)} %echo_ref) | copy-start | bytes 1572868
  0.0 23.3 %collective-permute-start = (bf16[1,3,8,128,128]{4,3,2,1,0:T(8,128)(2,1)}, bf16[1,3,8,128,128]{4,3,2,1,0:T(8,128)(2,1)S(1)}, u32[]{:S(2)}, u32[]{:S(2)}) collective-permute-start(bf16[1,3,8,128,128]{4,3,2,1,0:T(8,128)(2,1)} %panels_ref.1), channel_id=1, source_target_pairs={{0,1},{1,0},{2,3},{3,2},{4,5},{5,4},{6,7},{7,6},{8,9},{9,8},{10,11... | collective-permute-start | bytes 2359304 | tf_op jit(solution)/shard_map/ppermute | solution.py:188
  9.0 13.7 %copy-start.4 = (s32[3]{0:T(128)S(1)}, s32[3]{0:T(128)}, u32[]{:S(2)}) copy-start(s32[3]{0:T(128)} %acquirer_ref.3) | copy-start | bytes 40
  9.0 13.7 %copy-start.5 = (s32[1,3,64]{2,0,1:T(1,128)S(1)}, s32[1,3,64]{2,0,1:T(1,128)}, u32[]{:S(2)}) copy-start(s32[1,3,64]{2,0,1:T(1,128)} %param.12) | copy-start | bytes 2308
  9.0 13.7 %copy-start.6 = (s32[1,3,64]{2,0,1:T(1,128)S(1)}, s32[1,3,64]{2,0,1:T(1,128)}, u32[]{:S(2)}) copy-start(s32[1,3,64]{2,0,1:T(1,128)} %param.13) | copy-start | bytes 2308
  9.0 13.7 %copy-start.7 = (s32[1,3]{1,0:T(1,128)S(1)}, s32[1,3]{1,0:T(1,128)}, u32[]{:S(2)}) copy-start(s32[1,3]{1,0:T(1,128)} %counts_ref.1) | copy-start | bytes 40
  9.3 48.4 %copy-start = (bf16[1,3,8,128,128]{4,3,2,1,0:T(8,128)(2,1)S(1)}, bf16[1,3,8,128,128]{4,3,2,1,0:T(8,128)(2,1)}, u32[]{:S(2)}) copy-start(bf16[1,3,8,128,128]{4,3,2,1,0:T(8,128)(2,1)} %panels_ref.1) | copy-start | bytes 2359300
  44.6 13.1 %copy-start.3 = (s32[1024]{0:T(1024)S(1)}, s32[1024]{0:T(1024)}, u32[]{:S(2)}) copy-start(s32[1024]{0:T(1024)} %param.15) | copy-start | bytes 12292

commit v9 on v8

--- a/solution.py
+++ b/solution.py
@@ -64,47 +64,56 @@
 
 
 def pick_acquirers(acquirer, pieces, copies, counts, rows, columns, row_blocks):
-    transmits = acquirer.shape[0]
+    transmits = acquirer.shape[1]
+    tile = pieces.shape[2:]
 
     def kernel(acquirer_ref, pieces_ref, counts_ref, rows_ref, columns_ref, out_ref, slots_ref):
         place = lax.broadcasted_iota(jnp.int32, rows.shape[1:], 1)
         for transmit in range(transmits):
-            row = jnp.where(place < counts_ref[0, transmit], rows_ref[transmit], row_blocks)
+            count = jnp.broadcast_to(counts_ref[:, transmit : transmit + 1], place.shape)
+            row = jnp.where(place < count, rows_ref[transmit], row_blocks)
             slots_ref[transmit] = (row << COLUMN_BITS) | columns_ref[transmit]
-        for transmit in range(transmits):
-            for half in range(2):
-                picked = pieces_ref[lax.div(acquirer_ref[transmit], Z), half]
-                for copy in range(half, copies, 2):
-                    out_ref[copy, transmit] = picked
+            chip = jnp.broadcast_to(acquirer_ref[:, transmit : transmit + 1], tile) // Z
+            picked = [jnp.zeros(tile, jnp.float32)] * 2
+            for source in range(pieces.shape[0]):
+                picked = [
+                    jnp.where(chip == source, pieces_ref[source, half], picked[half]) for half in range(2)
+                ]
+            for copy in range(copies):
+                out_ref[copy, transmit] = picked[copy % 2]
 
     return pl.pallas_call(
         kernel,
         out_shape=(
-            jax.ShapeDtypeStruct((copies, transmits) + pieces.shape[2:], pieces.dtype),
+            jax.ShapeDtypeStruct((copies, transmits) + tile, pieces.dtype),
             jax.ShapeDtypeStruct(rows.shape, jnp.int32),
         ),
-        in_specs=[SMEM, VMEM, SMEM, VMEM, VMEM],
+        in_specs=[VMEM] * 5,
         out_specs=(VMEM, VMEM),
         compiler_params=PARAMS,
     )(acquirer, pieces, counts, rows, columns)
 
 
 def sum_and_copy(acquirer, parts, groups, copies):
-    transmits = acquirer.shape[0]
+    transmits = acquirer.shape[1]
+    tile = parts.shape[2:]
 
     def kernel(acquirer_ref, parts_ref, out_ref):
         for transmit in range(transmits):
-            start = lax.rem(acquirer_ref[transmit], Z) * groups
-            total = parts_ref[start, transmit]
-            for group in range(1, groups):
-                total += parts_ref[start + group, transmit]
+            z = jnp.broadcast_to(acquirer_ref[:, transmit : transmit + 1], tile) & (Z - 1)
+            total = jnp.zeros(tile, jnp.float32)
+            for source in range(Z):
+                here = parts_ref[source * groups, transmit]
+                for group in range(1, groups):
+                    here += parts_ref[source * groups + group, transmit]
+                total = jnp.where(z == source, here, total)
             for copy in range(copies):
                 out_ref[copy, transmit] = total
 
     return pl.pallas_call(
         kernel,
         out_shape=jax.ShapeDtypeStruct((copies,) + parts.shape[1:], parts.dtype),
-        in_specs=[SMEM, VMEM],
+        in_specs=[VMEM, VMEM],
         out_specs=VMEM,
         compiler_params=PARAMS,
     )(acquirer, parts)
@@ -118,8 +127,11 @@
     pairs = table.shape[0] // quarters
 
     def kernel(
-        slots_ref, index_ref, empty_ref, table_ref, panels_ref, others_ref, out_ref, weights, total
+        slots_given, index_ref, empty_ref, table_ref, panels_ref, others_ref,
+        out_ref, weights, total, slots_ref, arrived,
     ):
+        scalars = pltpu.make_async_copy(slots_given, slots_ref, arrived)
+        scalars.start()
         group = lax.axis_index("grp")
         core = group & 1
         mine = (lax.broadcasted_iota(jnp.int32, (windows, LANES), 1) // (LANES // 2)) == core
@@ -128,24 +140,36 @@
                 both = jnp.concatenate(
                     [table_ref[pair * quarters + quarter, transmit] for quarter in range(quarters)], axis=0
                 )
-                for i, aligned in enumerate((both, pltpu.roll(both, LANES // 2, 1))):
+                for place, aligned in enumerate((both, pltpu.roll(both, LANES // 2, 1))):
                     aligned = jnp.where(mine, aligned, 0.0)
-                    high = aligned.astype(jnp.bfloat16)
-                    low = (aligned - high.astype(jnp.float32)).astype(jnp.bfloat16)
-                    weights[(transmit * pairs + pair) * 2 + i] = jnp.concatenate([high, low], axis=0)
+                    for i, side in enumerate((aligned, pltpu.roll(aligned, LANES // 2, 1))):
+                        high = side.astype(jnp.bfloat16)
+                        low = (side - high.astype(jnp.float32)).astype(jnp.bfloat16)
+                        weights[i, (transmit * pairs + pair) * 2 + place] = jnp.concatenate(
+                            [high, low], axis=0
+                        )
         total[...] = empty_ref[...]
-        for first, source_ref in ((group * slots, panels_ref), ((group ^ 1) * slots, others_ref)):
-            for transmit in range(transmits):
-                for slot in range(slots):
-                    packed = slots_ref[transmit, 0, first + slot]
-                    row, column = packed >> COLUMN_BITS, packed & ((1 << COLUMN_BITS) - 1)
-                    terms = lax.dot_general(
-                        weights[transmit * pairs * 2 + (column ^ core)],
-                        source_ref[0, transmit, slot],
-                        NT,
-                        preferred_element_type=jnp.float32,
+        scalars.wait()
+        starts = (group * slots, (group ^ 1) * slots)
+        mine_of_block = (lax.broadcasted_iota(jnp.int32, (block, LANES), 1) // (LANES // 2)) == core
+        for transmit in range(transmits):
+            for slot in range(slots):
+                packed = [slots_ref[transmit, 0, start + slot] for start in starts]
+                columns = [(number & ((1 << COLUMN_BITS) - 1)) ^ core for number in packed]
+                other = pltpu.roll(others_ref[0, transmit, slot].astype(jnp.float32), LANES // 2, 1)
+                terms = lax.dot_general(
+                    jnp.concatenate(
+                        [weights[i, transmit * pairs * 2 + column] for i, column in enumerate(columns)], axis=0
+                    ),
+                    jnp.where(mine_of_block, panels_ref[0, transmit, slot], other.astype(jnp.bfloat16)),
+                    NT,
+                    preferred_element_type=jnp.float32,
+                )
+                for i, number in enumerate(packed):
+                    high, low = (
+                        terms[(2 * i + j) * windows : (2 * i + j + 1) * windows] for j in range(2)
                     )
-                    total[row] += terms[:windows] + terms[windows:]
+                    total[number >> COLUMN_BITS] += high + low
         number = lax.broadcasted_iota(jnp.int32, (windows, block), 0)
         for row in range(row_blocks):
             chosen = jnp.where(number == index_ref[row], total[row], 0.0)
@@ -154,11 +178,13 @@
     return pl.pallas_call(
         kernel,
         out_shape=jax.ShapeDtypeStruct((row_blocks, 1, block), jnp.float32),
-        in_specs=[SMEM, VMEM, VMEM, VMEM, VMEM, VMEM],
+        in_specs=[VMEM] * 6,
         out_specs=VMEM,
         scratch_shapes=[
-            pltpu.VMEM((transmits * pairs * 2, 2 * windows, LANES), jnp.bfloat16),
+            pltpu.VMEM((2, transmits * pairs * 2, 2 * windows, LANES), jnp.bfloat16),
             pltpu.VMEM(empty.shape, empty.dtype),
+            pltpu.SMEM(slot_table.shape, slot_table.dtype),
+            pltpu.SemaphoreType.DMA,
         ],
         compiler_params=PARAMS,
     )(slot_table, windows_of_voxels, empty, table, panels, others)
@@ -186,6 +212,7 @@
         (empty, panels, apodization, echo_data)
     )
     others = lax.ppermute(given, "grp", [(i, i ^ 1) for i in range(groups)])
+    acquirer = acquirer.reshape(1, -1)
     pieces = exchange(window_sums(apodization, echo_data), "slab", planes)
     picked, slot_table = pick_acquirers(
         acquirer, pieces, Z * groups, block_count, rows, columns, voxels.shape[0]

time: 71.9 us -> 70.7 us (0.983)
  Pallas kernels: 3.06 us -> 1.83 us
where the time goes in v9:
time: 70.7 us; the launch traced here: 70.4 us
  blocking collectives  58.9 us (83%)
  starting transfers between devices  8.92 us (13%)
  Pallas kernels  1.83 us (3%)
    all_to_all x4, blocking collectives, exchange(): lax.all_to_all(pieces, axis, split_axis=0, concat_axis=0, axis_index_grou...  58.9 us
    ppermute x1, starting transfers between devices, per_device(): others = lax.ppermute(given, 'grp', [(i, i ^ 1) for i in range(groups)])  8.92 us
  transfers between devices with their start and end apart: 1, of which 0 were waited for; matrix products, arithmetic and copies ran while one was open for 0% of the time, Pallas kernels for 1%

profile of v9, /device:TPU:1, one launch (start us, length us, event | category | flops | bytes accessed | tf_op | source)
XLA Modules:
  0.0 70.4 jit_solution(9551418451559629513)
XLA Ops:
  0.0 0.0 copy-start.2
  0.0 0.0 copy-start.1
  0.0 8.9 %collective-permute-start = (bf16[1,3,8,128,128]{4,3,2,1,0:T(8,128)(2,1)}, bf16[1,3,8,128,128]{4,3,2,1,0:T(8,128)(2,1)S(1)}, u32[]{:S(2)}, u32[]{:S(2)}) collective-permute-start(bf16[1,3,8,128,128]{4,3,2,1,0:T(8,128)(2,1)} %panels_ref.1), channel_id=1, source_target_pairs={{0,1},{1,0},{2,3},{3,2},{4,5},{5,4},{6,7},{7,6},{8,9},{9,8},{10,11... | collective-permute-start | bytes 2359304 | tf_op jit(solution)/shard_map/ppermute | solution.py:214
  8.9 0.0 copy-done.2
  9.0 0.0 copy-done.1
  9.0 0.0 copy-start.4
  9.0 0.0 copy-start.5
  9.0 0.0 copy-start.6
  9.0 0.0 copy-start.7
  9.0 0.3 shard_map.83
  9.3 0.0 copy-start
  9.3 13.4 %all_to_all.20.pieces_ref = f32[32,2,4,128]{3,2,1,0:T(4,128)S(1)} all-to-all(f32[32,2,4,128]{3,2,1,0:T(4,128)S(1)} %shard_map.83), channel_id=1, replica_groups={{0,16,32,48,64,80,96,112,128,144,160,176,192,208,224,240,256,272,288,30..., dimensions={0} | all-to-all | bytes 262144 | tf_op jit(solution)/shard_map/all_to_all | solution.py:194
  22.7 0.0 copy-done.4
  22.7 0.0 copy-done.5
  22.7 0.0 copy-done.6
  22.7 0.0 copy-done.7
  22.7 0.1 shard_map.84
  22.8 0.0 collective-permute-done.others_ref
  22.9 20.7 %all_to_all.21.parts_ref = f32[16,3,4,128]{3,2,1,0:T(4,128)S(1)} all-to-all(f32[16,3,4,128]{3,2,1,0:T(4,128)S(1)} %get-tuple-element.19), channel_id=1, replica_groups={{0,1,2,3,4,5,6,7,8,9,10,11,12,13,14,15},{16,17,18,19,20,21,22,23,24,25,..., dimensions={0} | all-to-all | bytes 196608 | tf_op jit(solution)/shard_map/all_to_all | solution.py:194
  43.5 0.1 shard_map.85
  43.6 0.0 copy-start.3
  43.6 13.1 %all_to_all.22.table_ref = f32[32,3,4,128]{3,2,1,0:T(4,128)S(1)} all-to-all(f32[32,3,4,128]{3,2,1,0:T(4,128)S(1)} %shard_map.85), channel_id=1, replica_groups={{0,16,32,48,64,80,96,112,128,144,160,176,192,208,224,240,256,272,288,30..., dimensions={0} | all-to-all | bytes 393216 | tf_op jit(solution)/shard_map/all_to_all | solution.py:194
  56.7 0.0 copy-done
  56.7 0.0 copy-done.3
  56.7 1.3 %shard_map.86 = f32[8,1,128]{2,1,0:T(1,128)S(1)} custom-call(s32[3,1,64]{2,1,0:T(1,128)S(1)} %get-tuple-element.15.slots_given, s32[8,1,128]{2,1,0:T(1,128)S(1)} %bitcast.4, f32[9,16,128]{2,1,0:T(8,128)S(1)} %shard_map.82.empty_ref, f32[32,3,4,128]{3,2,1,0:T(4,128)S(1)} %all_to_all.22.table_ref, bf16[1,3,8,128,128]{4,3,2,1,0:T(8,128)(2,1)S(1)} %copy-done, ...), custom_call_target="tpu_custom_call" | custom-call | tf_op jit(solution)/shard_map/pallas_call | solution.py:178
  58.1 11.8 %all_to_all.23 = f32[8,1,128]{2,1,0:T(1,128)S(1)} all-to-all(f32[8,1,128]{2,1,0:T(1,128)S(1)} %shard_map.86), channel_id=1, replica_groups=mesh['slab'=64,'grp'=8] {'grp'}, dimensions={0} | all-to-all | bytes 8192 | tf_op jit(solution)/shard_map/all_to_all | solution.py:194
  69.8 0.5 reduce_sum.9
  (1 shorter events, 0.0 us)
Async XLA Ops:
  0.0 8.9 %copy-start.2 = (f32[16,128]{1,0:T(8,128)S(1)}, f32[16,128]{1,0:T(8,128)}, u32[]{:S(2)}) copy-start(f32[16,128]{1,0:T(8,128)} %apod_ref) | copy-start | bytes 24580
  0.0 9.0 %copy-start.1 = (bf16[1,128,2048]{2,1,0:T(8,128)(2,1)S(1)}, bf16[1,128,2048]{2,1,0:T(8,128)(2,1)}, u32[]{:S(2)}) copy-start(bf16[1,128,2048]{2,1,0:T(8,128)(2,1)} %echo_ref) | copy-start | bytes 1572868
  0.0 22.8 %collective-permute-start = (bf16[1,3,8,128,128]{4,3,2,1,0:T(8,128)(2,1)}, bf16[1,3,8,128,128]{4,3,2,1,0:T(8,128)(2,1)S(1)}, u32[]{:S(2)}, u32[]{:S(2)}) collective-permute-start(bf16[1,3,8,128,128]{4,3,2,1,0:T(8,128)(2,1)} %panels_ref.1), channel_id=1, source_target_pairs={{0,1},{1,0},{2,3},{3,2},{4,5},{5,4},{6,7},{7,6},{8,9},{9,8},{10,11... | collective-permute-start | bytes 2359304 | tf_op jit(solution)/shard_map/ppermute | solution.py:214
  9.0 13.7 %copy-start.4 = (s32[3]{0:T(128)S(1)}, s32[3]{0:T(128)}, u32[]{:S(2)}) copy-start(s32[3]{0:T(128)} %param.9) | copy-start | bytes 40
  9.0 13.7 %copy-start.5 = (s32[1,3,64]{2,0,1:T(1,128)S(1)}, s32[1,3,64]{2,0,1:T(1,128)}, u32[]{:S(2)}) copy-start(s32[1,3,64]{2,0,1:T(1,128)} %param.12) | copy-start | bytes 2308
  9.0 13.7 %copy-start.6 = (s32[1,3,64]{2,0,1:T(1,128)S(1)}, s32[1,3,64]{2,0,1:T(1,128)}, u32[]{:S(2)}) copy-start(s32[1,3,64]{2,0,1:T(1,128)} %param.13) | copy-start | bytes 2308
  9.0 13.7 %copy-start.7 = (s32[1,3]{1,0:T(1,128)S(1)}, s32[1,3]{1,0:T(1,128)}, u32[]{:S(2)}) copy-start(s32[1,3]{1,0:T(1,128)} %counts_ref.1) | copy-start | bytes 40
  9.3 47.4 %copy-start = (bf16[1,3,8,128,128]{4,3,2,1,0:T(8,128)(2,1)S(1)}, bf16[1,3,8,128,128]{4,3,2,1,0:T(8,128)(2,1)}, u32[]{:S(2)}) copy-start(bf16[1,3,8,128,128]{4,3,2,1,0:T(8,128)(2,1)} %panels_ref.1) | copy-start | bytes 2359300
  43.6 13.1 %copy-start.3 = (s32[1024]{0:T(1024)S(1)}, s32[1024]{0:T(1024)}, u32[]{:S(2)}) copy-start(s32[1024]{0:T(1024)} %param.15) | copy-start | bytes 12292

commit v10 on v9

--- a/solution.py
+++ b/solution.py
@@ -72,7 +72,8 @@
         for transmit in range(transmits):
             count = jnp.broadcast_to(counts_ref[:, transmit : transmit + 1], place.shape)
             row = jnp.where(place < count, rows_ref[transmit], row_blocks)
-            slots_ref[transmit] = (row << COLUMN_BITS) | columns_ref[transmit]
+            packed = (row << COLUMN_BITS) | columns_ref[transmit]
+            slots_ref[transmit] = jnp.concatenate([packed] * (LANES // packed.shape[1]), axis=1)
             chip = jnp.broadcast_to(acquirer_ref[:, transmit : transmit + 1], tile) // Z
             picked = [jnp.zeros(tile, jnp.float32)] * 2
             for source in range(pieces.shape[0]):
@@ -86,7 +87,7 @@
         kernel,
         out_shape=(
             jax.ShapeDtypeStruct((copies, transmits) + tile, pieces.dtype),
-            jax.ShapeDtypeStruct(rows.shape, jnp.int32),
+            jax.ShapeDtypeStruct(rows.shape[:2] + (LANES,), jnp.int32),
         ),
         in_specs=[VMEM] * 5,
         out_specs=(VMEM, VMEM),
@@ -128,10 +129,8 @@
 
     def kernel(
         slots_given, index_ref, empty_ref, table_ref, panels_ref, others_ref,
-        out_ref, weights, total, slots_ref, arrived,
+        out_ref, weights, total,
     ):
-        scalars = pltpu.make_async_copy(slots_given, slots_ref, arrived)
-        scalars.start()
         group = lax.axis_index("grp")
         core = group & 1
         mine = (lax.broadcasted_iota(jnp.int32, (windows, LANES), 1) // (LANES // 2)) == core
@@ -142,26 +141,30 @@
                 )
                 for place, aligned in enumerate((both, pltpu.roll(both, LANES // 2, 1))):
                     aligned = jnp.where(mine, aligned, 0.0)
-                    for i, side in enumerate((aligned, pltpu.roll(aligned, LANES // 2, 1))):
-                        high = side.astype(jnp.bfloat16)
-                        low = (side - high.astype(jnp.float32)).astype(jnp.bfloat16)
-                        weights[i, (transmit * pairs + pair) * 2 + place] = jnp.concatenate(
-                            [high, low], axis=0
-                        )
+                    high = aligned.astype(jnp.bfloat16)
+                    low = (aligned - high.astype(jnp.float32)).astype(jnp.bfloat16)
+                    weights[(transmit * pairs + pair) * 2 + place] = jnp.concatenate([high, low], axis=0)
         total[...] = empty_ref[...]
-        scalars.wait()
         starts = (group * slots, (group ^ 1) * slots)
-        mine_of_block = (lax.broadcasted_iota(jnp.int32, (block, LANES), 1) // (LANES // 2)) == core
-        for transmit in range(transmits):
+        nothing = jnp.zeros((2 * windows, LANES), jnp.bfloat16)
+        for transmit in range(transmits):
+            listed = slots_given[transmit]
+            here = [pltpu.roll(listed, lax.rem(LANES - start, LANES), 1) for start in starts]
             for slot in range(slots):
-                packed = [slots_ref[transmit, 0, start + slot] for start in starts]
+                packed = [side[0, slot] for side in here]
                 columns = [(number & ((1 << COLUMN_BITS) - 1)) ^ core for number in packed]
-                other = pltpu.roll(others_ref[0, transmit, slot].astype(jnp.float32), LANES // 2, 1)
+                own, other = (weights[transmit * pairs * 2 + column] for column in columns)
                 terms = lax.dot_general(
                     jnp.concatenate(
-                        [weights[i, transmit * pairs * 2 + column] for i, column in enumerate(columns)], axis=0
+                        [
+                            jnp.concatenate([own, nothing], axis=1),
+                            jnp.concatenate([nothing, other], axis=1),
+                        ],
+                        axis=0,
                     ),
-                    jnp.where(mine_of_block, panels_ref[0, transmit, slot], other.astype(jnp.bfloat16)),
+                    jnp.concatenate(
+                        [panels_ref[0, transmit, slot], others_ref[0, transmit, slot]], axis=1
+                    ),
                     NT,
                     preferred_element_type=jnp.float32,
                 )
@@ -181,10 +184,8 @@
         in_specs=[VMEM] * 6,
         out_specs=VMEM,
         scratch_shapes=[
-            pltpu.VMEM((2, transmits * pairs * 2, 2 * windows, LANES), jnp.bfloat16),
+            pltpu.VMEM((transmits * pairs * 2, 2 * windows, LANES), jnp.bfloat16),
             pltpu.VMEM(empty.shape, empty.dtype),
-            pltpu.SMEM(slot_table.shape, slot_table.dtype),
-            pltpu.SemaphoreType.DMA,
         ],
         compiler_params=PARAMS,
     )(slot_table, windows_of_voxels, empty, table, panels, others)

time: 70.7 us -> 70.1 us (level)
  no operation moved by 1% of the time
where the time goes in v10:
time: 70.1 us; the launch traced here: 69.8 us
  blocking collectives  58.9 us (84%)
  starting transfers between devices  8.92 us (13%)
  Pallas kernels  1.3 us (2%)
    all_to_all x4, blocking collectives, exchange(): lax.all_to_all(pieces, axis, split_axis=0, concat_axis=0, axis_index_grou...  58.9 us
    ppermute x1, starting transfers between devices, per_device(): others = lax.ppermute(given, 'grp', [(i, i ^ 1) for i in range(groups)])  8.92 us
  transfers between devices with their start and end apart: 1, of which 0 were waited for; matrix products, arithmetic and copies ran while one was open for 0% of the time, Pallas kernels for 1%

profile of v10, /device:TPU:1, one launch (start us, length us, event | category | flops | bytes accessed | tf_op | source)
XLA Modules:
  0.0 69.8 jit_solution(14084947652015977148)
XLA Ops:
  0.0 0.0 copy-start.2
  0.0 0.0 copy-start.1
  0.0 8.9 %collective-permute-start = (bf16[1,3,8,128,128]{4,3,2,1,0:T(8,128)(2,1)}, bf16[1,3,8,128,128]{4,3,2,1,0:T(8,128)(2,1)S(1)}, u32[]{:S(2)}, u32[]{:S(2)}) collective-permute-start(bf16[1,3,8,128,128]{4,3,2,1,0:T(8,128)(2,1)} %panels_ref.1), channel_id=1, source_target_pairs={{0,1},{1,0},{2,3},{3,2},{4,5},{5,4},{6,7},{7,6},{8,9},{9,8},{10,11... | collective-permute-start | bytes 2359304 | tf_op jit(solution)/shard_map/ppermute | solution.py:215
  8.9 0.0 copy-done.2
  9.0 0.0 copy-done.1
  9.0 0.0 copy-start.4
  9.0 0.0 copy-start.5
  9.0 0.0 copy-start.6
  9.0 0.0 copy-start.7
  9.0 0.3 shard_map.83
  9.3 0.0 copy-start
  9.3 13.4 %all_to_all.20.pieces_ref = f32[32,2,4,128]{3,2,1,0:T(4,128)S(1)} all-to-all(f32[32,2,4,128]{3,2,1,0:T(4,128)S(1)} %shard_map.83), channel_id=1, replica_groups={{0,16,32,48,64,80,96,112,128,144,160,176,192,208,224,240,256,272,288,30..., dimensions={0} | all-to-all | bytes 262144 | tf_op jit(solution)/shard_map/all_to_all | solution.py:195
  22.7 0.0 copy-done.4
  22.7 0.0 copy-done.5
  22.7 0.0 copy-done.6
  22.7 0.0 copy-done.7
  22.7 0.1 shard_map.84
  22.9 0.0 collective-permute-done.others_ref
  22.9 20.7 %all_to_all.21.parts_ref = f32[16,3,4,128]{3,2,1,0:T(4,128)S(1)} all-to-all(f32[16,3,4,128]{3,2,1,0:T(4,128)S(1)} %get-tuple-element.19), channel_id=1, replica_groups={{0,1,2,3,4,5,6,7,8,9,10,11,12,13,14,15},{16,17,18,19,20,21,22,23,24,25,..., dimensions={0} | all-to-all | bytes 196608 | tf_op jit(solution)/shard_map/all_to_all | solution.py:195
  43.5 0.1 shard_map.85
  43.6 0.0 copy-start.3
  43.6 13.1 %all_to_all.22.table_ref = f32[32,3,4,128]{3,2,1,0:T(4,128)S(1)} all-to-all(f32[32,3,4,128]{3,2,1,0:T(4,128)S(1)} %shard_map.85), channel_id=1, replica_groups={{0,16,32,48,64,80,96,112,128,144,160,176,192,208,224,240,256,272,288,30..., dimensions={0} | all-to-all | bytes 393216 | tf_op jit(solution)/shard_map/all_to_all | solution.py:195
  56.7 0.0 copy-done
  56.8 0.0 copy-done.3
  56.8 0.8 %shard_map.86 = f32[8,1,128]{2,1,0:T(1,128)S(1)} custom-call(s32[3,1,128]{2,1,0:T(1,128)S(1)} %get-tuple-element.15.slots_given, s32[8,1,128]{2,1,0:T(1,128)S(1)} %bitcast.4, f32[9,16,128]{2,1,0:T(8,128)S(1)} %shard_map.82.empty_ref, f32[32,3,4,128]{3,2,1,0:T(4,128)S(1)} %all_to_all.22.table_ref, bf16[1,3,8,128,128]{4,3,2,1,0:T(8,128)(2,1)S(1)} %copy-done, ...), custom_call_target="tpu_custom_call" | custom-call | tf_op jit(solution)/shard_map/pallas_call | solution.py:181
  57.5 11.8 %all_to_all.23 = f32[8,1,128]{2,1,0:T(1,128)S(1)} all-to-all(f32[8,1,128]{2,1,0:T(1,128)S(1)} %shard_map.86), channel_id=1, replica_groups=mesh['slab'=64,'grp'=8] {'grp'}, dimensions={0} | all-to-all | bytes 8192 | tf_op jit(solution)/shard_map/all_to_all | solution.py:195
  69.3 0.5 reduce_sum.9
  (1 shorter events, 0.0 us)
Async XLA Ops:
  0.0 8.9 %copy-start.2 = (f32[16,128]{1,0:T(8,128)S(1)}, f32[16,128]{1,0:T(8,128)}, u32[]{:S(2)}) copy-start(f32[16,128]{1,0:T(8,128)} %apod_ref) | copy-start | bytes 24580
  0.0 9.0 %copy-start.1 = (bf16[1,128,2048]{2,1,0:T(8,128)(2,1)S(1)}, bf16[1,128,2048]{2,1,0:T(8,128)(2,1)}, u32[]{:S(2)}) copy-start(bf16[1,128,2048]{2,1,0:T(8,128)(2,1)} %echo_ref) | copy-start | bytes 1572868
  0.0 22.8 %collective-permute-start = (bf16[1,3,8,128,128]{4,3,2,1,0:T(8,128)(2,1)}, bf16[1,3,8,128,128]{4,3,2,1,0:T(8,128)(2,1)S(1)}, u32[]{:S(2)}, u32[]{:S(2)}) collective-permute-start(bf16[1,3,8,128,128]{4,3,2,1,0:T(8,128)(2,1)} %panels_ref.1), channel_id=1, source_target_pairs={{0,1},{1,0},{2,3},{3,2},{4,5},{5,4},{6,7},{7,6},{8,9},{9,8},{10,11... | collective-permute-start | bytes 2359304 | tf_op jit(solution)/shard_map/ppermute | solution.py:215
  9.0 13.7 %copy-start.4 = (s32[3]{0:T(128)S(1)}, s32[3]{0:T(128)}, u32[]{:S(2)}) copy-start(s32[3]{0:T(128)} %param.9) | copy-start | bytes 40
  9.0 13.7 %copy-start.5 = (s32[1,3,64]{2,0,1:T(1,128)S(1)}, s32[1,3,64]{2,0,1:T(1,128)}, u32[]{:S(2)}) copy-start(s32[1,3,64]{2,0,1:T(1,128)} %param.12) | copy-start | bytes 2308
  9.0 13.7 %copy-start.6 = (s32[1,3,64]{2,0,1:T(1,128)S(1)}, s32[1,3,64]{2,0,1:T(1,128)}, u32[]{:S(2)}) copy-start(s32[1,3,64]{2,0,1:T(1,128)} %param.13) | copy-start | bytes 2308
  9.0 13.7 %copy-start.7 = (s32[1,3]{1,0:T(1,128)S(1)}, s32[1,3]{1,0:T(1,128)}, u32[]{:S(2)}) copy-start(s32[1,3]{1,0:T(1,128)} %counts_ref.1) | copy-start | bytes 40
  9.3 47.4 %copy-start = (bf16[1,3,8,128,128]{4,3,2,1,0:T(8,128)(2,1)S(1)}, bf16[1,3,8,128,128]{4,3,2,1,0:T(8,128)(2,1)}, u32[]{:S(2)}) copy-start(bf16[1,3,8,128,128]{4,3,2,1,0:T(8,128)(2,1)} %panels_ref.1) | copy-start | bytes 2359300
  43.6 13.1 %copy-start.3 = (s32[1024]{0:T(1024)S(1)}, s32[1024]{0:T(1024)}, u32[]{:S(2)}) copy-start(s32[1024]{0:T(1024)} %param.15) | copy-start | bytes 12292

commit v11 on v10

--- a/solution.py
+++ b/solution.py
@@ -23,16 +23,25 @@
         out_shape=jax.ShapeDtypeStruct((row_blocks + 1, windows, block), jnp.float32),
         out_specs=VMEM,
         compiler_params=PARAMS,
-        cost_estimate=pl.CostEstimate(flops=200000000, bytes_accessed=0, transcendentals=0),
+        cost_estimate=pl.CostEstimate(flops=200_000_000, bytes_accessed=0, transcendentals=0),
     )()
 
 
-def window_sums(apodization, echo):
+def window_sums(apodization, echo, acquirer, counts, rows, columns, row_blocks):
     windows, channels = apodization.shape
     samples = echo.shape[-1]
     pairs, quarters = samples // (2 * LANES), windows // 4
 
-    def kernel(apod_ref, echo_ref, out_ref):
+    def kernel(
+        apod_ref, echo_ref, acquirer_ref, counts_ref, rows_ref, columns_ref, out_ref, acquirer_out, slots_ref
+    ):
+        acquirer_out[...] = acquirer_ref[...]
+        place = lax.broadcasted_iota(jnp.int32, rows.shape[1:], 1)
+        for transmit in range(rows.shape[0]):
+            count = jnp.broadcast_to(counts_ref[:, transmit : transmit + 1], place.shape)
+            row = jnp.where(place < count, rows_ref[transmit], row_blocks)
+            packed = (row << COLUMN_BITS) | columns_ref[transmit]
+            slots_ref[transmit] = jnp.concatenate([packed] * (LANES // packed.shape[1]), axis=1)
         apod = apod_ref[...]
         high = apod.astype(jnp.bfloat16)
         rest = apod - high.astype(jnp.float32)
@@ -56,24 +65,24 @@
 
     return pl.pallas_call(
         kernel,
-        out_shape=jax.ShapeDtypeStruct((pairs * quarters, 2, 4, LANES), jnp.float32),
-        in_specs=[VMEM, VMEM],
-        out_specs=VMEM,
-        compiler_params=PARAMS,
-    )(apodization, echo)
-
-
-def pick_acquirers(acquirer, pieces, copies, counts, rows, columns, row_blocks):
+        out_shape=(
+            jax.ShapeDtypeStruct((pairs * quarters, 2, 4, LANES), jnp.float32),
+            jax.ShapeDtypeStruct(acquirer.shape, jnp.int32),
+            jax.ShapeDtypeStruct(rows.shape[:2] + (LANES,), jnp.int32),
+        ),
+        in_specs=[VMEM] * 6,
+        out_specs=(VMEM,) * 3,
+        cost_estimate=pl.CostEstimate(flops=200_000_000, bytes_accessed=0, transcendentals=0),
+        compiler_params=PARAMS,
+    )(apodization, echo, acquirer, counts, rows, columns)
+
+
+def pick_acquirers(acquirer, pieces, copies):
     transmits = acquirer.shape[1]
     tile = pieces.shape[2:]
 
-    def kernel(acquirer_ref, pieces_ref, counts_ref, rows_ref, columns_ref, out_ref, slots_ref):
-        place = lax.broadcasted_iota(jnp.int32, rows.shape[1:], 1)
-        for transmit in range(transmits):
-            count = jnp.broadcast_to(counts_ref[:, transmit : transmit + 1], place.shape)
-            row = jnp.where(place < count, rows_ref[transmit], row_blocks)
-            packed = (row << COLUMN_BITS) | columns_ref[transmit]
-            slots_ref[transmit] = jnp.concatenate([packed] * (LANES // packed.shape[1]), axis=1)
+    def kernel(acquirer_ref, pieces_ref, out_ref):
+        for transmit in range(transmits):
             chip = jnp.broadcast_to(acquirer_ref[:, transmit : transmit + 1], tile) // Z
             picked = [jnp.zeros(tile, jnp.float32)] * 2
             for source in range(pieces.shape[0]):
@@ -85,14 +94,11 @@
 
     return pl.pallas_call(
         kernel,
-        out_shape=(
-            jax.ShapeDtypeStruct((copies, transmits) + tile, pieces.dtype),
-            jax.ShapeDtypeStruct(rows.shape[:2] + (LANES,), jnp.int32),
-        ),
-        in_specs=[VMEM] * 5,
-        out_specs=(VMEM, VMEM),
-        compiler_params=PARAMS,
-    )(acquirer, pieces, counts, rows, columns)
+        out_shape=jax.ShapeDtypeStruct((copies, transmits) + tile, pieces.dtype),
+        in_specs=[VMEM] * 2,
+        out_specs=VMEM,
+        compiler_params=PARAMS,
+    )(acquirer, pieces)
 
 
 def sum_and_copy(acquirer, parts, groups, copies):
@@ -116,6 +122,7 @@
         out_shape=jax.ShapeDtypeStruct((copies,) + parts.shape[1:], parts.dtype),
         in_specs=[VMEM, VMEM],
         out_specs=VMEM,
+        cost_estimate=pl.CostEstimate(flops=10_000_000_000, bytes_accessed=0, transcendentals=0),
         compiler_params=PARAMS,
     )(acquirer, parts)
 
@@ -209,18 +216,21 @@
     voxels = window_index.reshape(-1, 1, panels.shape[-1])
     rows, columns = (jnp.transpose(v, (1, 0, 2)) for v in (block_rows, block_columns))
     empty = empty_sums(voxels.shape[0], apodization.shape[0], voxels.shape[2])
-    empty, given, apodization, echo_data = lax.optimization_barrier(
-        (empty, panels, apodization, echo_data)
-    )
+    acquirer = acquirer.reshape(1, -1)
+    empty, apodization, echo_data, acquirer, block_count, rows, columns = lax.optimization_barrier(
+        (empty, apodization, echo_data, acquirer, block_count, rows, columns)
+    )
+    sums, acquirer, slot_table = window_sums(
+        apodization, echo_data, acquirer, block_count, rows, columns, voxels.shape[0]
+    )
+    sums, given = lax.optimization_barrier((sums, panels))
     others = lax.ppermute(given, "grp", [(i, i ^ 1) for i in range(groups)])
-    acquirer = acquirer.reshape(1, -1)
-    pieces = exchange(window_sums(apodization, echo_data), "slab", planes)
-    picked, slot_table = pick_acquirers(
-        acquirer, pieces, Z * groups, block_count, rows, columns, voxels.shape[0]
-    )
-    picked, others = lax.optimization_barrier((picked, others))
+    pieces = exchange(sums, "slab", planes)
+    picked = pick_acquirers(acquirer, pieces, Z * groups)
     parts = exchange(picked, ("slab", "grp"), lines)
-    table = exchange(sum_and_copy(acquirer, parts, groups, slabs // Z), "slab", planes)
+    summed = sum_and_copy(acquirer, parts, groups, slabs // Z)
+    summed, others = lax.optimization_barrier((summed, others))
+    table = exchange(summed, "slab", planes)
     partial = slot_sums(slot_table, voxels, empty, table, panels, others)
     return jnp.sum(exchange(partial, "grp"), axis=(0, 1))
 

time: 70.1 us -> 69.2 us (0.987)
  blocking collectives: 58.9 us -> 44.4 us
  waiting for transfers between devices: 0.01 us -> 6.46 us
  starting transfers between devices: 8.92 us -> 14.4 us
  local copies, waits for them, and re-layouts: 0.05 us -> 1.02 us
    all_to_all x4 -> x3, blocking collectives: 58.9 us -> 44.4 us  [exchange(): lax.all_to_all(pieces, axis, split_axis=0, concat_axis=0, axis_index_grou...]
    all_to_all x0 -> x1, starting transfers between devices: none -> 12.4 us  [exchange(): lax.all_to_all(pieces, axis, split_axis=0, concat_axis=0, axis_index_grou...]
    ppermute x1, starting transfers between devices: 8.92 us -> 2.01 us  [per_device(): others = lax.ppermute(given, 'grp', [(i, i ^ 1) for i in range(groups)])]
    all_to_all x0 -> x1, waiting for transfers between devices: none -> 6.46 us  [exchange(): lax.all_to_all(pieces, axis, split_axis=0, concat_axis=0, axis_index_grou...]
    unnamed x16, local copies, waits for them, and re-layouts: 0.05 us -> 1.02 us
  transfers between devices with their start and end apart: 1 -> 2, of which waited for: 0 -> 1; matrix products, arithmetic and copies ran while one was open for 0% -> 0% of each run, Pallas kernels for 1% -> 0%
where the time goes in v11:
time: 69.2 us; the launch traced here: 68.9 us
  blocking collectives  44.4 us (64%)
  starting transfers between devices  14.4 us (21%)
  waiting for transfers between devices  6.46 us (9%)
  Pallas kernels  1.92 us (3%)
  local copies, waits for them, and re-layouts  1.02 us (1%)
    all_to_all x3, blocking collectives, exchange(): lax.all_to_all(pieces, axis, split_axis=0, concat_axis=0, axis_index_grou...  44.4 us
    all_to_all x1, starting transfers between devices, exchange(): lax.all_to_all(pieces, axis, split_axis=0, concat_axis=0, axis_index_grou...  12.4 us
    all_to_all x1, waiting for transfers between devices, exchange(): lax.all_to_all(pieces, axis, split_axis=0, concat_axis=0, axis_index_grou...  6.46 us
    ppermute x1, starting transfers between devices, per_device(): others = lax.ppermute(given, 'grp', [(i, i ^ 1) for i in range(groups)])  2.01 us
  transfers between devices with their start and end apart: 2, of which 1 were waited for; matrix products, arithmetic and copies ran while one was open for 0% of the time, Pallas kernels for 0%

profile of v11, /device:TPU:1, one launch (start us, length us, event | category | flops | bytes accessed | tf_op | source)
XLA Modules:
  0.0 68.9 jit_solution(15622512540744294656)
XLA Ops:
  0.0 0.0 copy-start.3
  0.0 0.0 copy-start.2
  0.0 0.0 copy-start.4
  0.0 0.0 copy-start.5
  0.0 0.0 copy-start.6
  0.0 0.0 copy-start.7
  0.1 0.0 copy-start
  0.1 0.6 copy-done.3
  0.7 0.4 copy-done.2
  1.1 0.0 copy-done.4
  1.1 0.0 copy-done.5
  1.1 0.0 copy-done.6
  1.1 0.0 copy-done.7
  1.1 0.3 shard_map.83
  1.4 19.5 %all_to_all.20.pieces_ref = f32[32,2,4,128]{3,2,1,0:T(4,128)S(1)} all-to-all(f32[32,2,4,128]{3,2,1,0:T(4,128)S(1)} %get-tuple-element.29), channel_id=1, replica_groups={{0,16,32,48,64,80,96,112,128,144,160,176,192,208,224,240,256,272,288,30..., dimensions={0} | all-to-all | bytes 262144 | tf_op jit(solution)/shard_map/all_to_all | solution.py:202
  20.8 0.8 %shard_map.84 = f32[16,3,4,128]{3,2,1,0:T(4,128)} custom-call(s32[1,3]{1,0:T(1,128)S(1)} %get-tuple-element.27.acquirer_ref, f32[32,2,4,128]{3,2,1,0:T(4,128)S(1)} %all_to_all.20.pieces_ref), custom_call_target="tpu_custom_call" | custom-call | tf_op jit(solution)/shard_map/pallas_call | solution.py:95
  21.6 12.4 %all-to-all-start.1 = ((f32[16,3,4,128]{3,2,1,0:T(4,128)}), f32[16,3,4,128]{3,2,1,0:T(4,128)S(1)}, u32[]{:S(2)}, u32[]{:S(2)}) async-start(f32[16,3,4,128]{3,2,1,0:T(4,128)} %shard_map.84), calls=%async_computation.1 | async-start | bytes 196608 | tf_op jit(solution)/shard_map/all_to_all | solution.py:202
  34.0 0.0 copy-done
  34.0 2.0 %collective-permute-start = (bf16[1,3,8,128,128]{4,3,2,1,0:T(8,128)(2,1)S(1)}, bf16[1,3,8,128,128]{4,3,2,1,0:T(8,128)(2,1)S(1)}, u32[]{:S(2)}, u32[]{:S(2)}) collective-permute-start(bf16[1,3,8,128,128]{4,3,2,1,0:T(8,128)(2,1)S(1)} %copy-done), channel_id=1, source_target_pairs={{0,1},{1,0},{2,3},{3,2},{4,5},{5,4},{6,7},{7,6},{8,9},{9,8},{10,11... | collective-permute-start | bytes 2359304 | tf_op jit(solution)/shard_map/ppermute | solution.py:227
  36.0 6.5 %all-to-all-done.1.parts_ref = f32[16,3,4,128]{3,2,1,0:T(4,128)S(1)} async-done(((f32[16,3,4,128]{3,2,1,0:T(4,128)}), f32[16,3,4,128]{3,2,1,0:T(4,128)S(1)}, u32[]{:S(2)}, u32[]{:S(2)}) %all-to-all-start.1) | async-done | bytes 98336 | tf_op jit(solution)/shard_map/all_to_all | solution.py:202
  42.5 0.1 shard_map.85
  42.6 0.0 collective-permute-done.others_ref
  42.6 0.0 copy-start.1
  42.6 13.1 %all_to_all.21.table_ref = f32[32,3,4,128]{3,2,1,0:T(4,128)S(1)} all-to-all(f32[32,3,4,128]{3,2,1,0:T(4,128)S(1)} %shard_map.85), channel_id=1, replica_groups={{0,16,32,48,64,80,96,112,128,144,160,176,192,208,224,240,256,272,288,30..., dimensions={0} | all-to-all | bytes 393216 | tf_op jit(solution)/shard_map/all_to_all | solution.py:202
  55.7 0.0 copy-done.1
  55.7 0.8 %shard_map.86 = f32[8,1,128]{2,1,0:T(1,128)S(1)} custom-call(s32[3,1,128]{2,1,0:T(1,128)S(1)} %get-tuple-element.25.slots_given, s32[8,1,128]{2,1,0:T(1,128)S(1)} %bitcast.4, f32[9,16,128]{2,1,0:T(8,128)S(1)} %shard_map.82.empty_ref, f32[32,3,4,128]{3,2,1,0:T(4,128)S(1)} %all_to_all.21.table_ref, bf16[1,3,8,128,128]{4,3,2,1,0:T(8,128)(2,1)S(1)} %copy-done, ...), custom_call_target="tpu_custom_call" | custom-call | tf_op jit(solution)/shard_map/pallas_call | solution.py:188
  56.5 11.9 %all_to_all.22 = f32[8,1,128]{2,1,0:T(1,128)S(1)} all-to-all(f32[8,1,128]{2,1,0:T(1,128)S(1)} %shard_map.86), channel_id=1, replica_groups=mesh['slab'=64,'grp'=8] {'grp'}, dimensions={0} | all-to-all | bytes 8192 | tf_op jit(solution)/shard_map/all_to_all | solution.py:202
  68.3 0.5 reduce_sum.9
  (1 shorter events, 0.0 us)
Async XLA Ops:
  0.0 0.7 %copy-start.3 = (f32[16,128]{1,0:T(8,128)S(1)}, f32[16,128]{1,0:T(8,128)}, u32[]{:S(2)}) copy-start(f32[16,128]{1,0:T(8,128)} %apod_ref) | copy-start | bytes 24580
  0.0 1.1 %copy-start.2 = (bf16[1,128,2048]{2,1,0:T(8,128)(2,1)S(1)}, bf16[1,128,2048]{2,1,0:T(8,128)(2,1)}, u32[]{:S(2)}) copy-start(bf16[1,128,2048]{2,1,0:T(8,128)(2,1)} %echo_ref) | copy-start | bytes 1572868
  0.0 1.1 %copy-start.4 = (s32[1,3,64]{2,0,1:T(1,128)S(1)}, s32[1,3,64]{2,0,1:T(1,128)}, u32[]{:S(2)}) copy-start(s32[1,3,64]{2,0,1:T(1,128)} %param.12) | copy-start | bytes 2308
  0.0 1.1 %copy-start.5 = (s32[1,3,64]{2,0,1:T(1,128)S(1)}, s32[1,3,64]{2,0,1:T(1,128)}, u32[]{:S(2)}) copy-start(s32[1,3,64]{2,0,1:T(1,128)} %param.13) | copy-start | bytes 2308
  0.0 1.0 %copy-start.6 = (s32[3]{0:T(128)S(1)}, s32[3]{0:T(128)}, u32[]{:S(2)}) copy-start(s32[3]{0:T(128)} %param.9) | copy-start | bytes 40
  0.0 1.0 %copy-start.7 = (s32[1,3]{1,0:T(1,128)S(1)}, s32[1,3]{1,0:T(1,128)}, u32[]{:S(2)}) copy-start(s32[1,3]{1,0:T(1,128)} %counts_ref) | copy-start | bytes 40
  0.1 33.9 %copy-start = (bf16[1,3,8,128,128]{4,3,2,1,0:T(8,128)(2,1)S(1)}, bf16[1,3,8,128,128]{4,3,2,1,0:T(8,128)(2,1)}, u32[]{:S(2)}) copy-start(bf16[1,3,8,128,128]{4,3,2,1,0:T(8,128)(2,1)} %panels_ref.1) | copy-start | bytes 2359300
  21.6 20.9 %all-to-all-start.1 = ((f32[16,3,4,128]{3,2,1,0:T(4,128)}), f32[16,3,4,128]{3,2,1,0:T(4,128)S(1)}, u32[]{:S(2)}, u32[]{:S(2)}) async-start(f32[16,3,4,128]{3,2,1,0:T(4,128)} %shard_map.84), calls=%async_computation.1 | async-start | bytes 196608 | tf_op jit(solution)/shard_map/all_to_all | solution.py:202
  34.0 8.6 %collective-permute-start = (bf16[1,3,8,128,128]{4,3,2,1,0:T(8,128)(2,1)S(1)}, bf16[1,3,8,128,128]{4,3,2,1,0:T(8,128)(2,1)S(1)}, u32[]{:S(2)}, u32[]{:S(2)}) collective-permute-start(bf16[1,3,8,128,128]{4,3,2,1,0:T(8,128)(2,1)S(1)} %copy-done), channel_id=1, source_target_pairs={{0,1},{1,0},{2,3},{3,2},{4,5},{5,4},{6,7},{7,6},{8,9},{9,8},{10,11... | collective-permute-start | bytes 2359304 | tf_op jit(solution)/shard_map/ppermute | solution.py:227
  42.6 13.1 %copy-start.1 = (s32[1024]{0:T(1024)S(1)}, s32[1024]{0:T(1024)}, u32[]{:S(2)}) copy-start(s32[1024]{0:T(1024)} %param.15) | copy-start | bytes 12292

commit v12 on v11

--- a/solution.py
+++ b/solution.py
@@ -97,6 +97,7 @@
         out_shape=jax.ShapeDtypeStruct((copies, transmits) + tile, pieces.dtype),
         in_specs=[VMEM] * 2,
         out_specs=VMEM,
+        cost_estimate=pl.CostEstimate(flops=10_000_000_000, bytes_accessed=0, transcendentals=0),
         compiler_params=PARAMS,
     )(acquirer, pieces)
 
@@ -122,7 +123,7 @@
         out_shape=jax.ShapeDtypeStruct((copies,) + parts.shape[1:], parts.dtype),
         in_specs=[VMEM, VMEM],
         out_specs=VMEM,
-        cost_estimate=pl.CostEstimate(flops=10_000_000_000, bytes_accessed=0, transcendentals=0),
+        cost_estimate=pl.CostEstimate(flops=0, bytes_accessed=0, transcendentals=0),
         compiler_params=PARAMS,
     )(acquirer, parts)
 

time: 69.2 us -> 71.8 us (1.038)
  local copies, waits for them, and re-layouts: 1.02 us -> 3.72 us
  blocking collectives: 44.4 us -> 45.5 us
  starting transfers between devices: 14.4 us -> 13.4 us
    unnamed x16, local copies, waits for them, and re-layouts: 1.02 us -> 3.72 us
    all_to_all x1, starting transfers between devices: 12.4 us -> 10.5 us  [exchange(): lax.all_to_all(pieces, axis, split_axis=0, concat_axis=0, axis_index_grou...]
    all_to_all x3, blocking collectives: 44.4 us -> 45.5 us  [exchange(): lax.all_to_all(pieces, axis, split_axis=0, concat_axis=0, axis_index_grou...]
    ppermute x1, starting transfers between devices: 2.01 us -> 2.86 us  [per_device(): others = lax.ppermute(given, 'grp', [(i, i ^ 1) for i in range(groups)])]
where the time goes in v12:
time: 71.8 us; the launch traced here: 71.5 us
  blocking collectives  45.5 us (63%)
  starting transfers between devices  13.4 us (19%)
  waiting for transfers between devices  6.27 us (9%)
  local copies, waits for them, and re-layouts  3.72 us (5%)
  Pallas kernels  1.94 us (3%)
    all_to_all x3, blocking collectives, exchange(): lax.all_to_all(pieces, axis, split_axis=0, concat_axis=0, axis_index_grou...  45.5 us
    all_to_all x1, starting transfers between devices, exchange(): lax.all_to_all(pieces, axis, split_axis=0, concat_axis=0, axis_index_grou...  10.5 us
    all_to_all x1, waiting for transfers between devices, exchange(): lax.all_to_all(pieces, axis, split_axis=0, concat_axis=0, axis_index_grou...  6.27 us
    unnamed x16, local copies, waits for them, and re-layouts  3.72 us
    ppermute x1, starting transfers between devices, per_device(): others = lax.ppermute(given, 'grp', [(i, i ^ 1) for i in range(groups)])  2.86 us
  transfers between devices with their start and end apart: 2, of which 1 were waited for; matrix products, arithmetic and copies ran while one was open for 0% of the time, Pallas kernels for 0%

profile of v12, /device:TPU:1, one launch (start us, length us, event | category | flops | bytes accessed | tf_op | source)
XLA Modules:
  0.0 71.5 jit_solution(10076159096532030072)
XLA Ops:
  0.0 0.0 copy-start.3
  0.0 0.0 copy-start.2
  0.0 0.0 copy-start
  0.0 0.7 copy-done.3
  0.7 0.4 copy-done.2
  1.1 0.0 copy-start.4
  1.1 0.7 copy-done.4
  1.7 0.0 copy-start.5
  1.7 0.7 copy-done.5
  2.4 0.0 copy-start.6
  2.4 0.7 copy-done.6
  3.1 0.0 copy-start.7
  3.1 0.7 copy-done.7
  3.7 0.9 %shard_map.83 = (f32[32,2,4,128]{3,2,1,0:T(4,128)}, s32[1,3]{1,0:T(1,128)S(1)}, s32[3,1,128]{2,1,0:T(1,128)S(1)}) custom-call(f32[16,128]{1,0:T(8,128)S(1)} %copy-done.3, bf16[1,128,2048]{2,1,0:T(8,128)(2,1)S(1)} %copy-done.2, s32[1,3]{1,0:T(1,128)S(1)} %bitcast.7, s32[1,3]{1,0:T(1,128)S(1)} %copy-done.7, s32[3,1,64]{2,1,0:T(1,128)S(1)} %bitcast.5, ...), custom_call_target="tpu_custom_call" | custom-call | flops 200000000 | tf_op jit(solution)/shard_map/pallas_call | solution.py:66
  4.7 10.5 %all-to-all-start = ((f32[32,2,4,128]{3,2,1,0:T(4,128)}), f32[32,2,4,128]{3,2,1,0:T(4,128)S(1)}, u32[]{:S(2)}, u32[]{:S(2)}) async-start(f32[32,2,4,128]{3,2,1,0:T(4,128)} %get-tuple-element.29), calls=%async_computation | async-start | bytes 262144 | tf_op jit(solution)/shard_map/all_to_all | solution.py:203
  15.2 0.0 copy-done
  15.2 2.9 %collective-permute-start = (bf16[1,3,8,128,128]{4,3,2,1,0:T(8,128)(2,1)S(1)}, bf16[1,3,8,128,128]{4,3,2,1,0:T(8,128)(2,1)S(1)}, u32[]{:S(2)}, u32[]{:S(2)}) collective-permute-start(bf16[1,3,8,128,128]{4,3,2,1,0:T(8,128)(2,1)S(1)} %copy-done), channel_id=1, source_target_pairs={{0,1},{1,0},{2,3},{3,2},{4,5},{5,4},{6,7},{7,6},{8,9},{9,8},{10,11... | collective-permute-start | bytes 2359304 | tf_op jit(solution)/shard_map/ppermute | solution.py:228
  18.1 6.3 %all-to-all-done.pieces_ref = f32[32,2,4,128]{3,2,1,0:T(4,128)S(1)} async-done(((f32[32,2,4,128]{3,2,1,0:T(4,128)}), f32[32,2,4,128]{3,2,1,0:T(4,128)S(1)}, u32[]{:S(2)}, u32[]{:S(2)}) %all-to-all-start) | async-done | bytes 131104 | tf_op jit(solution)/shard_map/all_to_all | solution.py:203
  24.3 0.1 shard_map.84
  24.5 20.7 %all_to_all.20.parts_ref = f32[16,3,4,128]{3,2,1,0:T(4,128)S(1)} all-to-all(f32[16,3,4,128]{3,2,1,0:T(4,128)S(1)} %shard_map.84), channel_id=1, replica_groups={{0,1,2,3,4,5,6,7,8,9,10,11,12,13,14,15},{16,17,18,19,20,21,22,23,24,25,..., dimensions={0} | all-to-all | bytes 196608 | tf_op jit(solution)/shard_map/all_to_all | solution.py:203
  45.1 0.1 shard_map.85
  45.2 0.0 collective-permute-done.others_ref
  45.3 0.0 copy-start.1
  45.3 13.1 %all_to_all.21.table_ref = f32[32,3,4,128]{3,2,1,0:T(4,128)S(1)} all-to-all(f32[32,3,4,128]{3,2,1,0:T(4,128)S(1)} %shard_map.85), channel_id=1, replica_groups={{0,16,32,48,64,80,96,112,128,144,160,176,192,208,224,240,256,272,288,30..., dimensions={0} | all-to-all | bytes 393216 | tf_op jit(solution)/shard_map/all_to_all | solution.py:203
  58.4 0.0 copy-done.1
  58.4 0.8 %shard_map.86 = f32[8,1,128]{2,1,0:T(1,128)S(1)} custom-call(s32[3,1,128]{2,1,0:T(1,128)S(1)} %get-tuple-element.25.slots_given, s32[8,1,128]{2,1,0:T(1,128)S(1)} %bitcast.4, f32[9,16,128]{2,1,0:T(8,128)S(1)} %shard_map.82.empty_ref, f32[32,3,4,128]{3,2,1,0:T(4,128)S(1)} %all_to_all.21.table_ref, bf16[1,3,8,128,128]{4,3,2,1,0:T(8,128)(2,1)S(1)} %copy-done, ...), custom_call_target="tpu_custom_call" | custom-call | tf_op jit(solution)/shard_map/pallas_call | solution.py:189
  59.1 11.8 %all_to_all.22 = f32[8,1,128]{2,1,0:T(1,128)S(1)} all-to-all(f32[8,1,128]{2,1,0:T(1,128)S(1)} %shard_map.86), channel_id=1, replica_groups=mesh['slab'=64,'grp'=8] {'grp'}, dimensions={0} | all-to-all | bytes 8192 | tf_op jit(solution)/shard_map/all_to_all | solution.py:203
  70.9 0.5 reduce_sum.9
  (1 shorter events, 0.0 us)
Async XLA Ops:
  0.0 0.7 copy-start.3
  0.0 1.1 %copy-start.2 = (bf16[1,128,2048]{2,1,0:T(8,128)(2,1)S(1)}, bf16[1,128,2048]{2,1,0:T(8,128)(2,1)}, u32[]{:S(2)}) copy-start(bf16[1,128,2048]{2,1,0:T(8,128)(2,1)} %echo_ref) | copy-start | bytes 1572868
  0.0 15.2 %copy-start = (bf16[1,3,8,128,128]{4,3,2,1,0:T(8,128)(2,1)S(1)}, bf16[1,3,8,128,128]{4,3,2,1,0:T(8,128)(2,1)}, u32[]{:S(2)}) copy-start(bf16[1,3,8,128,128]{4,3,2,1,0:T(8,128)(2,1)} %panels_ref.1) | copy-start | bytes 2359300
  1.1 0.7 copy-start.4
  1.7 0.7 copy-start.5
  2.4 0.7 copy-start.6
  3.1 0.7 copy-start.7
  4.7 19.7 %all-to-all-start = ((f32[32,2,4,128]{3,2,1,0:T(4,128)}), f32[32,2,4,128]{3,2,1,0:T(4,128)S(1)}, u32[]{:S(2)}, u32[]{:S(2)}) async-start(f32[32,2,4,128]{3,2,1,0:T(4,128)} %get-tuple-element.29), calls=%async_computation | async-start | bytes 262144 | tf_op jit(solution)/shard_map/all_to_all | solution.py:203
  15.2 30.1 %collective-permute-start = (bf16[1,3,8,128,128]{4,3,2,1,0:T(8,128)(2,1)S(1)}, bf16[1,3,8,128,128]{4,3,2,1,0:T(8,128)(2,1)S(1)}, u32[]{:S(2)}, u32[]{:S(2)}) collective-permute-start(bf16[1,3,8,128,128]{4,3,2,1,0:T(8,128)(2,1)S(1)} %copy-done), channel_id=1, source_target_pairs={{0,1},{1,0},{2,3},{3,2},{4,5},{5,4},{6,7},{7,6},{8,9},{9,8},{10,11... | collective-permute-start | bytes 2359304 | tf_op jit(solution)/shard_map/ppermute | solution.py:228
  45.3 13.1 %copy-start.1 = (s32[1024]{0:T(1024)S(1)}, s32[1024]{0:T(1024)}, u32[]{:S(2)}) copy-start(s32[1024]{0:T(1024)} %param.15) | copy-start | bytes 12292
